TPU v7x, 512 devices: a whole 4x8x8 slice. The times are simulated.
512 devices in a mesh: wa: 16 (over x, z_lo, core), gx: 32 (over z_hi, y).
Axes of the slice: x: 4, y: 8, z: 8 (z_hi: 4, z_lo: 2; z = z_hi * 2 + z_lo), core: 2. Of those that a mesh axis runs over, the one named last changes fastest.
Arguments:
- part_pos: float32 [3, 32, 128, 128], P(None, 'wa', 'gx'), may hold values from 0 to 32, as said below
- part_vel: float32 [3, 32, 128, 128], P(None, 'wa', 'gx'), may hold values from -6 to 6
- random_kicks: float32 [4, 32, 128, 128], P(None, 'wa', 'gx'), may hold values from -5 to 5
- vert_pos: float32 [3, 512, 498], P(None, ('wa', 'gx')), may hold values from -3 to 128
- vert_vel: float32 [3, 512, 498], P(None, ('wa', 'gx')), may hold values from -6 to 6
- cover_start: int32 [512], P('wa'), may hold values from 0 to 29, as said below
- bond_ends: int32 [1488, 2], replicated, may hold values from 0 to 497, as said below
- triangles: int32 [992, 3], replicated, may hold values from 0 to 497, as said below
- rest_len: float32 [1488], replicated, may hold values from 1 to 3
- rest_area: float32 [992], replicated, may hold values from 0.5 to 3
Outputs:
- final_part_pos: float32 [3, 32, 128, 128], P(None, 'wa', 'gx')
- final_part_vel: float32 [3, 32, 128, 128], P(None, 'wa', 'gx')
- final_vert_pos: float32 [3, 512, 498], P(None, ('wa', 'gx'))
- final_vert_vel: float32 [3, 512, 498], P(None, ('wa', 'gx'))
Inputs may be any that keep to these rules, and one draw needn't show every extreme that they name: `part_pos`: components 0 and 1 lie in [0, 1), component 2 in [0, 32). `cover_start`: A cell's covered slabs may lie anywhere along its row, far from the slab that holds it. In every row some slab is covered by exactly 5 cells and none by more. `bond_ends`: the two vertices of a bond differ. `triangles`: the three vertices of a triangle differ.
All inputs are finite; a program needn't handle non-finite values.
Results may differ from a plain program's by a relative error of at most 0.0003.
Values sent between devices are 32-bit elements; how exact they have to be, the bound alone decides.
No kernel may reach another device: no remote copies, remote signals or barrier semaphores. Data moves between devices by JAX's collectives and lax.ppermute only.
A program may use at most 64 MiB of HBM per device.

v0:
```python
import jax
import jax.numpy as jnp
from jax import lax
from jax.sharding import PartitionSpec as P

SPAN = 3
STEPS = 2
MAXCOV = 5


TIME_STEP = 0.04
SOLVENT_REPULSION = 25.0
SOLVENT_FRICTION = 4.5
NOISE_SCALE = 15.0
MEMBRANE_REPULSION = 4.0
MEMBRANE_FRICTION = 4.5
BOND_STIFFNESS = 2.0
AREA_STIFFNESS = 0.5
HALF_ROOT = 0.7071067811865476


def extended(block, sides, width):
    for axis, dim in sides:
        count = lax.axis_size(axis)
        forward = [(i, i + 1) for i in range(count - 1)]
        backward = [(target, source) for source, target in forward]
        low = lax.ppermute(
            lax.slice_in_dim(block, block.shape[dim] - width, None, axis=dim), axis, forward
        )
        high = lax.ppermute(lax.slice_in_dim(block, 0, width, axis=dim), axis, backward)
        block = jnp.concatenate([low, block, high], axis=dim)
    return block


def solvent_terms(own_part, near_part, shift_w, shift_f, near_mask):
    delta_w = own_part[0][:, :, None] - near_part[0][:, None, :] - shift_w
    delta_f = own_part[1][:, :, None] - near_part[1][:, None, :] - shift_f
    delta_z = own_part[2][:, :, None] - near_part[2][:, None, :]
    speed_w = own_part[3][:, :, None] - near_part[3][:, None, :]
    speed_f = own_part[4][:, :, None] - near_part[4][:, None, :]
    speed_z = own_part[5][:, :, None] - near_part[5][:, None, :]
    theta_pair = (
        own_part[6][:, :, None] * near_part[7][:, None, :]
        + own_part[7][:, :, None] * near_part[6][:, None, :]
    ) * HALF_ROOT
    weight = (
        jnp.maximum(1.0 - (delta_w * delta_w + delta_f * delta_f + delta_z * delta_z), 0.0)
        * near_mask[:, None, None]
    )
    scalar = (
        SOLVENT_REPULSION * weight
        - SOLVENT_FRICTION
        * weight
        * weight
        * (delta_w * speed_w + delta_f * speed_f + delta_z * speed_z)
        + NOISE_SCALE * weight * theta_pair
    )
    return jnp.stack(
        [jnp.sum(scalar * delta_w, 2), jnp.sum(scalar * delta_f, 2), jnp.sum(scalar * delta_z, 2)]
    )


def couple_cell(part_frame, part_speed, cell_frame, cell_speed, cell_weight):
    delta_w = part_frame[0][None, :] - cell_frame[0][:, None]
    delta_f = part_frame[1][None, :] - cell_frame[1][:, None]
    delta_z = part_frame[2][None, :] - cell_frame[2][:, None]
    speed_w = part_speed[0][None, :] - cell_speed[0][:, None]
    speed_f = part_speed[1][None, :] - cell_speed[1][:, None]
    speed_z = part_speed[2][None, :] - cell_speed[2][:, None]
    weight = (
        jnp.maximum(1.0 - (delta_w * delta_w + delta_f * delta_f + delta_z * delta_z), 0.0)
        * cell_weight
    )
    scalar = MEMBRANE_REPULSION * weight - MEMBRANE_FRICTION * weight * weight * (
        delta_w * speed_w + delta_f * speed_f + delta_z * speed_z
    )
    push_w = scalar * delta_w
    push_f = scalar * delta_f
    push_z = scalar * delta_z
    on_parts = jnp.stack([jnp.sum(push_w, 0), jnp.sum(push_f, 0), jnp.sum(push_z, 0)])
    on_cell = -jnp.stack([jnp.sum(push_w, 1), jnp.sum(push_f, 1), jnp.sum(push_z, 1)])
    return (on_parts, on_cell)


def slab_coupling(part_frame, part_speed, row_frame, row_speed, starts, slab_id):
    cell_count = starts.shape[0]
    order_ids = jnp.arange(cell_count, dtype=jnp.int32)
    covered = (starts <= slab_id) & (slab_id < starts + SPAN)
    sort_key = jnp.where(covered, 0, cell_count).astype(jnp.int32) + order_ids
    chosen = jnp.argsort(sort_key)[:MAXCOV]
    weights = covered[chosen].astype(jnp.float32)
    cell_frames = jnp.moveaxis(row_frame[:, chosen], 1, 0)
    cell_speeds = jnp.moveaxis(row_speed[:, chosen], 1, 0)

    def visit(running, member):
        cell_frame, cell_speed, cell_weight = member
        on_parts, on_cell = couple_cell(part_frame, part_speed, cell_frame, cell_speed, cell_weight)
        return (running + on_parts, on_cell)

    summed, pushes = lax.scan(
        visit, jnp.zeros(part_frame.shape, jnp.float32), (cell_frames, cell_speeds, weights)
    )
    one_hot = (chosen[:, None] == order_ids[None, :]).astype(jnp.float32)
    reaction = jnp.einsum("mr,mcv->crv", one_hot, pushes, precision=lax.Precision.HIGHEST)
    return (summed, reaction)


def slab_frame(tile_pos, base_f):
    tiles_w = tile_pos.shape[1]
    tiles_f = tile_pos.shape[2]
    along_w = jnp.arange(tiles_w, dtype=jnp.int32).astype(jnp.float32)[:, None, None]
    along_f = (base_f + jnp.arange(tiles_f, dtype=jnp.int32)).astype(jnp.float32)[None, :, None]
    framed = jnp.stack([tile_pos[0] + along_w, tile_pos[1] + along_f, tile_pos[2]])
    return framed.reshape(3, -1)


def bond_energy(positions, bond_ends, triangles, rest_len, rest_area):
    bond_head = positions[:, :, bond_ends[:, 0]]
    bond_tail = positions[:, :, bond_ends[:, 1]]
    stretch = jnp.sum((bond_head - bond_tail) ** 2, 0)
    sq_len = rest_len * rest_len
    energy = 0.25 * BOND_STIFFNESS * jnp.sum((stretch - sq_len) ** 2 / sq_len)
    corner_one = positions[:, :, triangles[:, 0]]
    corner_two = positions[:, :, triangles[:, 1]]
    corner_three = positions[:, :, triangles[:, 2]]
    edge_one = corner_two - corner_one
    edge_two = corner_three - corner_one
    normal_w = edge_one[1] * edge_two[2] - edge_one[2] * edge_two[1]
    normal_f = edge_one[2] * edge_two[0] - edge_one[0] * edge_two[2]
    normal_z = edge_one[0] * edge_two[1] - edge_one[1] * edge_two[0]
    area_sq = 0.25 * (normal_w * normal_w + normal_f * normal_f + normal_z * normal_z)
    sq_area = rest_area * rest_area
    return energy + 0.25 * AREA_STIFFNESS * jnp.sum((area_sq - sq_area) ** 2 / sq_area)


def bond_force(positions, bond_ends, triangles, rest_len, rest_area):
    return -jax.grad(bond_energy)(positions, bond_ends, triangles, rest_len, rest_area)


def body(
    part_pos,
    part_vel,
    random_kicks,
    vert_pos,
    vert_vel,
    cover_start,
    bond_ends,
    triangles,
    rest_len,
    rest_area,
):
    tiles_w = part_pos.shape[1]
    tiles_f = part_pos.shape[2]
    per_tile = part_pos.shape[3]
    row_index = lax.axis_index("wa")
    slab_index = lax.axis_index("gx")
    rows_all = lax.axis_size("wa")
    slabs_all = lax.axis_size("gx")
    glob_w = row_index * tiles_w + jnp.arange(tiles_w, dtype=jnp.int32)
    glob_f = slab_index * tiles_f + jnp.arange(tiles_f, dtype=jnp.int32)
    row_frame = vert_pos
    row_speed = vert_vel
    for step_index in range(STEPS):
        bundle = jnp.concatenate(
            [part_pos, part_vel, random_kicks[2 * step_index : 2 * step_index + 2]], 0
        )
        padded = extended(bundle, (("wa", 1), ("gx", 2)), 1)
        row_frame, row_speed = (
            lax.all_gather(vert_pos, "gx", axis=1, tiled=True),
            lax.all_gather(vert_vel, "gx", axis=1, tiled=True),
        )
        part_frame = slab_frame(part_pos, slab_index * tiles_f)
        membrane, reaction = slab_coupling(
            part_frame, part_vel.reshape(3, -1), row_frame, row_speed, cover_start, slab_index
        )
        membrane = membrane.reshape(3, tiles_w, tiles_f, per_tile)
        own_part = bundle.reshape(8, tiles_w * tiles_f, per_tile)
        solvent = jnp.zeros((3, tiles_w * tiles_f, per_tile), jnp.float32)
        for off_w in (-1, 0, 1):
            valid_w = (glob_w + off_w >= 0) & (glob_w + off_w < rows_all * tiles_w)
            for off_f in (-1, 0, 1):
                valid_f = (glob_f + off_f >= 0) & (glob_f + off_f < slabs_all * tiles_f)
                near_mask = (valid_w[:, None] & valid_f[None, :]).astype(jnp.float32).reshape(-1)
                near_part = padded[
                    :, 1 + off_w : 1 + off_w + tiles_w, 1 + off_f : 1 + off_f + tiles_f
                ].reshape(8, tiles_w * tiles_f, per_tile)
                solvent = solvent + solvent_terms(
                    own_part, near_part, float(off_w), float(off_f), near_mask
                )
        solvent = solvent.reshape(3, tiles_w, tiles_f, per_tile)
        own_react = lax.psum_scatter(reaction, "gx", scatter_dimension=1, tiled=True)
        vert_vel = vert_vel + TIME_STEP * (
            own_react + bond_force(vert_pos, bond_ends, triangles, rest_len, rest_area)
        )
        vert_pos = vert_pos + TIME_STEP * vert_vel
        part_vel = part_vel + TIME_STEP * (solvent + membrane)
        part_pos = part_pos + TIME_STEP * part_vel
    return (part_pos, part_vel, vert_pos, vert_vel)


def solution(mesh):
    in_specs = (
        P(None, "wa", "gx", None),
        P(None, "wa", "gx", None),
        P(None, "wa", "gx", None),
        P(None, ("wa", "gx"), None),
        P(None, ("wa", "gx"), None),
        P("wa"),
        P(),
        P(),
        P(),
        P(),
    )
    out_specs = (
        P(None, "wa", "gx", None),
        P(None, "wa", "gx", None),
        P(None, ("wa", "gx"), None),
        P(None, ("wa", "gx"), None),
    )
    return jax.shard_map(body, mesh=mesh, in_specs=in_specs, out_specs=out_specs, check_vma=False)
```

profile of v0, /device:TPU:4, one launch (start us, length us, event | category | flops | bytes accessed | tf_op | source)
XLA Modules:
  0.0 1166.0 jit_solution(17285253067503286250)
XLA Ops:
  9.3 3.7 collective-permute-start.1
  13.0 1.9 collective-permute-start
  20.5 92.7 %all_gather.12 = f32[3,32,498]{2,0,1:T(4,128)} all-gather(f32[3,1,498]{2,0,1:T(4,128)S(1)} %copy.84), channel_id=1, replica_groups=mesh['wa'=16,'gx'=32] {'gx'}, dimensions={1}, use_global_device_ids=true | all-gather | bytes 197208 | tf_op jit(solution)/shard_map/all_gather | solution.py:169
  113.2 1.6 sort.19
  115.5 2.9 gather_fusion.3
  118.4 2.9 gather_fusion.4
  121.3 2.9 gather_fusion.5
  124.3 2.7 gather_fusion.6
  127.1 2.7 gather_fusion.7
  129.9 1.4 slice_reduce_fusion.6
  132.3 76.7 %all_gather.13 = f32[3,32,498]{2,0,1:T(4,128)S(1)} all-gather(f32[3,1,498]{2,0,1:T(4,128)S(1)} %copy.85), channel_id=1, replica_groups=mesh['wa'=16,'gx'=32] {'gx'}, dimensions={1}, use_global_device_ids=true | all-gather | bytes 197208 | tf_op jit(solution)/shard_map/all_gather | solution.py:170
  209.0 1.5 gather_fusion
  218.9 6.1 scatter_custom_fusion
  225.0 6.5 scatter_custom_fusion.1
  231.5 6.4 scatter_fusion
  237.9 9.7 scatter_custom_fusion.3
  247.6 9.7 scatter_custom_fusion.4
  260.2 4.7 collective-permute-start.2
  265.1 25.6 %while.26 = (s32[]{:T(128)}, f32[3,1024]{1,0:T(4,128)S(1)}, f32[5,3,498]{2,0,1:T(8,128)S(1)}, f32[3,1024]{1,0:T(4,128)S(1)}, f32[5,3,498]{2,1,0:T(4,128)S(1)}, /...) while((s32[]{:T(128)}, f32[3,1024]{1,0:T(4,128)S(1)}, ...), condition=%wide.region_35.36_spmd.clone, body=%wide.region_28.35_spmd.clone.sunk | while | flops 16840624 | bytes 200759 | solution.py:100
  266.4 3.7 fusion.312
  271.5 3.7 fusion.312
  276.6 3.7 fusion.312
  281.7 3.7 fusion.312
  286.8 3.7 fusion.312
  290.8 2.0 multiply_reduce_fusion.13
  292.8 2.0 multiply_reduce_fusion.14
  295.1 2.0 multiply_reduce_fusion.16
  297.2 2.0 fusion.143
  299.3 2.0 fusion.124
  301.4 2.0 multiply_reduce_fusion.20
  303.4 2.0 multiply_reduce_fusion.21
  305.5 2.5 multiply_reduce_fusion.23
  308.2 1.9 collective-permute-start.4
  310.1 4.5 collective-permute-start.5
  317.4 13.3 %collective-permute-start.6 = (f32[8,4,1,128]{3,2,1,0:T(1,128)S(1)}, f32[8,4,1,128]{3,2,1,0:T(1,128)S(1)}, u32[]{:S(2)}, u32[]{:S(2)}) collective-permute-start(f32[8,4,1,128]{3,2,1,0:T(1,128)S(1)} %get-tuple-element.446), channel_id=1, source_target_pairs={{0,1},{1,2},{2,3},{3,4},{4,5},{5,6},{6,7},{7,8},{8,9},{9,10},{10,1... | collective-permute-start | bytes 49160 | tf_op jit(solution)/shard_map/ppermute | solution.py:27
  331.0 2.0 multiply_reduce_fusion.1
  333.1 2.6 multiply_reduce_fusion.2
  335.8 2.6 multiply_reduce_fusion.4
  338.5 2.6 fusion.213
  341.2 3.2 multiply_reduce_fusion.11
  344.4 2.6 fusion.194
  347.1 2.6 multiply_reduce_fusion.8
  349.7 2.6 multiply_reduce_fusion.9
  352.3 260.5 %all-reduce.29.cloned.1.call-done = f32[3,32,498]{2,1,0:T(8,128)} async-done(((f32[3,32,498]{2,1,0:T(8,128)}), f32[3,32,498]{2,1,0:T(8,128)}) %all-reduce.29.cloned.1.call-update) | async-done | bytes 191248
  614.3 2.9 gather_fusion.10
  617.2 2.9 gather_fusion.11
  620.1 2.9 gather_fusion.12
  623.0 2.7 gather_fusion.13
  625.8 2.7 gather_fusion.14
  628.5 80.0 %all_gather.14 = f32[3,32,498]{2,0,1:T(4,128)S(1)} all-gather(f32[3,1,498]{2,0,1:T(4,128)S(1)} %copy.92), channel_id=1, replica_groups=mesh['wa'=16,'gx'=32] {'gx'}, dimensions={1}, use_global_device_ids=true | all-gather | bytes 197208 | tf_op jit(solution)/shard_map/all_gather | solution.py:169
  709.2 76.8 %all_gather.15 = f32[3,32,498]{2,0,1:T(4,128)S(1)} all-gather(f32[3,1,498]{2,0,1:T(4,128)S(1)} %copy.93), channel_id=1, replica_groups=mesh['wa'=16,'gx'=32] {'gx'}, dimensions={1}, use_global_device_ids=true | all-gather | bytes 197208 | tf_op jit(solution)/shard_map/all_gather | solution.py:170
  786.7 25.5 %while.27 = (s32[]{:T(128)}, f32[3,1024]{1,0:T(4,128)S(1)}, f32[5,3,498]{2,0,1:T(8,128)S(1)}, f32[3,1024]{1,0:T(4,128)S(1)}, f32[5,3,498]{2,1,0:T(4,128)S(1)}, /...) while((s32[]{:T(128)}, f32[3,1024]{1,0:T(4,128)S(1)}, ...), condition=%wide.region_77.78_spmd.clone, body=%wide.region_70.77_spmd.clone.sunk | while | flops 16840624 | bytes 200759 | solution.py:100
  788.0 3.7 fusion.314
  793.1 3.7 fusion.314
  798.3 3.7 fusion.314
  803.4 3.7 fusion.314
  808.5 3.7 fusion.314
  815.8 6.4 scatter_custom_fusion.5
  822.3 6.5 scatter_custom_fusion.6
  828.8 6.1 scatter_fusion.1
  835.0 9.7 scatter_custom_fusion.8
  844.7 9.7 scatter_custom_fusion.9
  857.1 300.0 %all-reduce.31.cloned.1.call-done = f32[3,32,498]{2,1,0:T(8,128)} async-done(((f32[3,32,498]{2,1,0:T(8,128)}), f32[3,32,498]{2,1,0:T(8,128)}) %all-reduce.31.cloned.1.call-update) | async-done | bytes 191248
  1157.0 2.0 multiply_add_fusion.4
  (331 shorter events, 46.7 us)
Async XLA Ops:
  7.2 106.0 %copy-start.55 = (s32[32]{0:T(128)S(1)}, s32[32]{0:T(128)}, u32[]{:S(2)}) copy-start(s32[32]{0:T(128)} %param.19) | copy-start | bytes 388
  7.2 108.2 %copy-start.4 = (f32[3,1,498]{2,1,0:T(1,128)S(1)}, f32[3,1,498]{2,1,0:T(1,128)}, u32[]{:S(2)}) copy-start(f32[3,1,498]{2,1,0:T(1,128)} %param.18) | copy-start | bytes 17932
  7.2 108.2 %copy-start.34 = (s32[992,3]{0,1:T(4,128)S(1)}, s32[992,3]{0,1:T(4,128)}, u32[]{:S(2)}) copy-start(s32[992,3]{0,1:T(4,128)} %param.21) | copy-start | bytes 35716
  7.2 117.1 %copy-start.32 = (s32[1488,2]{0,1:T(2,128)S(1)}, s32[1488,2]{0,1:T(2,128)}, u32[]{:S(2)}) copy-start(s32[1488,2]{0,1:T(2,128)} %param.20) | copy-start | bytes 35716
  7.2 605.5 %all-reduce.29.cloned.1.call-start = ((), (), s32[]{:S(2)}) async-start(), calls=%async_computation | async-start | bytes 393216
  9.3 249.5 %collective-permute-start.1 = (f32[8,1,4,128]{3,2,1,0:T(4,128)}, f32[8,1,4,128]{3,2,1,0:T(4,128)S(1)}, u32[]{:S(2)}, u32[]{:S(2)}) collective-permute-start(f32[8,1,4,128]{3,2,1,0:T(4,128)} %get-tuple-element.485), channel_id=1, source_target_pairs={{32,0},{64,32},{96,64},{128,96},{160,128},{192,160},{224,192},{256... | collective-permute-start | bytes 49160 | tf_op jit(solution)/shard_map/ppermute | solution.py:30
  13.0 245.8 %collective-permute-start = (f32[8,1,4,128]{3,2,1,0:T(4,128)}, f32[8,1,4,128]{3,2,1,0:T(4,128)S(1)}, u32[]{:S(2)}, u32[]{:S(2)}) collective-permute-start(f32[8,1,4,128]{3,2,1,0:T(4,128)} %get-tuple-element.484), channel_id=1, source_target_pairs={{0,32},{32,64},{64,96},{96,128},{128,160},{160,192},{192,224},{224... | collective-permute-start | bytes 49160 | tf_op jit(solution)/shard_map/ppermute | solution.py:27
  115.4 96.3 %copy-start.33 = (s32[1024]{0:T(1024)}, s32[1024]{0:T(1024)S(1)}, u32[]{:S(2)}) copy-start(s32[1024]{0:T(1024)S(1)} %pad_clamp_fusion.5) | copy-start | bytes 12292
  115.5 103.4 %copy-start.31 = (s32[992,1]{0,1:T(1,128)}, s32[992,1]{0,1:T(1,128)S(1)}, u32[]{:S(2)}) copy-start(s32[992,1]{0,1:T(1,128)S(1)} %get-tuple-element.493) | copy-start | bytes 11908
  115.5 109.5 %copy-start.30 = (s32[992,1]{0,1:T(1,128)}, s32[992,1]{0,1:T(1,128)S(1)}, u32[]{:S(2)}) copy-start(s32[992,1]{0,1:T(1,128)S(1)} %get-tuple-element.492) | copy-start | bytes 11908
  131.4 0.7 copy-start.5
  131.4 0.7 copy-start.49
  131.4 0.7 copy-start.50
  131.4 0.7 copy-start.51
  131.4 0.7 copy-start.52
  131.4 0.7 copy-start.53
  131.4 0.7 copy-start.54
  131.5 77.5 %copy-start = (f32[3,2,4,128]{3,2,1,0:T(4,128)S(1)}, f32[3,2,4,128]{3,2,1,0:T(4,128)}, u32[]{:S(2)}) copy-start(f32[3,2,4,128]{3,2,1,0:T(4,128)} %param.15) | copy-start | bytes 36868
  217.4 86.0 %copy-start.37 = (f32[8]{0:T(128)}, f32[8]{0:T(128)S(1)}, u32[]{:S(2)}) copy-start(f32[8]{0:T(128)S(1)} %reshape.1284) | copy-start | bytes 100
  257.4 1.5 copy-start.1
  257.4 7.5 copy-start.41
  257.4 7.5 copy-start.40
  258.9 6.1 collective-permute-start.3
  260.2 34.8 %collective-permute-start.2 = (f32[8,4,1,128]{3,2,1,0:T(1,128)S(1)}, f32[8,4,1,128]{3,2,1,0:T(1,128)S(1)}, u32[]{:S(2)}, u32[]{:S(2)}) collective-permute-start(f32[8,4,1,128]{3,2,1,0:T(1,128)S(1)} %get-tuple-element.448), channel_id=1, source_target_pairs={{0,1},{1,2},{2,3},{3,4},{4,5},{5,6},{6,7},{7,8},{8,9},{9,10},{10,1... | collective-permute-start | bytes 49160 | tf_op jit(solution)/shard_map/ppermute | solution.py:27
  265.1 25.7 %copy-start.48 = (f32[8]{0:T(128)S(1)}, f32[8]{0:T(128)}, u32[]{:S(2)}) copy-start(f32[8]{0:T(128)} %reshape.1291) | copy-start | bytes 100
  265.1 27.8 %copy-start.47 = (f32[8]{0:T(128)S(1)}, f32[8]{0:T(128)}, u32[]{:S(2)}) copy-start(f32[8]{0:T(128)} %reshape.1290) | copy-start | bytes 100
  290.6 4.4 copy-start.46
  290.7 6.5 copy-start.45
  290.7 8.5 copy-start.42
  290.8 10.6 copy-start.39
  295.0 10.6 copy-start.43
  295.0 10.6 copy-start.44
  297.1 17.5 %copy-start.35 = (s32[5]{0:T(128)S(1)}, s32[5]{0:T(128)}, u32[]{:S(2)}) copy-start(s32[5]{0:T(128)} %get-tuple-element.533) | copy-start | bytes 64
  308.2 7.6 collective-permute-start.4
  310.1 6.0 collective-permute-start.5
  315.7 841.3 %all-reduce.31.cloned.1.call-start = ((), (), s32[]{:S(2)}) async-start(), calls=%async_computation.1 | async-start | bytes 393216
  316.1 14.8 %collective-permute-start.7 = (f32[8,4,1,128]{3,2,1,0:T(1,128)S(1)}, f32[8,4,1,128]{3,2,1,0:T(1,128)S(1)}, u32[]{:S(2)}, u32[]{:S(2)}) collective-permute-start(f32[8,4,1,128]{3,2,1,0:T(1,128)S(1)} %get-tuple-element.447), channel_id=1, source_target_pairs={{1,0},{2,1},{3,2},{4,3},{5,4},{6,5},{7,6},{8,7},{9,8},{10,9},{11,1... | collective-permute-start | bytes 49160 | tf_op jit(solution)/shard_map/ppermute | solution.py:30
  317.4 18.3 %collective-permute-start.6 = (f32[8,4,1,128]{3,2,1,0:T(1,128)S(1)}, f32[8,4,1,128]{3,2,1,0:T(1,128)S(1)}, u32[]{:S(2)}, u32[]{:S(2)}) collective-permute-start(f32[8,4,1,128]{3,2,1,0:T(1,128)S(1)} %get-tuple-element.446), channel_id=1, source_target_pairs={{0,1},{1,2},{2,3},{3,4},{4,5},{5,6},{6,7},{7,8},{8,9},{9,10},{10,1... | collective-permute-start | bytes 49160 | tf_op jit(solution)/shard_map/ppermute | solution.py:27
  335.7 13.9 %copy-start.38 = (f32[8]{0:T(128)S(1)}, f32[8]{0:T(128)}, u32[]{:S(2)}) copy-start(f32[8]{0:T(128)} %copy-done.37) | copy-start | bytes 100
  335.8 277.0 %copy-start.2 = (f32[3,1,498]{2,1,0:T(1,128)S(1)}, f32[3,1,498]{2,1,0:T(1,128)}, u32[]{:S(2)}) copy-start(f32[3,1,498]{2,1,0:T(1,128)} %param.17) | copy-start | bytes 17932
  854.4 1.7 copy-start.6
  854.4 1.7 copy-start.7
  854.5 1.7 copy-start.8
  854.5 1.7 copy-start.9
  854.5 1.7 copy-start.10
  854.5 1.7 copy-start.11
  854.5 1.7 copy-start.12
  854.5 1.7 copy-start.13
  854.5 1.7 copy-start.14
  854.5 1.7 copy-start.15
  854.5 1.7 copy-start.16
  854.5 1.7 copy-start.17
  854.6 1.7 copy-start.18
  854.6 1.7 copy-start.19
  854.6 1.7 copy-start.20
  854.6 1.7 copy-start.21
  854.6 1.7 copy-start.22
  854.6 1.7 copy-start.23
  854.6 1.7 copy-start.24
  854.6 1.7 copy-start.25
  854.6 1.7 copy-start.26
  854.6 1.7 copy-start.27
  854.7 1.7 copy-start.28
  854.7 1.7 copy-start.29
  (2 other events, 1.4 us)
Sparse Core Ops, SparseCore 0:
  315.9 296.8 all-reduce.28
  856.3 300.7 all-reduce.30
where the time goes:
time: 1180 us; the launch traced here: 1170 us
  waiting for transfers between devices  561 us (48%)
  blocking collectives  326 us (28%)
  other arithmetic  165 us (14%)
  local copies, waits for them, and re-layouts  63.2 us (5%)
  starting transfers between devices  32.7 us (3%)
  between operations  16 us (1%)
    unnamed x4, waiting for transfers between devices  560 us
    all_gather x2, blocking collectives, body(): lax.all_gather(vert_pos, 'gx', axis=1, tiled=True)  173 us
    all_gather x2, blocking collectives, body(): lax.all_gather(vert_vel, 'gx', axis=1, tiled=True)  154 us
    reduce_sum x16, other arithmetic, solvent_terms(): jnp.sum(scalar * delta_w, 2)  37.9 us
    reduce_sum x10, other arithmetic, couple_cell(): jnp.sum(push_w, 1)  36.5 us
  transfers between devices with their start and end apart: 10, of which 3 were waited for; matrix products, arithmetic and copies ran while one was open for 11% of the time, Pallas kernels for 0%

commit v1 on v0

v1 whole, which is shorter than its diff:
```python
import functools

import jax
import jax.numpy as jnp
from jax import lax
from jax.experimental import pallas as pl
from jax.experimental.pallas import tpu as pltpu
from jax.sharding import PartitionSpec as P

SPAN = 3
MAXCOV = 5
DT = 0.04
FAR = 1000.0
ZMID = 16.0
NOISE = 15.0 * 0.7071067811865476
TW = 2
TF = 4
LANES = 128
NV = 498
NVP = 512
NB = 1488
NBP = 1536
NT = 992
NTP = 1024
COLS = NBP + 2 * NTP
SLABS = 32
ROWS = 16

F32 = jnp.float32
BF16 = jnp.bfloat16


def nn(a, b):
    return lax.dot_general(a, b, (((1,), (0,)), ((), ())), preferred_element_type=F32)


def nt(a, b):
    return lax.dot_general(a, b, (((1,), (1,)), ((), ())), preferred_element_type=F32)


def split3(x):
    a = x.astype(BF16).astype(F32)
    r = x - a
    b = r.astype(BF16).astype(F32)
    return a, b, r - b


def row_ids(n):
    return lax.broadcasted_iota(jnp.int32, (8, n), 0)


def rows_of(pieces, n):
    row = row_ids(n)
    out = jnp.zeros((8, n), F32)
    for r, piece in pieces:
        out = jnp.where(row == r, piece, out)
    return out


def dots(st, n):
    row = row_ids(n)
    vel = pltpu.roll(st, 5, 0)
    sq = jnp.sum(jnp.where(row < 3, st * st, 0.0), 0, keepdims=True)
    xv = jnp.sum(jnp.where(row < 3, st * vel, 0.0), 0, keepdims=True)
    return vel, sq, xv


def left_features(st):
    n = st.shape[1]
    a, b, c = split3(st)
    _, sq, xv = dots(st, n)
    s1, s2, s3 = split3(1.0 - sq)
    v1, v2, v3 = split3(xv)
    e1 = rows_of([(0, s1), (1, s2), (2, s3), (3, v1), (4, v2), (5, v3), (6, 1.0), (7, 1.0)], n)
    e2 = rows_of([(0, 1.0)], n)
    return jnp.concatenate([a, a, a, b, b, c, e1, e2], 0)


def right_features(st):
    n = st.shape[1]
    row = row_ids(n)
    vel, sq, xv = dots(st, n)
    s1, s2, s3 = split3(-sq)
    v1, v2, v3 = split3(4.5 * xv)

    def pack(block, e1, e2):
        a, b, c = split3(block)
        return jnp.concatenate([a, b, c, a, b, a, e1, e2], 0).astype(BF16)

    zero = jnp.zeros((8, n), F32)
    near = pack(
        jnp.where(row < 3, 2.0 * st, 0.0),
        rows_of([(0, 1.0), (1, 1.0), (2, 1.0), (6, s1), (7, s2)], n),
        rows_of([(0, s3)], n),
    )
    pos = pltpu.roll(st, 3, 0)
    drag = pack(
        -4.5 * jnp.where(row < 3, vel, jnp.where(row < 6, pos, 0.0)),
        rows_of([(3, 4.5), (4, 4.5), (5, 4.5), (6, v1), (7, v2)], n),
        rows_of([(0, v3)], n),
    )
    up = pltpu.roll(st, 7, 0)
    down = pltpu.roll(st, 1, 0)
    kick = pack(
        NOISE * jnp.where(row == 6, up, jnp.where(row == 7, down, 0.0)),
        rows_of([(6, 25.0)], n),
        zero,
    )
    return near, drag, kick


def sum_features(st):
    n = st.shape[1]
    row = row_ids(n)
    q = jnp.where(row < 3, st, jnp.where(row == 3, 1.0, 0.0))
    a, b, c = split3(q)
    return jnp.concatenate([a, b, c, jnp.zeros((8, n), F32)], 0).astype(BF16)


def halves(s):
    hi = s.astype(BF16)
    return hi, (s - hi.astype(F32)).astype(BF16)


def moment(acc):
    return acc[0:8] + acc[8:16] + acc[16:24]


def cover_slots(starts, j, idx, slot_map, count_ref):
    for m in range(8):
        idx[m] = 0
    count = jnp.int32(0)
    shifts = (-2, -1, 1, 2)
    counts = [jnp.int32(0) for _ in shifts]
    for c in range(SLABS):
        s = starts[c]
        idx[jnp.minimum(count, 7)] = c
        covered = (s <= j) & (j < s + SPAN)
        count = count + covered.astype(jnp.int32)
        if slot_map is not None:
            for k, shift in enumerate(shifts):
                slot_map[k * SLABS + c] = jnp.minimum(counts[k], 7)
                cov = (s <= j + shift) & (j + shift < s + SPAN)
                counts[k] = counts[k] + cov.astype(jnp.int32)
    count = jnp.minimum(count, MAXCOV)
    count_ref[0] = count
    return count


def bond_force(pos, m_ref, rest_len, rest_area):
    p3 = jnp.concatenate(split3(pos), 0).astype(BF16)

    def fold(x):
        return x[0:24] + x[24:48] + x[48:72]

    def back(g, cols):
        g3 = jnp.concatenate(split3(g), 0).astype(BF16)
        return fold(nt(g3, m_ref[:, cols]))

    one, two, three = slice(0, NBP), slice(NBP, NBP + NTP), slice(NBP + NTP, COLS)
    d = fold(nn(p3, m_ref[:, one]))
    sq_len = rest_len * rest_len
    stretch = d[0:8] * d[0:8] + d[8:16] * d[8:16] + d[16:24] * d[16:24]
    coef = (stretch - sq_len) * (-2.0 / sq_len)
    force = back(jnp.concatenate([coef * d[0:8], coef * d[8:16], coef * d[16:24]], 0), one)
    e1 = fold(nn(p3, m_ref[:, two]))
    e2 = fold(nn(p3, m_ref[:, three]))

    def cross(a, b):
        ax, ay, az = a
        bx, by, bz = b
        return ay * bz - az * by, az * bx - ax * bz, ax * by - ay * bx

    a = (e1[0:8], e1[8:16], e1[16:24])
    b = (e2[0:8], e2[8:16], e2[16:24])
    n = cross(a, b)
    sq_area = rest_area * rest_area
    area = 0.25 * (n[0] * n[0] + n[1] * n[1] + n[2] * n[2])
    coef = (area - sq_area) * (-0.125 / sq_area)
    g = (coef * n[0], coef * n[1], coef * n[2])
    force = force + back(jnp.concatenate(cross(b, g), 0), two)
    return force + back(jnp.concatenate(cross(g, a), 0), three)


def particle_frames(i, j, own, wl, wh, gl, gh):
    row = row_ids(LANES)

    def framed(tile, w, f, bad):
        shift = jnp.where(row == 2, -ZMID, 0.0)
        shift = jnp.where(row == 0, w + bad, shift)
        shift = jnp.where(row == 1, f, shift)
        return tile + shift

    wlo = jnp.where(i == 0, FAR, 0.0)
    whi = jnp.where(i == ROWS - 1, FAR, 0.0)
    flo = jnp.where(j == 0, FAR, 0.0)
    fhi = jnp.where(j == SLABS - 1, FAR, 0.0)
    near = []
    for w in range(TW + 2):
        bad_w = wlo if w == 0 else whi if w == TW + 1 else 0.0
        for f in range(TF + 2):
            if f == 0:
                tile, bad = gl[w], bad_w + flo
            elif f == TF + 1:
                tile, bad = gh[w], bad_w + fhi
            elif w == 0:
                tile, bad = wl[0, f - 1], bad_w
            elif w == TW + 1:
                tile, bad = wh[0, f - 1], bad_w
            else:
                tile, bad = own[w - 1, f - 1], 0.0
            near.append(framed(tile, float(w - 1), float(f - 1), bad))
    return near


def forces(near, count, cs, ms, lfeat, lcell, rnear, rdrag, qown, fpart, fcell):
    nst = jnp.concatenate(near, 1)
    own_tiles = [near[(w + 1) * (TF + 2) + f + 1] for w in range(TW) for f in range(TF)]
    own = jnp.concatenate(own_tiles, 1)
    ra, rc, rb = right_features(own)
    rnear[...] = ra
    rdrag[...] = rc
    qown[...] = sum_features(own)
    lfeat[...] = left_features(nst).T.astype(BF16)
    qnear = sum_features(nst)
    for w in range(TW):
        for f in range(TF):
            t = w * TF + f
            cols = slice(t * LANES, (t + 1) * LANES)
            rt = jnp.concatenate([ra[:, cols], rc[:, cols], rb[:, cols]], 1)
            acc = jnp.zeros((32, LANES), F32)
            for dw in range(3):
                first = ((w + dw) * (TF + 2) + f) * LANES
                out = nn(lfeat[first : first + 3 * LANES, :], rt)
                weight = jnp.maximum(out[:, :LANES], 0.0)
                s = weight * (out[:, 2 * LANES :] - weight * out[:, LANES : 2 * LANES])
                hi, lo = halves(s)
                q = qnear[:, first : first + 3 * LANES]
                acc = acc + nn(q, hi) + nn(q, lo)
            fpart[:, cols] = acc

    def one_cell(m, carry):
        st = cs[m]
        lcell[...] = left_features(st).T.astype(BF16)
        q = sum_features(st)
        total = jnp.zeros((32, NVP), F32)
        for k in range(4):
            cols = slice(k * 256, (k + 1) * 256)
            weight = jnp.maximum(nn(lcell[...], rnear[:, cols]), 0.0)
            s = weight * (4.0 - weight * nn(lcell[...], rdrag[:, cols]))
            hi, lo = halves(s)
            fpart[:, cols] += nn(q, hi) + nn(q, lo)
            qo = qown[:, cols]
            total = total + nt(qo, hi) + nt(qo, lo)
        fcell[m] = total
        return carry

    lax.fori_loop(0, count, one_cell, 0)
    return own


def move_particles(own_refs, fpart, own, store):
    mom = moment(fpart[...])
    force = own * mom[3:4] - mom
    n = own.shape[1]
    row = row_ids(n)
    kick = pltpu.roll(jnp.where(row < 3, DT * force, 0.0), 3, 0)
    for w in range(TW):
        for f in range(TF):
            t = w * TF + f
            st = own_refs[w, f] + kick[:, t * LANES : (t + 1) * LANES]
            vel = pltpu.roll(st, 5, 0)
            st = st + jnp.where(row_ids(LANES) < 3, DT * vel, 0.0)
            store(w, f, st)


def first_kernel(
    starts, own, wl, wh, gl, gh, kicks, cells, hi_ids, lo_ids, rest_len, rest_area,
    out_t, out_c, out_r, m_ref,
    idx, cnt, cs, ps, lfeat, lcell, rnear, rdrag, qown, fpart, fcell,
):
    i = lax.axis_index("wa")
    j = lax.axis_index("gx")
    count = cover_slots(starts, j, idx, None, cnt)
    for k in range(COLS // 512):
        cols = slice(k * 512, (k + 1) * 512)
        vid = lax.broadcasted_iota(jnp.int32, (NVP, 512), 0)
        plus = (vid == hi_ids[:, cols]).astype(F32)
        minus = (vid == lo_ids[:, cols]).astype(F32)
        m_ref[:, cols] = (plus - minus).astype(BF16)
    ps[...] = jnp.zeros((48, NVP), F32)
    row = row_ids(NVP)
    shift = jnp.where(row == 1, -(j * TF).astype(F32), jnp.where(row == 2, -ZMID, 0.0))
    away = jnp.where(row < 3, FAR, 0.0)
    for m in range(MAXCOV):
        st = jnp.where(m < count, cells[idx[m]] + shift, away)
        cs[m] = st
        for c in range(6):
            ps[c * 8 + m : c * 8 + m + 1, :] = st[c : c + 1, :]
    near = particle_frames(i, j, own, wl, wh, gl, gh)
    fcell[...] = jnp.zeros(fcell.shape, F32)
    own_st = forces(near, count, cs, None, lfeat, lcell, rnear, rdrag, qown, fpart, fcell)

    def store(w, f, st):
        out_t[w, f, 0:6, :] = st[0:6]
        out_t[w, f, 6:8, :] = kicks[w, f]

    move_particles(own, fpart, own_st, store)
    out_r[...] = jnp.zeros((24, NVP), F32)
    for m in range(MAXCOV):
        mom = moment(fcell[m])
        react = DT * (cs[m] * mom[3:4] - mom)
        for c in range(3):
            out_r[c * 8 + m : c * 8 + m + 1, :] = react[c : c + 1, :]
    bond = bond_force(ps[0:24, :], m_ref, rest_len[...], rest_area[...])
    out_c[0:24, :] = ps[0:24, :]
    out_c[24:48, :] = ps[24:48, :] + DT * bond + out_r[...]


def second_kernel(
    starts, own, wl, wh, gl, gh, cst, r0, r1, r2, r3, m_ref, rest_len, rest_area,
    out_t, out_s,
    idx, cnt, smap, cs, ps, lfeat, lcell, rnear, rdrag, qown, fpart, fcell,
):
    i = lax.axis_index("wa")
    j = lax.axis_index("gx")
    count = cover_slots(starts, j, idx, smap, cnt)
    ps[...] = cst[...]
    for m in range(MAXCOV):
        cell = idx[m]
        s = starts[cell]
        for k, (shift, ref) in enumerate(((-2, r0), (-1, r1), (1, r2), (2, r3))):
            slot = smap[k * SLABS + cell]
            there = (m < count) & (s <= j + shift) & (j + shift < s + SPAN)
            for c in range(3):
                at = 24 + c * 8 + m
                got = ref[pl.ds(c * 8 + slot, 1), :]
                ps[at : at + 1, :] += jnp.where(there, got, 0.0)
    ps[0:24, :] += DT * ps[24:48, :]
    for m in range(MAXCOV):
        cs[m] = jnp.zeros((8, NVP), F32)
        for c in range(6):
            cs[m, c : c + 1, :] = ps[c * 8 + m : c * 8 + m + 1, :]
    near = particle_frames(i, j, own, wl, wh, gl, gh)
    fcell[...] = jnp.zeros(fcell.shape, F32)
    own_st = forces(near, count, cs, None, lfeat, lcell, rnear, rdrag, qown, fpart, fcell)

    def store(w, f, st):
        out_t[w, f] = st

    move_particles(own, fpart, own_st, store)
    bond = bond_force(ps[0:24, :], m_ref, rest_len[...], rest_area[...])
    ps[24:48, :] += DT * bond
    out_s[...] = jnp.zeros(out_s.shape, F32)
    row = row_ids(NVP)
    shift = jnp.where(row == 1, (j * TF).astype(F32), jnp.where(row == 2, ZMID, 0.0))
    for m in range(MAXCOV):
        cell = idx[m]
        mom = moment(fcell[m])
        react = DT * (cs[m] * mom[3:4] - mom)
        share = pltpu.roll(jnp.where(row < 3, react, 0.0), 3, 0)
        for c in range(6):
            cs[m, c : c + 1, :] = ps[c * 8 + m : c * 8 + m + 1, :]
        whole = jnp.where(starts[cell] == j, cs[m] + shift, 0.0)

        @pl.when(m < count)
        def _():
            out_s[cell] = whole + share


def vmem():
    return pl.BlockSpec(memory_space=pltpu.VMEM)


def smem():
    return pl.BlockSpec(memory_space=pltpu.SMEM)


def common_scratch():
    return [
        pltpu.VMEM((8, 8, NVP), F32),
        pltpu.VMEM((48, NVP), F32),
        pltpu.VMEM((24 * LANES, 64), BF16),
        pltpu.VMEM((NVP, 64), BF16),
        pltpu.VMEM((64, 8 * LANES), BF16),
        pltpu.VMEM((64, 8 * LANES), BF16),
        pltpu.VMEM((32, 8 * LANES), BF16),
        pltpu.VMEM((32, 8 * LANES), F32),
        pltpu.VMEM((8, 32, NVP), F32),
    ]


def moves(axis, shift):
    count = lax.axis_size(axis)
    return [(k, k + shift) for k in range(count) if 0 <= k + shift < count]


def halo(tiles):
    wl = lax.ppermute(tiles[TW - 1 :], "wa", moves("wa", 1))
    wh = lax.ppermute(tiles[:1], "wa", moves("wa", -1))
    last = jnp.concatenate([wl[:, TF - 1], tiles[:, TF - 1], wh[:, TF - 1]], 0)
    head = jnp.concatenate([wl[:, 0], tiles[:, 0], wh[:, 0]], 0)
    gl = lax.ppermute(last, "gx", moves("gx", 1))
    gh = lax.ppermute(head, "gx", moves("gx", -1))
    return wl, wh, gl, gh


def body(
    part_pos, part_vel, random_kicks, vert_pos, vert_vel,
    cover_start, bond_ends, triangles, rest_len, rest_area,
):
    tiles = jnp.transpose(
        jnp.concatenate([part_pos, part_vel, random_kicks[0:2]], 0), (1, 2, 0, 3)
    )
    kicks = jnp.transpose(random_kicks[2:4], (1, 2, 0, 3))
    heads = [bond_ends[:, 0], triangles[:, 1], triangles[:, 2]]
    tails = [bond_ends[:, 1], triangles[:, 0], triangles[:, 0]]
    sizes = [NBP, NTP, NTP]

    def lay(parts):
        return jnp.concatenate(
            [jnp.pad(p, (0, n - p.shape[0]), constant_values=-1) for p, n in zip(parts, sizes)]
        )[None]

    hi_ids, lo_ids = lay(heads), lay(tails)
    rl = jnp.pad(rest_len, (0, NBP - NB), constant_values=1.0)[None]
    ra = jnp.pad(rest_area, (0, NTP - NT), constant_values=1.0)[None]
    cell = jnp.concatenate(
        [
            jnp.pad(vert_pos[:, 0], ((0, 0), (0, NVP - NV)), constant_values=FAR),
            jnp.pad(vert_vel[:, 0], ((0, 2), (0, NVP - NV))),
        ],
        0,
    )
    cells = lax.all_to_all(
        jnp.broadcast_to(cell[None], (SLABS, 8, NVP)), "gx", 0, 0, tiled=True
    )
    shape = jax.ShapeDtypeStruct
    wl, wh, gl, gh = halo(tiles)
    new_tiles, cst, share, incidence = pl.pallas_call(
        first_kernel,
        out_shape=(
            shape((TW, TF, 8, LANES), F32),
            shape((48, NVP), F32),
            shape((24, NVP), F32),
            shape((NVP, COLS), BF16),
        ),
        in_specs=[smem()] + [vmem()] * 11,
        out_specs=tuple([vmem()] * 4),
        scratch_shapes=[pltpu.SMEM((8,), jnp.int32), pltpu.SMEM((1,), jnp.int32)]
        + common_scratch(),
        name="first_step",
    )(cover_start, tiles, wl, wh, gl, gh, kicks, cells, hi_ids, lo_ids, rl, ra)
    got = [lax.ppermute(share, "gx", moves("gx", -s)) for s in (-2, -1, 1, 2)]
    wl, wh, gl, gh = halo(new_tiles)
    last_tiles, sends = pl.pallas_call(
        second_kernel,
        out_shape=(shape((TW, TF, 8, LANES), F32), shape((SLABS, 8, NVP), F32)),
        in_specs=[smem()] + [vmem()] * 13,
        out_specs=(vmem(), vmem()),
        scratch_shapes=[
            pltpu.SMEM((8,), jnp.int32),
            pltpu.SMEM((1,), jnp.int32),
            pltpu.SMEM((4 * SLABS,), jnp.int32),
        ]
        + common_scratch(),
        name="second_step",
    )(cover_start, new_tiles, wl, wh, gl, gh, cst, *got, incidence, rl, ra)
    final = jnp.sum(lax.all_to_all(sends, "gx", 0, 0, tiled=True), 0)
    new_vel = final[3:6, None, :NV]
    new_pos = final[0:3, None, :NV] + DT * new_vel
    out = jnp.transpose(last_tiles, (2, 0, 1, 3))
    return out[0:3], out[3:6], new_pos, new_vel


def solution(mesh):
    in_specs = (
        P(None, "wa", "gx", None),
        P(None, "wa", "gx", None),
        P(None, "wa", "gx", None),
        P(None, ("wa", "gx"), None),
        P(None, ("wa", "gx"), None),
        P("wa"),
        P(),
        P(),
        P(),
        P(),
    )
    out_specs = (
        P(None, "wa", "gx", None),
        P(None, "wa", "gx", None),
        P(None, ("wa", "gx"), None),
        P(None, ("wa", "gx"), None),
    )
    return jax.shard_map(body, mesh=mesh, in_specs=in_specs, out_specs=out_specs, check_vma=False)
```

time: 1180 us -> 157 us (0.13)
  the two profiles are of different devices: /device:TPU:4 before, /device:TPU:10 now
where the time goes in v1:
time: 157 us; the launch traced here: 154 us
  starting transfers between devices  67.4 us (43%)
  Pallas kernels  37.3 us (24%)
  waiting for transfers between devices  32.5 us (21%)
  local copies, waits for them, and re-layouts  15.9 us (10%)
    pallas_call x1, Pallas kernels, body(): pl.pallas_call(first_kernel, out_shape=(shape((TW, TF, 8, LANES), F32), s...  19.4 us
    pallas_call x1, Pallas kernels, body(): pl.pallas_call(second_kernel, out_shape=(shape((TW, TF, 8, LANES), F32),...  17.9 us
    all_to_all x1, starting transfers between devices, body(): final = jnp.sum(lax.all_to_all(sends, 'gx', 0, 0, tiled=True), 0)  16.4 us
    all_to_all x1, starting transfers between devices, body(): lax.all_to_all(jnp.broadcast_to(cell[None], (SLABS, 8, NVP)), 'gx', 0, 0,...  15.3 us
    all_to_all x1, waiting for transfers between devices, body(): final = jnp.sum(lax.all_to_all(sends, 'gx', 0, 0, tiled=True), 0)  13.8 us
    ppermute x4, starting transfers between devices, body(): got = [lax.ppermute(share, 'gx', moves('gx', -s)) for s in (-2, -1, 1, 2)]  13.8 us
    all_to_all x1, waiting for transfers between devices, body(): lax.all_to_all(jnp.broadcast_to(cell[None], (SLABS, 8, NVP)), 'gx', 0, 0,...  7.65 us
    ppermute x2, starting transfers between devices, halo(): wh = lax.ppermute(tiles[:1], 'wa', moves('wa', -1))  6.96 us
  transfers between devices with their start and end apart: 14, of which 7 were waited for; matrix products, arithmetic and copies ran while one was open for 7% of the time, Pallas kernels for 0%

profile of v1, /device:TPU:10, one launch (start us, length us, event | category | flops | bytes accessed | tf_op | source)
XLA Modules:
  0.0 154.2 jit_solution(2619167670585479234)
XLA Ops:
  0.6 0.7 copy.15
  1.3 0.7 copy.16
  2.1 0.7 fusion.7
  2.8 0.0 copy-start.1
  2.8 3.7 %collective-permute-start.1 = (f32[1,4,8,128]{3,2,1,0:T(8,128)S(1)}, f32[1,4,8,128]{3,2,1,0:T(8,128)S(1)}, u32[]{:S(2)}, u32[]{:S(2)}) collective-permute-start(f32[1,4,8,128]{3,2,1,0:T(8,128)S(1)} %get-tuple-element.30), channel_id=1, source_target_pairs={{32,0},{64,32},{96,64},{128,96},{160,128},{192,160},{224,192},{256... | collective-permute-start | bytes 49160 | tf_op jit(solution)/shard_map/ppermute | solution.py:400
  6.5 1.9 %collective-permute-start = (f32[1,4,8,128]{3,2,1,0:T(8,128)S(1)}, f32[1,4,8,128]{3,2,1,0:T(8,128)S(1)}, u32[]{:S(2)}, u32[]{:S(2)}) collective-permute-start(f32[1,4,8,128]{3,2,1,0:T(8,128)S(1)} %get-tuple-element.31), channel_id=1, source_target_pairs={{0,32},{32,64},{64,96},{96,128},{128,160},{160,192},{192,224},{224... | collective-permute-start | bytes 49160 | tf_op jit(solution)/shard_map/ppermute | solution.py:399
  8.4 0.7 copy_bitcast_fusion.1
  9.2 0.9 broadcast_in_dim.22
  10.0 15.3 %all-to-all-start = ((f32[32,8,512]{2,1,0:T(8,128)}), f32[32,8,512]{2,1,0:T(8,128)S(1)}, u32[]{:S(2)}, u32[]{:S(2)}) async-start(f32[32,8,512]{2,1,0:T(8,128)} %broadcast_in_dim.22), calls=%async_computation | async-start | bytes 1048576 | tf_op jit(solution)/shard_map/all_to_all | solution.py:435
  25.3 0.8 fusion.6
  26.2 0.8 slice_reduce_fusion
  27.0 0.0 collective-permute-done.1.wh
  27.0 0.0 copy-start.8
  27.0 0.0 collective-permute-done.wl
  27.1 3.4 %collective-permute-start.2 = (f32[4,8,128]{2,1,0:T(8,128)S(1)}, f32[4,8,128]{2,1,0:T(8,128)S(1)}, u32[]{:S(2)}, u32[]{:S(2)}) collective-permute-start(f32[4,8,128]{2,1,0:T(8,128)S(1)} %pad_maximum_fusion), channel_id=1, source_target_pairs={{0,1},{1,2},{2,3},{3,4},{4,5},{5,6},{6,7},{7,8},{8,9},{9,10},{10,1... | collective-permute-start | bytes 49160 | tf_op jit(solution)/shard_map/ppermute | solution.py:403
  30.5 2.5 %collective-permute-start.3 = (f32[4,8,128]{2,1,0:T(8,128)S(1)}, f32[4,8,128]{2,1,0:T(8,128)S(1)}, u32[]{:S(2)}, u32[]{:S(2)}) collective-permute-start(f32[4,8,128]{2,1,0:T(8,128)S(1)} %pad_maximum_fusion.1), channel_id=1, source_target_pairs={{1,0},{2,1},{3,2},{4,3},{5,4},{6,5},{7,6},{8,7},{9,8},{10,9},{11,1... | collective-permute-start | bytes 49160 | tf_op jit(solution)/shard_map/ppermute | solution.py:404
  33.0 1.3 pad.42
  34.2 0.7 pad.41
  34.9 0.6 broadcast_in_dim.25.rest_len
  35.5 0.6 copy.31
  36.2 0.6 broadcast_in_dim.24.lo_ids
  36.8 0.6 broadcast_in_dim.23.hi_ids
  37.4 0.2 collective-permute-done.2.gl
  37.6 0.9 collective-permute-done.3.gh
  38.5 7.7 %all-to-all-done.cells = f32[32,8,512]{2,1,0:T(8,128)S(1)} async-done(((f32[32,8,512]{2,1,0:T(8,128)}), f32[32,8,512]{2,1,0:T(8,128)S(1)}, u32[]{:S(2)}, u32[]{:S(2)}) %all-to-all-start) | async-done | bytes 524320 | tf_op jit(solution)/shard_map/all_to_all | solution.py:435
  46.1 0.0 copy-done.8
  46.2 0.8 copy-done
  46.9 19.4 %first_step.1 = (f32[2,4,8,128]{3,2,1,0:T(8,128)}, f32[48,512]{1,0:T(8,128)}, f32[24,512]{1,0:T(8,128)}, bf16[512,3584]{1,0:T(8,128)(2,1)}) custom-call(s32[32]{0:T(128)} %starts.3, f32[2,4,8,128]{3,2,1,0:T(8,128)} %copy-done.1, f32[1,4,8,128]{3,2,1,0:T(8,128)} %copy-done.9, f32[1,4,8,128]{3,2,1,0:T(8,128)} %copy-done.8, f32[4,8,128]{2,1,0:T(8,128)} %copy-done.12, ...), custom_call_target="tpu_custom_call" | custom-call | tf_op jit(solution)/shard_map/first_step/pallas_call | solution.py:440
  66.3 0.7 fusion.3
  67.0 3.3 %collective-permute-start.5 = (f32[1,4,8,128]{3,2,1,0:T(8,128)S(1)}, f32[1,4,8,128]{3,2,1,0:T(8,128)S(1)}, u32[]{:S(2)}, u32[]{:S(2)}) collective-permute-start(f32[1,4,8,128]{3,2,1,0:T(8,128)S(1)} %get-tuple-element.26), channel_id=1, source_target_pairs={{32,0},{64,32},{96,64},{128,96},{160,128},{192,160},{224,192},{256... | collective-permute-start | bytes 49160 | tf_op jit(solution)/shard_map/ppermute | solution.py:400
  70.3 0.7 slice_bitcast_fusion
  71.0 1.3 collective-permute-start.11
  72.3 1.9 %collective-permute-start.10 = (f32[24,512]{1,0:T(8,128)}, f32[24,512]{1,0:T(8,128)S(1)}, u32[]{:S(2)}, u32[]{:S(2)}) collective-permute-start(f32[24,512]{1,0:T(8,128)} %get-tuple-element.12), channel_id=1, source_target_pairs={{1,0},{2,1},{3,2},{4,3},{5,4},{6,5},{7,6},{8,7},{9,8},{10,9},{11,1... | collective-permute-start | bytes 147464 | tf_op jit(solution)/shard_map/ppermute | solution.py:454
  74.3 4.0 %collective-permute-start.9 = (f32[24,512]{1,0:T(8,128)}, f32[24,512]{1,0:T(8,128)S(1)}, u32[]{:S(2)}, u32[]{:S(2)}) collective-permute-start(f32[24,512]{1,0:T(8,128)} %get-tuple-element.12), channel_id=1, source_target_pairs={{0,1},{1,2},{2,3},{3,4},{4,5},{5,6},{6,7},{7,8},{8,9},{9,10},{10,1... | collective-permute-start | bytes 147464 | tf_op jit(solution)/shard_map/ppermute | solution.py:454
  78.3 6.6 %collective-permute-start.8 = (f32[24,512]{1,0:T(8,128)}, f32[24,512]{1,0:T(8,128)S(1)}, u32[]{:S(2)}, u32[]{:S(2)}) collective-permute-start(f32[24,512]{1,0:T(8,128)} %get-tuple-element.12), channel_id=1, source_target_pairs={{0,2},{1,3},{2,4},{3,5},{4,6},{5,7},{6,8},{7,9},{8,10},{9,11},{10,... | collective-permute-start | bytes 147464 | tf_op jit(solution)/shard_map/ppermute | solution.py:454
  84.9 0.0 collective-permute-done.5.wh
  84.9 0.0 copy-start.6
  84.9 1.9 %collective-permute-start.4 = (f32[1,4,8,128]{3,2,1,0:T(8,128)S(1)}, f32[1,4,8,128]{3,2,1,0:T(8,128)S(1)}, u32[]{:S(2)}, u32[]{:S(2)}) collective-permute-start(f32[1,4,8,128]{3,2,1,0:T(8,128)S(1)} %get-tuple-element.27), channel_id=1, source_target_pairs={{0,32},{32,64},{64,96},{96,128},{128,160},{160,192},{192,224},{224... | collective-permute-start | bytes 49160 | tf_op jit(solution)/shard_map/ppermute | solution.py:399
  86.8 4.0 %collective-permute-done.4.wl = f32[1,4,8,128]{3,2,1,0:T(8,128)S(1)} collective-permute-done((f32[1,4,8,128]{3,2,1,0:T(8,128)S(1)}, f32[1,4,8,128]{3,2,1,0:T(8,128)S(1)}, u32[]{:S(2)}, u32[]{:S(2)}) %collective-permute-start.4) | collective-permute-done | bytes 16416 | tf_op jit(solution)/shard_map/ppermute | solution.py:399
  90.8 3.4 %collective-permute-start.6 = (f32[4,8,128]{2,1,0:T(8,128)S(1)}, f32[4,8,128]{2,1,0:T(8,128)S(1)}, u32[]{:S(2)}, u32[]{:S(2)}) collective-permute-start(f32[4,8,128]{2,1,0:T(8,128)S(1)} %pad_maximum_fusion.2), channel_id=1, source_target_pairs={{0,1},{1,2},{2,3},{3,4},{4,5},{5,6},{6,7},{7,8},{8,9},{9,10},{10,1... | collective-permute-start | bytes 49160 | tf_op jit(solution)/shard_map/ppermute | solution.py:403
  94.3 2.2 %collective-permute-done.6.gl = f32[4,8,128]{2,1,0:T(8,128)S(1)} collective-permute-done((f32[4,8,128]{2,1,0:T(8,128)S(1)}, f32[4,8,128]{2,1,0:T(8,128)S(1)}, u32[]{:S(2)}, u32[]{:S(2)}) %collective-permute-start.6) | collective-permute-done | bytes 16416 | tf_op jit(solution)/shard_map/ppermute | solution.py:403
  96.5 1.9 %collective-permute-start.7 = (f32[4,8,128]{2,1,0:T(8,128)S(1)}, f32[4,8,128]{2,1,0:T(8,128)S(1)}, u32[]{:S(2)}, u32[]{:S(2)}) collective-permute-start(f32[4,8,128]{2,1,0:T(8,128)S(1)} %pad_maximum_fusion.3), channel_id=1, source_target_pairs={{1,0},{2,1},{3,2},{4,3},{5,4},{6,5},{7,6},{8,7},{9,8},{10,9},{11,1... | collective-permute-start | bytes 49160 | tf_op jit(solution)/shard_map/ppermute | solution.py:404
  98.4 3.7 %collective-permute-done.7.gh = f32[4,8,128]{2,1,0:T(8,128)S(1)} collective-permute-done((f32[4,8,128]{2,1,0:T(8,128)S(1)}, f32[4,8,128]{2,1,0:T(8,128)S(1)}, u32[]{:S(2)}, u32[]{:S(2)}) %collective-permute-start.7) | collective-permute-done | bytes 16416 | tf_op jit(solution)/shard_map/ppermute | solution.py:404
  102.1 0.0 collective-permute-done.11.r3
  102.1 0.0 collective-permute-done.10.r2
  102.1 0.0 collective-permute-done.9.r1
  102.1 0.0 collective-permute-done.8.r0
  102.1 0.0 copy-start.5
  102.2 0.0 copy-done.6
  102.2 0.0 copy-done.7
  102.2 0.0 copy-done.10
  102.2 0.5 copy-done.11
  102.7 0.0 copy-done.2
  102.7 0.0 copy-done.3
  102.7 0.0 copy-done.4
  102.8 0.0 copy-done.5
  102.8 17.9 %second_step.1 = (f32[2,4,8,128]{3,2,1,0:T(8,128)}, f32[32,8,512]{2,1,0:T(8,128)}) custom-call(s32[32]{0:T(128)} %starts.3, f32[2,4,8,128]{3,2,1,0:T(8,128)} %get-tuple-element.10.own, f32[1,4,8,128]{3,2,1,0:T(8,128)} %copy-done.7, f32[1,4,8,128]{3,2,1,0:T(8,128)} %copy-done.6, f32[4,8,128]{2,1,0:T(8,128)} %copy-done.10, f32[4,8,128]{2,1,0:T(8,128)} %copy-done.11, ...), custom_call_target="tpu_custom_call" | custom-call | tf_op jit(solution)/shard_map/second_step/pallas_call | solution.py:456
  120.7 16.4 %all-to-all-start.1 = ((f32[32,8,512]{2,1,0:T(8,128)}), f32[32,8,512]{2,1,0:T(8,128)S(1)}, u32[]{:S(2)}, u32[]{:S(2)}) async-start(f32[32,8,512]{2,1,0:T(8,128)} %get-tuple-element.15), calls=%async_computation.1 | async-start | bytes 1048576 | tf_op jit(solution)/shard_map/all_to_all | solution.py:469
  137.1 0.8 fusion.2
  138.0 0.6 copy.21
  138.6 0.6 copy.20
  139.2 13.8 %all-to-all-done.1 = f32[32,8,512]{2,1,0:T(8,128)S(1)} async-done(((f32[32,8,512]{2,1,0:T(8,128)}), f32[32,8,512]{2,1,0:T(8,128)S(1)}, u32[]{:S(2)}, u32[]{:S(2)}) %all-to-all-start.1) | async-done | bytes 524320 | tf_op jit(solution)/shard_map/all_to_all | solution.py:469
  153.0 0.6 broadcast_in_dim.27
  153.6 0.6 add.25
  (31 shorter events, 0.2 us)
Async XLA Ops:
  2.8 43.3 %copy-start.1 = (f32[2,4,8,128]{3,2,1,0:T(8,128)}, f32[2,4,8,128]{3,2,1,0:T(8,128)S(1)}, u32[]{:S(2)}) copy-start(f32[2,4,8,128]{3,2,1,0:T(8,128)S(1)} %maximum_bitcast_fusion.own) | copy-start | bytes 98308
  2.8 24.2 %collective-permute-start.1 = (f32[1,4,8,128]{3,2,1,0:T(8,128)S(1)}, f32[1,4,8,128]{3,2,1,0:T(8,128)S(1)}, u32[]{:S(2)}, u32[]{:S(2)}) collective-permute-start(f32[1,4,8,128]{3,2,1,0:T(8,128)S(1)} %get-tuple-element.30), channel_id=1, source_target_pairs={{32,0},{64,32},{96,64},{128,96},{160,128},{192,160},{224,192},{256... | collective-permute-start | bytes 49160 | tf_op jit(solution)/shard_map/ppermute | solution.py:400
  6.5 20.5 %collective-permute-start = (f32[1,4,8,128]{3,2,1,0:T(8,128)S(1)}, f32[1,4,8,128]{3,2,1,0:T(8,128)S(1)}, u32[]{:S(2)}, u32[]{:S(2)}) collective-permute-start(f32[1,4,8,128]{3,2,1,0:T(8,128)S(1)} %get-tuple-element.31), channel_id=1, source_target_pairs={{0,32},{32,64},{64,96},{96,128},{128,160},{160,192},{192,224},{224... | collective-permute-start | bytes 49160 | tf_op jit(solution)/shard_map/ppermute | solution.py:399
  10.0 36.1 %all-to-all-start = ((f32[32,8,512]{2,1,0:T(8,128)}), f32[32,8,512]{2,1,0:T(8,128)S(1)}, u32[]{:S(2)}, u32[]{:S(2)}) async-start(f32[32,8,512]{2,1,0:T(8,128)} %broadcast_in_dim.22), calls=%async_computation | async-start | bytes 1048576 | tf_op jit(solution)/shard_map/all_to_all | solution.py:435
  27.0 19.1 %copy-start.8 = (f32[1,4,8,128]{3,2,1,0:T(8,128)}, f32[1,4,8,128]{3,2,1,0:T(8,128)S(1)}, u32[]{:S(2)}) copy-start(f32[1,4,8,128]{3,2,1,0:T(8,128)S(1)} %collective-permute-done.1.wh) | copy-start | bytes 49156
  27.0 19.1 %copy-start.9 = (f32[1,4,8,128]{3,2,1,0:T(8,128)}, f32[1,4,8,128]{3,2,1,0:T(8,128)S(1)}, u32[]{:S(2)}) copy-start(f32[1,4,8,128]{3,2,1,0:T(8,128)S(1)} %collective-permute-done.wl) | copy-start | bytes 49156
  27.1 10.5 %collective-permute-start.2 = (f32[4,8,128]{2,1,0:T(8,128)S(1)}, f32[4,8,128]{2,1,0:T(8,128)S(1)}, u32[]{:S(2)}, u32[]{:S(2)}) collective-permute-start(f32[4,8,128]{2,1,0:T(8,128)S(1)} %pad_maximum_fusion), channel_id=1, source_target_pairs={{0,1},{1,2},{2,3},{3,4},{4,5},{5,6},{6,7},{7,8},{8,9},{9,10},{10,1... | collective-permute-start | bytes 49160 | tf_op jit(solution)/shard_map/ppermute | solution.py:403
  30.5 8.0 %collective-permute-start.3 = (f32[4,8,128]{2,1,0:T(8,128)S(1)}, f32[4,8,128]{2,1,0:T(8,128)S(1)}, u32[]{:S(2)}, u32[]{:S(2)}) collective-permute-start(f32[4,8,128]{2,1,0:T(8,128)S(1)} %pad_maximum_fusion.1), channel_id=1, source_target_pairs={{1,0},{2,1},{3,2},{4,3},{5,4},{6,5},{7,6},{8,7},{9,8},{10,9},{11,1... | collective-permute-start | bytes 49160 | tf_op jit(solution)/shard_map/ppermute | solution.py:404
  37.6 8.6 %copy-start.12 = (f32[4,8,128]{2,1,0:T(8,128)}, f32[4,8,128]{2,1,0:T(8,128)S(1)}, u32[]{:S(2)}) copy-start(f32[4,8,128]{2,1,0:T(8,128)S(1)} %collective-permute-done.2.gl) | copy-start | bytes 49156
  38.5 7.7 %copy-start.13 = (f32[4,8,128]{2,1,0:T(8,128)}, f32[4,8,128]{2,1,0:T(8,128)S(1)}, u32[]{:S(2)}) copy-start(f32[4,8,128]{2,1,0:T(8,128)S(1)} %collective-permute-done.3.gh) | copy-start | bytes 49156
  46.1 0.8 copy-start
  67.0 17.8 %collective-permute-start.5 = (f32[1,4,8,128]{3,2,1,0:T(8,128)S(1)}, f32[1,4,8,128]{3,2,1,0:T(8,128)S(1)}, u32[]{:S(2)}, u32[]{:S(2)}) collective-permute-start(f32[1,4,8,128]{3,2,1,0:T(8,128)S(1)} %get-tuple-element.26), channel_id=1, source_target_pairs={{32,0},{64,32},{96,64},{128,96},{160,128},{192,160},{224,192},{256... | collective-permute-start | bytes 49160 | tf_op jit(solution)/shard_map/ppermute | solution.py:400
  71.0 31.1 %collective-permute-start.11 = (f32[24,512]{1,0:T(8,128)}, f32[24,512]{1,0:T(8,128)S(1)}, u32[]{:S(2)}, u32[]{:S(2)}) collective-permute-start(f32[24,512]{1,0:T(8,128)} %get-tuple-element.12), channel_id=1, source_target_pairs={{2,0},{3,1},{4,2},{5,3},{6,4},{7,5},{8,6},{9,7},{10,8},{11,9},{12,... | collective-permute-start | bytes 147464 | tf_op jit(solution)/shard_map/ppermute | solution.py:454
  72.3 29.8 %collective-permute-start.10 = (f32[24,512]{1,0:T(8,128)}, f32[24,512]{1,0:T(8,128)S(1)}, u32[]{:S(2)}, u32[]{:S(2)}) collective-permute-start(f32[24,512]{1,0:T(8,128)} %get-tuple-element.12), channel_id=1, source_target_pairs={{1,0},{2,1},{3,2},{4,3},{5,4},{6,5},{7,6},{8,7},{9,8},{10,9},{11,1... | collective-permute-start | bytes 147464 | tf_op jit(solution)/shard_map/ppermute | solution.py:454
  74.3 27.9 %collective-permute-start.9 = (f32[24,512]{1,0:T(8,128)}, f32[24,512]{1,0:T(8,128)S(1)}, u32[]{:S(2)}, u32[]{:S(2)}) collective-permute-start(f32[24,512]{1,0:T(8,128)} %get-tuple-element.12), channel_id=1, source_target_pairs={{0,1},{1,2},{2,3},{3,4},{4,5},{5,6},{6,7},{7,8},{8,9},{9,10},{10,1... | collective-permute-start | bytes 147464 | tf_op jit(solution)/shard_map/ppermute | solution.py:454
  78.3 23.8 %collective-permute-start.8 = (f32[24,512]{1,0:T(8,128)}, f32[24,512]{1,0:T(8,128)S(1)}, u32[]{:S(2)}, u32[]{:S(2)}) collective-permute-start(f32[24,512]{1,0:T(8,128)} %get-tuple-element.12), channel_id=1, source_target_pairs={{0,2},{1,3},{2,4},{3,5},{4,6},{5,7},{6,8},{7,9},{8,10},{9,11},{10,... | collective-permute-start | bytes 147464 | tf_op jit(solution)/shard_map/ppermute | solution.py:454
  84.9 17.3 %copy-start.6 = (f32[1,4,8,128]{3,2,1,0:T(8,128)}, f32[1,4,8,128]{3,2,1,0:T(8,128)S(1)}, u32[]{:S(2)}) copy-start(f32[1,4,8,128]{3,2,1,0:T(8,128)S(1)} %collective-permute-done.5.wh) | copy-start | bytes 49156
  84.9 6.0 %collective-permute-start.4 = (f32[1,4,8,128]{3,2,1,0:T(8,128)S(1)}, f32[1,4,8,128]{3,2,1,0:T(8,128)S(1)}, u32[]{:S(2)}, u32[]{:S(2)}) collective-permute-start(f32[1,4,8,128]{3,2,1,0:T(8,128)S(1)} %get-tuple-element.27), channel_id=1, source_target_pairs={{0,32},{32,64},{64,96},{96,128},{128,160},{160,192},{192,224},{224... | collective-permute-start | bytes 49160 | tf_op jit(solution)/shard_map/ppermute | solution.py:399
  90.8 11.3 %copy-start.7 = (f32[1,4,8,128]{3,2,1,0:T(8,128)}, f32[1,4,8,128]{3,2,1,0:T(8,128)S(1)}, u32[]{:S(2)}) copy-start(f32[1,4,8,128]{3,2,1,0:T(8,128)S(1)} %collective-permute-done.4.wl) | copy-start | bytes 49156
  90.8 5.6 %collective-permute-start.6 = (f32[4,8,128]{2,1,0:T(8,128)S(1)}, f32[4,8,128]{2,1,0:T(8,128)S(1)}, u32[]{:S(2)}, u32[]{:S(2)}) collective-permute-start(f32[4,8,128]{2,1,0:T(8,128)S(1)} %pad_maximum_fusion.2), channel_id=1, source_target_pairs={{0,1},{1,2},{2,3},{3,4},{4,5},{5,6},{6,7},{7,8},{8,9},{9,10},{10,1... | collective-permute-start | bytes 49160 | tf_op jit(solution)/shard_map/ppermute | solution.py:403
  96.5 5.7 %copy-start.10 = (f32[4,8,128]{2,1,0:T(8,128)}, f32[4,8,128]{2,1,0:T(8,128)S(1)}, u32[]{:S(2)}) copy-start(f32[4,8,128]{2,1,0:T(8,128)S(1)} %collective-permute-done.6.gl) | copy-start | bytes 49156
  96.5 5.6 %collective-permute-start.7 = (f32[4,8,128]{2,1,0:T(8,128)S(1)}, f32[4,8,128]{2,1,0:T(8,128)S(1)}, u32[]{:S(2)}, u32[]{:S(2)}) collective-permute-start(f32[4,8,128]{2,1,0:T(8,128)S(1)} %pad_maximum_fusion.3), channel_id=1, source_target_pairs={{1,0},{2,1},{3,2},{4,3},{5,4},{6,5},{7,6},{8,7},{9,8},{10,9},{11,1... | collective-permute-start | bytes 49160 | tf_op jit(solution)/shard_map/ppermute | solution.py:404
  102.1 0.6 copy-start.11
  102.1 0.6 copy-start.2
  102.1 0.6 copy-start.3
  102.1 0.6 copy-start.4
  102.1 0.6 copy-start.5
  120.7 32.3 %all-to-all-start.1 = ((f32[32,8,512]{2,1,0:T(8,128)}), f32[32,8,512]{2,1,0:T(8,128)S(1)}, u32[]{:S(2)}, u32[]{:S(2)}) async-start(f32[32,8,512]{2,1,0:T(8,128)} %get-tuple-element.15), calls=%async_computation.1 | async-start | bytes 1048576 | tf_op jit(solution)/shard_map/all_to_all | solution.py:469

commit v2 on v1

v2 whole, which is shorter than its diff:
```python
import jax
import jax.numpy as jnp
from jax import lax
from jax.experimental import pallas as pl
from jax.experimental.pallas import tpu as pltpu
from jax.sharding import PartitionSpec as P

SPAN = 3
MAXCOV = 5
DT = 0.04
FAR = 1000.0
ZMID = 16.0
NOISE = 15.0 * 0.7071067811865476
TW = 2
TF = 4
LANES = 128
NV = 498
NVP = 512
NB = 1488
NBP = 1536
NT = 992
NTP = 1024
COLS = NBP + 2 * NTP
SLABS = 32
ROWS = 16

F32 = jnp.float32
BF16 = jnp.bfloat16


def nn(a, b):
    return lax.dot_general(a, b, (((1,), (0,)), ((), ())), preferred_element_type=F32)


def nt(a, b):
    return lax.dot_general(a, b, (((1,), (1,)), ((), ())), preferred_element_type=F32)


def split3(x):
    a = x.astype(BF16).astype(F32)
    r = x - a
    b = r.astype(BF16).astype(F32)
    return a, b, r - b


def row_ids(n):
    return lax.broadcasted_iota(jnp.int32, (8, n), 0)


def rows_of(pieces, n):
    row = row_ids(n)
    out = jnp.zeros((8, n), F32)
    for r, piece in pieces:
        out = jnp.where(row == r, piece, out)
    return out


def dots(st, n):
    row = row_ids(n)
    vel = pltpu.roll(st, 5, 0)
    sq = jnp.sum(jnp.where(row < 3, st * st, 0.0), 0, keepdims=True)
    xv = jnp.sum(jnp.where(row < 3, st * vel, 0.0), 0, keepdims=True)
    return vel, sq, xv


def left_features(st):
    n = st.shape[1]
    a, b, c = split3(st)
    _, sq, xv = dots(st, n)
    s1, s2, s3 = split3(1.0 - sq)
    v1, v2, v3 = split3(xv)
    e1 = rows_of([(0, s1), (1, s2), (2, s3), (3, v1), (4, v2), (5, v3), (6, 1.0), (7, 1.0)], n)
    e2 = rows_of([(0, 1.0)], n)
    return jnp.concatenate([a, a, a, b, b, c, e1, e2], 0)


def right_features(st):
    n = st.shape[1]
    row = row_ids(n)
    vel, sq, xv = dots(st, n)
    s1, s2, s3 = split3(-sq)
    v1, v2, v3 = split3(4.5 * xv)

    def pack(block, e1, e2):
        a, b, c = split3(block)
        return jnp.concatenate([a, b, c, a, b, a, e1, e2], 0).astype(BF16)

    zero = jnp.zeros((8, n), F32)
    near = pack(
        jnp.where(row < 3, 2.0 * st, 0.0),
        rows_of([(0, 1.0), (1, 1.0), (2, 1.0), (6, s1), (7, s2)], n),
        rows_of([(0, s3)], n),
    )
    pos = pltpu.roll(st, 3, 0)
    drag = pack(
        -4.5 * jnp.where(row < 3, vel, jnp.where(row < 6, pos, 0.0)),
        rows_of([(3, 4.5), (4, 4.5), (5, 4.5), (6, v1), (7, v2)], n),
        rows_of([(0, v3)], n),
    )
    up = pltpu.roll(st, 7, 0)
    down = pltpu.roll(st, 1, 0)
    kick = pack(
        NOISE * jnp.where(row == 6, up, jnp.where(row == 7, down, 0.0)),
        rows_of([(6, 25.0)], n),
        zero,
    )
    return near, drag, kick


def sum_features(st):
    n = st.shape[1]
    row = row_ids(n)
    q = jnp.where(row < 3, st, jnp.where(row == 3, 1.0, 0.0))
    a, b, c = split3(q)
    return jnp.concatenate([a, b, c, jnp.zeros((8, n), F32)], 0).astype(BF16)


def halves(s):
    hi = s.astype(BF16)
    return hi, (s - hi.astype(F32)).astype(BF16)


def moment(acc):
    return acc[0:8] + acc[8:16] + acc[16:24]


def cover_slots(starts, j, idx, slot_map, count_ref):
    for m in range(8):
        idx[m] = 0
    count = jnp.int32(0)
    shifts = (-2, -1, 1, 2)
    counts = [jnp.int32(0) for _ in shifts]
    for c in range(SLABS):
        s = starts[c]
        idx[jnp.minimum(count, 7)] = c
        covered = (s <= j) & (j < s + SPAN)
        count = count + covered.astype(jnp.int32)
        if slot_map is not None:
            for k, shift in enumerate(shifts):
                slot_map[k * SLABS + c] = jnp.minimum(counts[k], 7)
                cov = (s <= j + shift) & (j + shift < s + SPAN)
                counts[k] = counts[k] + cov.astype(jnp.int32)
    count = jnp.minimum(count, MAXCOV)
    count_ref[0] = count
    return count


def bond_force(pos, m_ref, par):
    p3 = jnp.concatenate(split3(pos), 0).astype(BF16)

    def fold(x):
        return x[0:24] + x[24:48] + x[48:72]

    def back(g, cols):
        g3 = jnp.concatenate(split3(g), 0).astype(BF16)
        return fold(nt(g3, m_ref[:, cols]))

    one, two, three = slice(0, NBP), slice(NBP, NBP + NTP), slice(NBP + NTP, COLS)
    d = fold(nn(p3, m_ref[:, one]))
    stretch = d[0:8] * d[0:8] + d[8:16] * d[8:16] + d[16:24] * d[16:24]
    coef = (stretch - par[0:1, :]) * par[1:2, :]
    force = back(jnp.concatenate([coef * d[0:8], coef * d[8:16], coef * d[16:24]], 0), one)
    e1 = fold(nn(p3, m_ref[:, two]))
    e2 = fold(nn(p3, m_ref[:, three]))

    def cross(a, b):
        ax, ay, az = a
        bx, by, bz = b
        return ay * bz - az * by, az * bx - ax * bz, ax * by - ay * bx

    a = (e1[0:8], e1[8:16], e1[16:24])
    b = (e2[0:8], e2[8:16], e2[16:24])
    n = cross(a, b)
    area = 0.25 * (n[0] * n[0] + n[1] * n[1] + n[2] * n[2])
    coef = (area - par[2:3, :NTP]) * par[3:4, :NTP]
    g = (coef * n[0], coef * n[1], coef * n[2])
    force = force + back(jnp.concatenate(cross(b, g), 0), two)
    return force + back(jnp.concatenate(cross(g, a), 0), three)


def solvent(near, lfeat, fpart):
    nst = jnp.concatenate(near, 1)
    own = own_of(near)
    ra, rc, rb = right_features(own)
    lfeat[...] = left_features(nst).T.astype(BF16)
    qnear = sum_features(nst)
    for w in range(TW):
        for f in range(TF):
            t = w * TF + f
            cols = slice(t * LANES, (t + 1) * LANES)
            rt = jnp.concatenate([ra[:, cols], rc[:, cols], rb[:, cols]], 1)
            acc = jnp.zeros((32, LANES), F32)
            for dw in range(3):
                first = ((w + dw) * (TF + 2) + f) * LANES
                out = nn(lfeat[first : first + 3 * LANES, :], rt)
                weight = jnp.maximum(out[:, :LANES], 0.0)
                s = weight * (out[:, 2 * LANES :] - weight * out[:, LANES : 2 * LANES])
                hi, lo = halves(s)
                q = qnear[:, first : first + 3 * LANES]
                acc = acc + nn(q, hi) + nn(q, lo)
            fpart[:, cols] = acc
    return own


def own_of(near):
    return jnp.concatenate(
        [near[(w + 1) * (TF + 2) + f + 1] for w in range(TW) for f in range(TF)], 1
    )


def membrane(own, count, cs, lcell, rnear, rdrag, qown, fpart, fcell):
    ra, rc, _ = right_features(own)
    rnear[...] = ra
    rdrag[...] = rc
    qown[...] = sum_features(own)
    fpart[...] = jnp.zeros(fpart.shape, F32)
    fcell[...] = jnp.zeros(fcell.shape, F32)

    def one_cell(m, carry):
        st = cs[m]
        lcell[...] = left_features(st).T.astype(BF16)
        q = sum_features(st)
        total = jnp.zeros((32, NVP), F32)
        for k in range(4):
            cols = slice(k * 256, (k + 1) * 256)
            weight = jnp.maximum(nn(lcell[...], rnear[:, cols]), 0.0)
            s = weight * (4.0 - weight * nn(lcell[...], rdrag[:, cols]))
            hi, lo = halves(s)
            fpart[:, cols] += nn(q, hi) + nn(q, lo)
            qo = qown[:, cols]
            total = total + nt(qo, hi) + nt(qo, lo)
        fcell[m] = total
        return carry

    lax.fori_loop(0, count, one_cell, 0)


def force_of(own, fpart):
    mom = moment(fpart[...])
    return jnp.where(row_ids(own.shape[1]) < 3, own * mom[3:4] - mom, 0.0)


def moved(tile, force):
    st = tile + pltpu.roll(DT * force, 3, 0)
    vel = pltpu.roll(st, 5, 0)
    return st + jnp.where(row_ids(LANES) < 3, DT * vel, 0.0)


def own_frame(t0, t1):
    row = row_ids(LANES)
    out = []
    for w, ref in enumerate((t0, t1)):
        for f in range(TF):
            shift = jnp.where(row == 0, float(w), jnp.where(row == 1, float(f), 0.0))
            out.append(ref[0, f] + jnp.where(row == 2, -ZMID, shift))
    return jnp.concatenate(out, 1)


def near_frames(t0, t1, wl, wh, gl, gh):
    i = lax.axis_index("wa")
    j = lax.axis_index("gx")
    row = row_ids(LANES)
    wlo = jnp.where(i == 0, FAR, 0.0)
    whi = jnp.where(i == ROWS - 1, FAR, 0.0)
    flo = jnp.where(j == 0, FAR, 0.0)
    fhi = jnp.where(j == SLABS - 1, FAR, 0.0)
    near = []
    for w, ref in enumerate((wl, t0, t1, wh)):
        bad_w = wlo if w == 0 else whi if w == TW + 1 else 0.0
        for f in range(TF + 2):
            if f == 0:
                tile, bad = gl[w], bad_w + flo
            elif f == TF + 1:
                tile, bad = gh[w], bad_w + fhi
            else:
                tile, bad = ref[0, f - 1], bad_w
            shift = jnp.where(row == 2, -ZMID, 0.0)
            shift = jnp.where(row == 0, float(w - 1) + bad, shift)
            near.append(tile + jnp.where(row == 1, float(f - 1), shift))
    return near


def early_kernel(
    t0, t1, wl, wh, gl, gh, bonds, corners, rest_len, rest_area,
    out_f, m_ref, par_ref,
    lfeat, fpart,
):
    def fill(start, ids, hi, lo, size, padded):
        m_ref[:, start + padded - LANES : start + padded] = jnp.zeros((NVP, LANES), BF16)
        for a in range(0, size, 512):
            b = min(a + 512, size)
            vid = lax.broadcasted_iota(jnp.int32, (NVP, b - a), 0)
            plus = (vid == ids[hi : hi + 1, a:b]).astype(F32)
            minus = (vid == ids[lo : lo + 1, a:b]).astype(F32)
            m_ref[:, start + a : start + b] = (plus - minus).astype(BF16)

    fill(0, bonds, 0, 1, NB, NBP)
    fill(NBP, corners, 1, 0, NT, NTP)
    fill(NBP + NTP, corners, 2, 0, NT, NTP)
    par_ref[...] = jnp.ones((4, NBP), F32)
    sq = rest_len[...] * rest_len[...]
    par_ref[0:1, 0:NB] = sq
    par_ref[1:2, 0:NB] = -2.0 / sq
    sq = rest_area[...] * rest_area[...]
    par_ref[2:3, 0:NT] = sq
    par_ref[3:4, 0:NT] = -0.125 / sq
    own = solvent(near_frames(t0, t1, wl, wh, gl, gh), lfeat, fpart)
    out_f[...] = force_of(own, fpart)


def lay_rows(ps, m, st):
    for c in range(6):
        ps[c * 8 + m : c * 8 + m + 1, :] = st[c : c + 1, :]


def first_kernel(
    starts, t0, t1, kicks, cells, solv,
    out_0, out_1, out_c, out_r,
    idx, cnt, cs, lcell, rnear, rdrag, qown, fpart, fcell,
):
    j = lax.axis_index("gx")
    count = cover_slots(starts, j, idx, None, cnt)
    out_c[...] = jnp.zeros((48, NVP), F32)
    row = row_ids(NVP)
    shift = jnp.where(row == 1, -(j * TF).astype(F32), jnp.where(row == 2, -ZMID, 0.0))
    away = jnp.where(row < 3, FAR, 0.0)
    for m in range(MAXCOV):
        cs[m] = jnp.zeros((8, NVP), F32)
        for k in range(4):
            cs[m, 0:6, k * LANES : (k + 1) * LANES] = cells[idx[m], k * 6 : k * 6 + 6, :]
        st = jnp.where(m < count, cs[m] + shift, away)
        cs[m] = st
        lay_rows(out_c, m, st)
    own = own_frame(t0, t1)
    membrane(own, count, cs, lcell, rnear, rdrag, qown, fpart, fcell)
    force = solv[...] + force_of(own, fpart)
    for w, (ref, out) in enumerate(((t0, out_0), (t1, out_1))):
        for f in range(TF):
            t = w * TF + f
            st = moved(ref[0, f], force[:, t * LANES : (t + 1) * LANES])
            out[0, f, 0:6, :] = st[0:6]
            out[0, f, 6:8, :] = kicks[w, f]
    out_r[...] = jnp.zeros((24, NVP), F32)
    for m in range(MAXCOV):
        mom = moment(fcell[m])
        react = DT * (cs[m] * mom[3:4] - mom)
        for c in range(3):
            out_r[c * 8 + m : c * 8 + m + 1, :] = react[c : c + 1, :]


def bond_kernel(cst, m_ref, par_ref, out_b):
    out_b[...] = DT * bond_force(cst[0:24, :], m_ref, par_ref)


def second_kernel(
    starts, t0, t1, cst, share, bond, r0, r1, r2, r3, m_ref, par_ref,
    out_f, out_s,
    idx, cnt, smap, cs, ps, lcell, rnear, rdrag, qown, fpart, fcell,
):
    j = lax.axis_index("gx")
    count = cover_slots(starts, j, idx, smap, cnt)
    ps[0:24, :] = cst[0:24, :]
    ps[24:48, :] = cst[24:48, :] + bond[...] + share[...]
    for m in range(MAXCOV):
        cell = idx[m]
        s = starts[cell]
        for k, (shift, ref) in enumerate(((-2, r0), (-1, r1), (1, r2), (2, r3))):
            slot = smap[k * SLABS + cell]
            there = (m < count) & (s <= j + shift) & (j + shift < s + SPAN)
            for c in range(3):
                at = 24 + c * 8 + m
                got = ref[pl.ds(c * 8 + slot, 1), :]
                ps[at : at + 1, :] += jnp.where(there, got, 0.0)
    ps[0:24, :] += DT * ps[24:48, :]
    for m in range(MAXCOV):
        cs[m] = jnp.zeros((8, NVP), F32)
        for c in range(6):
            cs[m, c : c + 1, :] = ps[c * 8 + m : c * 8 + m + 1, :]
    own = own_frame(t0, t1)
    membrane(own, count, cs, lcell, rnear, rdrag, qown, fpart, fcell)
    out_f[...] = force_of(own, fpart)
    ps[24:48, :] += DT * bond_force(ps[0:24, :], m_ref, par_ref)
    out_s[...] = jnp.zeros(out_s.shape, F32)
    row = row_ids(NVP)
    shift = jnp.where(row == 1, (j * TF).astype(F32), jnp.where(row == 2, ZMID, 0.0))
    for m in range(MAXCOV):
        cell = idx[m]
        mom = moment(fcell[m])
        react = DT * (cs[m] * mom[3:4] - mom)
        push = pltpu.roll(jnp.where(row < 3, react, 0.0), 3, 0)
        for c in range(6):
            cs[m, c : c + 1, :] = ps[c * 8 + m : c * 8 + m + 1, :]
        whole = push + jnp.where(starts[cell] == j, cs[m] + shift, 0.0)

        @pl.when(m < count)
        def _():
            for k in range(4):
                out_s[cell, k * 6 : k * 6 + 6, :] = whole[0:6, k * LANES : (k + 1) * LANES]


def late_kernel(t0, t1, wl, wh, gl, gh, memb, out_p, out_v, lfeat, fpart):
    own = solvent(near_frames(t0, t1, wl, wh, gl, gh), lfeat, fpart)
    force = memb[...] + force_of(own, fpart)
    for w, ref in enumerate((t0, t1)):
        for f in range(TF):
            t = w * TF + f
            st = moved(ref[0, f], force[:, t * LANES : (t + 1) * LANES])
            for c in range(3):
                out_p[c, w, f : f + 1, :] = st[c : c + 1]
                out_v[c, w, f : f + 1, :] = st[c + 3 : c + 4]


def vmem():
    return pl.BlockSpec(memory_space=pltpu.VMEM)


def smem():
    return pl.BlockSpec(memory_space=pltpu.SMEM)


def slot_scratch(extra):
    return (
        [pltpu.SMEM((8,), jnp.int32), pltpu.SMEM((1,), jnp.int32)]
        + extra
        + [
            pltpu.VMEM((NVP, 64), BF16),
            pltpu.VMEM((64, 8 * LANES), BF16),
            pltpu.VMEM((64, 8 * LANES), BF16),
            pltpu.VMEM((32, 8 * LANES), BF16),
            pltpu.VMEM((32, 8 * LANES), F32),
            pltpu.VMEM((8, 32, NVP), F32),
        ]
    )


def solvent_scratch():
    return [pltpu.VMEM((24 * LANES, 64), BF16), pltpu.VMEM((32, 8 * LANES), F32)]


def call(kernel, name, outs, scratch, args, scalars=0):
    return pl.pallas_call(
        kernel,
        out_shape=tuple(jax.ShapeDtypeStruct(s, t) for s, t in outs),
        in_specs=[smem()] * scalars + [vmem()] * (len(args) - scalars),
        out_specs=tuple(vmem() for _ in outs),
        scratch_shapes=scratch,
        name=name,
    )(*args)


def moves(axis, shift):
    count = lax.axis_size(axis)
    return [(k, k + shift) for k in range(count) if 0 <= k + shift < count]


def halo(t0, t1):
    wl = lax.ppermute(t1, "wa", moves("wa", 1))
    wh = lax.ppermute(t0, "wa", moves("wa", -1))

    def column(f):
        return jnp.concatenate([wl[:, f], t0[:, f], t1[:, f], wh[:, f]], 0)

    gl = lax.ppermute(column(TF - 1), "gx", moves("gx", 1))
    gh = lax.ppermute(column(0), "gx", moves("gx", -1))
    return wl, wh, gl, gh


def body(
    part_pos, part_vel, random_kicks, vert_pos, vert_vel,
    cover_start, bond_ends, triangles, rest_len, rest_area,
):
    cell = jnp.concatenate(
        [
            jnp.pad(vert_pos[:, 0], ((0, 0), (0, NVP - NV)), constant_values=FAR),
            jnp.pad(vert_vel[:, 0], ((0, 0), (0, NVP - NV))),
        ],
        0,
    )
    cell = jnp.transpose(cell.reshape(6, 4, LANES), (1, 0, 2)).reshape(24, LANES)
    cells = lax.all_to_all(
        jnp.broadcast_to(cell[None], (SLABS, 24, LANES)), "gx", 0, 0, tiled=True
    )
    tiles = jnp.transpose(
        jnp.concatenate([part_pos, part_vel, random_kicks[0:2]], 0), (1, 2, 0, 3)
    )
    t0, t1 = tiles[:1], tiles[1:]
    kicks = jnp.transpose(random_kicks[2:4], (1, 2, 0, 3))
    part = ((8, TW * TF * LANES), F32)
    row = ((1, TF, 8, LANES), F32)
    solv, incidence, par = call(
        early_kernel,
        "early",
        [part, ((NVP, COLS), BF16), ((4, NBP), F32)],
        solvent_scratch(),
        (t0, t1, *halo(t0, t1), bond_ends.T, triangles.T, rest_len[None], rest_area[None]),
    )
    cell_scratch = pltpu.VMEM((8, 8, NVP), F32)
    n0, n1, cst, share = call(
        first_kernel,
        "first",
        [row, row, ((48, NVP), F32), ((24, NVP), F32)],
        slot_scratch([cell_scratch]),
        (cover_start, t0, t1, kicks, cells, solv),
        1,
    )
    got = [lax.ppermute(share, "gx", moves("gx", -s)) for s in (-2, -1, 1, 2)]
    (bond,) = call(bond_kernel, "bond", [((24, NVP), F32)], [], (cst, incidence, par))
    memb, sends = call(
        second_kernel,
        "second",
        [part, ((SLABS, 24, LANES), F32)],
        slot_scratch(
            [pltpu.SMEM((4 * SLABS,), jnp.int32), cell_scratch, pltpu.VMEM((48, NVP), F32)]
        ),
        (cover_start, n0, n1, cst, share, bond, *got, incidence, par),
        1,
    )
    final = jnp.sum(lax.all_to_all(sends, "gx", 0, 0, tiled=True), 0)
    out_pos, out_vel = call(
        late_kernel,
        "late",
        [((3, TW, TF, LANES), F32)] * 2,
        solvent_scratch(),
        (n0, n1, *halo(n0, n1), memb),
    )
    final = jnp.transpose(final.reshape(4, 6, LANES), (1, 0, 2)).reshape(6, NVP)
    new_vel = final[3:6, None, :NV]
    new_pos = final[0:3, None, :NV] + DT * new_vel
    return out_pos, out_vel, new_pos, new_vel


def solution(mesh):
    in_specs = (
        P(None, "wa", "gx", None),
        P(None, "wa", "gx", None),
        P(None, "wa", "gx", None),
        P(None, ("wa", "gx"), None),
        P(None, ("wa", "gx"), None),
        P("wa"),
        P(),
        P(),
        P(),
        P(),
    )
    out_specs = (
        P(None, "wa", "gx", None),
        P(None, "wa", "gx", None),
        P(None, ("wa", "gx"), None),
        P(None, ("wa", "gx"), None),
    )
    return jax.shard_map(body, mesh=mesh, in_specs=in_specs, out_specs=out_specs, check_vma=False)
```

time: 157 us -> 139 us (0.89)
  the two profiles are of different devices: /device:TPU:10 before, /device:TPU:134 now
where the time goes in v2:
time: 139 us; the launch traced here: 138 us
  starting transfers between devices  74.9 us (54%)
  Pallas kernels  45 us (32%)
  local copies, waits for them, and re-layouts  10.6 us (8%)
  waiting for transfers between devices  6.73 us (5%)
    pallas_call x5, Pallas kernels, call(): pl.pallas_call(kernel, out_shape=tuple((jax.ShapeDtypeStruct(s, t) for s,...  45 us
    all_to_all x1, starting transfers between devices, body(): final = jnp.sum(lax.all_to_all(sends, 'gx', 0, 0, tiled=True), 0)  20.2 us
    all_to_all x1, starting transfers between devices, body(): lax.all_to_all(jnp.broadcast_to(cell[None], (SLABS, 24, LANES)), 'gx', 0,...  14.5 us
    ppermute x4, starting transfers between devices, body(): got = [lax.ppermute(share, 'gx', moves('gx', -s)) for s in (-2, -1, 1, 2)]  13.5 us
    ppermute x2, starting transfers between devices, halo(): gh = lax.ppermute(column(0), 'gx', moves('gx', -1))  10.1 us
    ppermute x2, starting transfers between devices, halo(): wh = lax.ppermute(t0, 'wa', moves('wa', -1))  7.53 us
    ppermute x2, waiting for transfers between devices, halo(): gl = lax.ppermute(column(TF - 1), 'gx', moves('gx', 1))  6.69 us
    unnamed x39, local copies, waits for them, and re-layouts  5.91 us
  transfers between devices with their start and end apart: 14, of which 1 were waited for; matrix products, arithmetic and copies ran while one was open for 3% of the time, Pallas kernels for 26%

profile of v2, /device:TPU:134, one launch (start us, length us, event | category | flops | bytes accessed | tf_op | source)
XLA Modules:
  0.0 138.4 jit_solution(12698753738786248090)
XLA Ops:
  0.6 0.7 fusion.3
  1.4 0.7 copy.20
  2.1 0.7 copy.21
  2.8 0.0 copy-start.1
  2.8 0.0 copy-start.2
  2.8 1.9 %collective-permute-start = (f32[1,4,8,128]{3,2,1,0:T(8,128)S(1)}, f32[1,4,8,128]{3,2,1,0:T(8,128)S(1)}, u32[]{:S(2)}, u32[]{:S(2)}) collective-permute-start(f32[1,4,8,128]{3,2,1,0:T(8,128)S(1)} %get-tuple-element.30.t1), channel_id=1, source_target_pairs={{0,32},{32,64},{64,96},{96,128},{128,160},{160,192},{192,224},{224... | collective-permute-start | bytes 49160 | tf_op jit(solution)/shard_map/ppermute | solution.py:457
  4.8 4.5 %collective-permute-start.1 = (f32[1,4,8,128]{3,2,1,0:T(8,128)S(1)}, f32[1,4,8,128]{3,2,1,0:T(8,128)S(1)}, u32[]{:S(2)}, u32[]{:S(2)}) collective-permute-start(f32[1,4,8,128]{3,2,1,0:T(8,128)S(1)} %get-tuple-element.31.t0), channel_id=1, source_target_pairs={{32,0},{64,32},{96,64},{128,96},{160,128},{192,160},{224,192},{256... | collective-permute-start | bytes 49160 | tf_op jit(solution)/shard_map/ppermute | solution.py:458
  9.3 0.7 copy_bitcast_fusion.1
  10.0 0.8 broadcast_in_dim.18
  10.8 14.5 %all-to-all-start = ((f32[32,24,128]{2,1,0:T(8,128)}), f32[32,24,128]{2,1,0:T(8,128)S(1)}, u32[]{:S(2)}, u32[]{:S(2)}) async-start(f32[32,24,128]{2,1,0:T(8,128)} %broadcast_in_dim.18), calls=%async_computation | async-start | bytes 786432 | tf_op jit(solution)/shard_map/all_to_all | solution.py:480
  25.3 0.0 collective-permute-done.wl
  25.3 0.0 copy-start.9
  25.4 0.0 collective-permute-done.1.wh
  25.4 0.0 copy-start.10
  25.4 3.4 %collective-permute-start.2 = (f32[4,8,128]{2,1,0:T(8,128)S(1)}, f32[4,8,128]{2,1,0:T(8,128)S(1)}, u32[]{:S(2)}, u32[]{:S(2)}) collective-permute-start(f32[4,8,128]{2,1,0:T(8,128)S(1)} %pad_maximum_fusion), channel_id=1, source_target_pairs={{0,1},{1,2},{2,3},{3,4},{4,5},{5,6},{6,7},{7,8},{8,9},{9,10},{10,1... | collective-permute-start | bytes 49160 | tf_op jit(solution)/shard_map/ppermute | solution.py:463
  28.8 5.5 %collective-permute-start.3 = (f32[4,8,128]{2,1,0:T(8,128)S(1)}, f32[4,8,128]{2,1,0:T(8,128)S(1)}, u32[]{:S(2)}, u32[]{:S(2)}) collective-permute-start(f32[4,8,128]{2,1,0:T(8,128)S(1)} %pad_maximum_fusion.1), channel_id=1, source_target_pairs={{1,0},{2,1},{3,2},{4,3},{5,4},{6,5},{7,6},{8,7},{9,8},{10,9},{11,1... | collective-permute-start | bytes 49160 | tf_op jit(solution)/shard_map/ppermute | solution.py:464
  34.3 1.3 broadcast_in_dim.19.rest_len
  35.6 0.6 copy.31
  36.2 0.0 collective-permute-done.2.gl
  36.2 0.0 collective-permute-done.3.gh
  36.2 0.0 copy-start.14
  36.2 0.0 copy-done.1
  36.2 0.0 copy-done.2
  36.2 0.0 copy-done.9
  36.2 0.0 copy-done.10
  36.2 0.5 copy-done.13
  36.8 0.0 copy-done.14
  36.8 12.1 %early.1 = (f32[8,1024]{1,0:T(8,128)}, bf16[512,3584]{1,0:T(8,128)(2,1)}, f32[4,1536]{1,0:T(4,128)}) custom-call(f32[1,4,8,128]{3,2,1,0:T(8,128)} %copy-done.2, f32[1,4,8,128]{3,2,1,0:T(8,128)} %copy-done.1, f32[1,4,8,128]{3,2,1,0:T(8,128)} %copy-done.9, f32[1,4,8,128]{3,2,1,0:T(8,128)} %copy-done.10, f32[4,8,128]{2,1,0:T(8,128)} %copy-done.13, ...), custom_call_target="tpu_custom_call" | custom-call | tf_op jit(solution)/shard_map/early/pallas_call | solution.py:441
  48.9 0.0 all-to-all-done.cells
  48.9 0.8 copy-done
  49.7 8.4 %first.1 = (f32[1,4,8,128]{3,2,1,0:T(8,128)}, f32[1,4,8,128]{3,2,1,0:T(8,128)}, f32[48,512]{1,0:T(8,128)}, f32[24,512]{1,0:T(8,128)}) custom-call(s32[32]{0:T(128)} %starts.3, f32[1,4,8,128]{3,2,1,0:T(8,128)} %copy-done.2, f32[1,4,8,128]{3,2,1,0:T(8,128)} %copy-done.1, f32[2,4,2,128]{3,2,1,0:T(2,128)} %bitcast.52, f32[32,24,128]{2,1,0:T(8,128)} %copy-done, ...), custom_call_target="tpu_custom_call" | custom-call | tf_op jit(solution)/shard_map/first/pallas_call | solution.py:441
  58.1 4.9 %collective-permute-start.10 = (f32[24,512]{1,0:T(8,128)}, f32[24,512]{1,0:T(8,128)S(1)}, u32[]{:S(2)}, u32[]{:S(2)}) collective-permute-start(f32[24,512]{1,0:T(8,128)} %get-tuple-element.19.share), channel_id=1, source_target_pairs={{1,0},{2,1},{3,2},{4,3},{5,4},{6,5},{7,6},{8,7},{9,8},{10,9},{11,1... | collective-permute-start | bytes 147464 | tf_op jit(solution)/shard_map/ppermute | solution.py:506
  63.0 1.9 %collective-permute-start.11 = (f32[24,512]{1,0:T(8,128)}, f32[24,512]{1,0:T(8,128)S(1)}, u32[]{:S(2)}, u32[]{:S(2)}) collective-permute-start(f32[24,512]{1,0:T(8,128)} %get-tuple-element.19.share), channel_id=1, source_target_pairs={{2,0},{3,1},{4,2},{5,3},{6,4},{7,5},{8,6},{9,7},{10,8},{11,9},{12,... | collective-permute-start | bytes 147464 | tf_op jit(solution)/shard_map/ppermute | solution.py:506
  64.9 4.8 %collective-permute-start.8 = (f32[24,512]{1,0:T(8,128)}, f32[24,512]{1,0:T(8,128)S(1)}, u32[]{:S(2)}, u32[]{:S(2)}) collective-permute-start(f32[24,512]{1,0:T(8,128)} %get-tuple-element.19.share), channel_id=1, source_target_pairs={{0,2},{1,3},{2,4},{3,5},{4,6},{5,7},{6,8},{7,9},{8,10},{9,11},{10,... | collective-permute-start | bytes 147464 | tf_op jit(solution)/shard_map/ppermute | solution.py:506
  69.7 1.9 %collective-permute-start.9 = (f32[24,512]{1,0:T(8,128)}, f32[24,512]{1,0:T(8,128)S(1)}, u32[]{:S(2)}, u32[]{:S(2)}) collective-permute-start(f32[24,512]{1,0:T(8,128)} %get-tuple-element.19.share), channel_id=1, source_target_pairs={{0,1},{1,2},{2,3},{3,4},{4,5},{5,6},{6,7},{7,8},{8,9},{9,10},{10,1... | collective-permute-start | bytes 147464 | tf_op jit(solution)/shard_map/ppermute | solution.py:506
  71.7 3.0 %collective-permute-start.5 = (f32[1,4,8,128]{3,2,1,0:T(8,128)}, f32[1,4,8,128]{3,2,1,0:T(8,128)S(1)}, u32[]{:S(2)}, u32[]{:S(2)}) collective-permute-start(f32[1,4,8,128]{3,2,1,0:T(8,128)} %get-tuple-element.16.t0), channel_id=1, source_target_pairs={{32,0},{64,32},{96,64},{128,96},{160,128},{192,160},{224,192},{256... | collective-permute-start | bytes 49160 | tf_op jit(solution)/shard_map/ppermute | solution.py:458
  74.7 0.7 slice_bitcast_fusion.13
  75.3 4.5 %bond.1 = f32[24,512]{1,0:T(8,128)} custom-call(f32[48,512]{1,0:T(8,128)} %get-tuple-element.18.cst, bf16[512,3584]{1,0:T(8,128)(2,1)} %get-tuple-element.20.m_ref, f32[4,1536]{1,0:T(4,128)} %get-tuple-element.21.par_ref), custom_call_target="tpu_custom_call" | custom-call | tf_op jit(solution)/shard_map/bond/pallas_call | solution.py:441
  79.9 0.0 collective-permute-done.10.r2
  79.9 0.0 copy-done.3
  79.9 1.9 %collective-permute-start.4 = (f32[1,4,8,128]{3,2,1,0:T(8,128)S(1)}, f32[1,4,8,128]{3,2,1,0:T(8,128)S(1)}, u32[]{:S(2)}, u32[]{:S(2)}) collective-permute-start(f32[1,4,8,128]{3,2,1,0:T(8,128)S(1)} %copy-done.3), channel_id=1, source_target_pairs={{0,32},{32,64},{64,96},{96,128},{128,160},{160,192},{192,224},{224... | collective-permute-start | bytes 49160 | tf_op jit(solution)/shard_map/ppermute | solution.py:457
  81.8 0.0 collective-permute-done.11.r3
  81.8 0.0 copy-start.6
  81.9 0.0 collective-permute-done.8.r0
  81.9 0.0 copy-start.7
  81.9 0.0 collective-permute-done.9.r1
  81.9 0.6 copy-done.6
  82.5 0.0 copy-done.7
  82.5 0.6 copy-done.8
  83.1 12.1 %second.1 = (f32[8,1024]{1,0:T(8,128)}, f32[32,24,128]{2,1,0:T(8,128)}) custom-call(s32[32]{0:T(128)} %starts.3, f32[1,4,8,128]{3,2,1,0:T(8,128)} %get-tuple-element.16.t0, f32[1,4,8,128]{3,2,1,0:T(8,128)} %get-tuple-element.17.t1, f32[48,512]{1,0:T(8,128)} %get-tuple-element.18.cst, f32[24,512]{1,0:T(8,128)} %get-tuple-element.19.share, f32[24,512]{1,0:T(8,128)} %bond.1, ...), custom_call_target="tpu_custom_call" | custom-call | tf_op jit(solution)/shard_map/second/pallas_call | solution.py:441
  95.2 20.2 %all-to-all-start.1 = ((f32[32,24,128]{2,1,0:T(8,128)}), f32[32,24,128]{2,1,0:T(8,128)S(1)}, u32[]{:S(2)}, u32[]{:S(2)}) async-start(f32[32,24,128]{2,1,0:T(8,128)} %get-tuple-element.25), calls=%async_computation.1 | async-start | bytes 786432 | tf_op jit(solution)/shard_map/all_to_all | solution.py:518
  115.4 0.0 collective-permute-done.4.wl
  115.4 0.0 collective-permute-done.5.wh
  115.4 4.6 %collective-permute-start.7 = (f32[4,8,128]{2,1,0:T(8,128)S(1)}, f32[4,8,128]{2,1,0:T(8,128)S(1)}, u32[]{:S(2)}, u32[]{:S(2)}) collective-permute-start(f32[4,8,128]{2,1,0:T(8,128)S(1)} %pad_maximum_fusion.3), channel_id=1, source_target_pairs={{1,0},{2,1},{3,2},{4,3},{5,4},{6,5},{7,6},{8,7},{9,8},{10,9},{11,1... | collective-permute-start | bytes 49160 | tf_op jit(solution)/shard_map/ppermute | solution.py:464
  120.0 1.9 %collective-permute-start.6 = (f32[4,8,128]{2,1,0:T(8,128)S(1)}, f32[4,8,128]{2,1,0:T(8,128)S(1)}, u32[]{:S(2)}, u32[]{:S(2)}) collective-permute-start(f32[4,8,128]{2,1,0:T(8,128)S(1)} %pad_maximum_fusion.2), channel_id=1, source_target_pairs={{0,1},{1,2},{2,3},{3,4},{4,5},{5,6},{6,7},{7,8},{8,9},{9,10},{10,1... | collective-permute-start | bytes 49160 | tf_op jit(solution)/shard_map/ppermute | solution.py:463
  122.0 0.0 collective-permute-done.7.gh
  122.0 0.0 copy-start.15
  122.0 6.7 %collective-permute-done.6.gl = f32[4,8,128]{2,1,0:T(8,128)S(1)} collective-permute-done((f32[4,8,128]{2,1,0:T(8,128)S(1)}, f32[4,8,128]{2,1,0:T(8,128)S(1)}, u32[]{:S(2)}, u32[]{:S(2)}) %collective-permute-start.6) | collective-permute-done | bytes 16416 | tf_op jit(solution)/shard_map/ppermute | solution.py:463
  128.7 0.0 copy-done.15
  128.7 0.6 copy-done.16
  129.3 7.9 %late.1 = (f32[3,2,4,128]{3,2,1,0:T(4,128)}, f32[3,2,4,128]{3,2,1,0:T(4,128)}) custom-call(f32[1,4,8,128]{3,2,1,0:T(8,128)} %get-tuple-element.16.t0, f32[1,4,8,128]{3,2,1,0:T(8,128)} %get-tuple-element.17.t1, f32[1,4,8,128]{3,2,1,0:T(8,128)} %copy-done.12, f32[1,4,8,128]{3,2,1,0:T(8,128)} %copy-done.11, f32[4,8,128]{2,1,0:T(8,128)} %copy-done.16, ...), custom_call_target="tpu_custom_call" | custom-call | tf_op jit(solution)/shard_map/late/pallas_call | solution.py:441
  137.2 0.0 all-to-all-done.1
  137.2 0.6 add.11
  137.8 0.6 broadcast_in_dim.21
  (31 shorter events, 0.2 us)
Async XLA Ops:
  2.8 33.4 %copy-start.1 = (f32[1,4,8,128]{3,2,1,0:T(8,128)}, f32[1,4,8,128]{3,2,1,0:T(8,128)S(1)}, u32[]{:S(2)}) copy-start(f32[1,4,8,128]{3,2,1,0:T(8,128)S(1)} %get-tuple-element.30.t1) | copy-start | bytes 49156
  2.8 33.4 %copy-start.2 = (f32[1,4,8,128]{3,2,1,0:T(8,128)}, f32[1,4,8,128]{3,2,1,0:T(8,128)S(1)}, u32[]{:S(2)}) copy-start(f32[1,4,8,128]{3,2,1,0:T(8,128)S(1)} %get-tuple-element.31.t0) | copy-start | bytes 49156
  2.8 22.5 %collective-permute-start = (f32[1,4,8,128]{3,2,1,0:T(8,128)S(1)}, f32[1,4,8,128]{3,2,1,0:T(8,128)S(1)}, u32[]{:S(2)}, u32[]{:S(2)}) collective-permute-start(f32[1,4,8,128]{3,2,1,0:T(8,128)S(1)} %get-tuple-element.30.t1), channel_id=1, source_target_pairs={{0,32},{32,64},{64,96},{96,128},{128,160},{160,192},{192,224},{224... | collective-permute-start | bytes 49160 | tf_op jit(solution)/shard_map/ppermute | solution.py:457
  4.8 20.6 %collective-permute-start.1 = (f32[1,4,8,128]{3,2,1,0:T(8,128)S(1)}, f32[1,4,8,128]{3,2,1,0:T(8,128)S(1)}, u32[]{:S(2)}, u32[]{:S(2)}) collective-permute-start(f32[1,4,8,128]{3,2,1,0:T(8,128)S(1)} %get-tuple-element.31.t0), channel_id=1, source_target_pairs={{32,0},{64,32},{96,64},{128,96},{160,128},{192,160},{224,192},{256... | collective-permute-start | bytes 49160 | tf_op jit(solution)/shard_map/ppermute | solution.py:458
  10.8 38.1 %all-to-all-start = ((f32[32,24,128]{2,1,0:T(8,128)}), f32[32,24,128]{2,1,0:T(8,128)S(1)}, u32[]{:S(2)}, u32[]{:S(2)}) async-start(f32[32,24,128]{2,1,0:T(8,128)} %broadcast_in_dim.18), calls=%async_computation | async-start | bytes 786432 | tf_op jit(solution)/shard_map/all_to_all | solution.py:480
  25.3 10.9 %copy-start.9 = (f32[1,4,8,128]{3,2,1,0:T(8,128)}, f32[1,4,8,128]{3,2,1,0:T(8,128)S(1)}, u32[]{:S(2)}) copy-start(f32[1,4,8,128]{3,2,1,0:T(8,128)S(1)} %collective-permute-done.wl) | copy-start | bytes 49156
  25.4 10.9 %copy-start.10 = (f32[1,4,8,128]{3,2,1,0:T(8,128)}, f32[1,4,8,128]{3,2,1,0:T(8,128)S(1)}, u32[]{:S(2)}) copy-start(f32[1,4,8,128]{3,2,1,0:T(8,128)S(1)} %collective-permute-done.1.wh) | copy-start | bytes 49156
  25.4 10.8 %collective-permute-start.2 = (f32[4,8,128]{2,1,0:T(8,128)S(1)}, f32[4,8,128]{2,1,0:T(8,128)S(1)}, u32[]{:S(2)}, u32[]{:S(2)}) collective-permute-start(f32[4,8,128]{2,1,0:T(8,128)S(1)} %pad_maximum_fusion), channel_id=1, source_target_pairs={{0,1},{1,2},{2,3},{3,4},{4,5},{5,6},{6,7},{7,8},{8,9},{9,10},{10,1... | collective-permute-start | bytes 49160 | tf_op jit(solution)/shard_map/ppermute | solution.py:463
  28.8 7.4 %collective-permute-start.3 = (f32[4,8,128]{2,1,0:T(8,128)S(1)}, f32[4,8,128]{2,1,0:T(8,128)S(1)}, u32[]{:S(2)}, u32[]{:S(2)}) collective-permute-start(f32[4,8,128]{2,1,0:T(8,128)S(1)} %pad_maximum_fusion.1), channel_id=1, source_target_pairs={{1,0},{2,1},{3,2},{4,3},{5,4},{6,5},{7,6},{8,7},{9,8},{10,9},{11,1... | collective-permute-start | bytes 49160 | tf_op jit(solution)/shard_map/ppermute | solution.py:464
  36.2 0.6 copy-start.13
  36.2 0.6 copy-start.14
  48.9 0.8 copy-start
  58.1 21.8 %copy-start.3 = (f32[1,4,8,128]{3,2,1,0:T(8,128)S(1)}, f32[1,4,8,128]{3,2,1,0:T(8,128)}, u32[]{:S(2)}) copy-start(f32[1,4,8,128]{3,2,1,0:T(8,128)} %get-tuple-element.17.t1) | copy-start | bytes 49156
  58.1 21.8 %collective-permute-start.10 = (f32[24,512]{1,0:T(8,128)}, f32[24,512]{1,0:T(8,128)S(1)}, u32[]{:S(2)}, u32[]{:S(2)}) collective-permute-start(f32[24,512]{1,0:T(8,128)} %get-tuple-element.19.share), channel_id=1, source_target_pairs={{1,0},{2,1},{3,2},{4,3},{5,4},{6,5},{7,6},{8,7},{9,8},{10,9},{11,1... | collective-permute-start | bytes 147464 | tf_op jit(solution)/shard_map/ppermute | solution.py:506
  63.0 18.9 %collective-permute-start.11 = (f32[24,512]{1,0:T(8,128)}, f32[24,512]{1,0:T(8,128)S(1)}, u32[]{:S(2)}, u32[]{:S(2)}) collective-permute-start(f32[24,512]{1,0:T(8,128)} %get-tuple-element.19.share), channel_id=1, source_target_pairs={{2,0},{3,1},{4,2},{5,3},{6,4},{7,5},{8,6},{9,7},{10,8},{11,9},{12,... | collective-permute-start | bytes 147464 | tf_op jit(solution)/shard_map/ppermute | solution.py:506
  64.9 16.9 %collective-permute-start.8 = (f32[24,512]{1,0:T(8,128)}, f32[24,512]{1,0:T(8,128)S(1)}, u32[]{:S(2)}, u32[]{:S(2)}) collective-permute-start(f32[24,512]{1,0:T(8,128)} %get-tuple-element.19.share), channel_id=1, source_target_pairs={{0,2},{1,3},{2,4},{3,5},{4,6},{5,7},{6,8},{7,9},{8,10},{9,11},{10,... | collective-permute-start | bytes 147464 | tf_op jit(solution)/shard_map/ppermute | solution.py:506
  69.7 12.1 %collective-permute-start.9 = (f32[24,512]{1,0:T(8,128)}, f32[24,512]{1,0:T(8,128)S(1)}, u32[]{:S(2)}, u32[]{:S(2)}) collective-permute-start(f32[24,512]{1,0:T(8,128)} %get-tuple-element.19.share), channel_id=1, source_target_pairs={{0,1},{1,2},{2,3},{3,4},{4,5},{5,6},{6,7},{7,8},{8,9},{9,10},{10,1... | collective-permute-start | bytes 147464 | tf_op jit(solution)/shard_map/ppermute | solution.py:506
  71.7 43.7 %collective-permute-start.5 = (f32[1,4,8,128]{3,2,1,0:T(8,128)}, f32[1,4,8,128]{3,2,1,0:T(8,128)S(1)}, u32[]{:S(2)}, u32[]{:S(2)}) collective-permute-start(f32[1,4,8,128]{3,2,1,0:T(8,128)} %get-tuple-element.16.t0), channel_id=1, source_target_pairs={{32,0},{64,32},{96,64},{128,96},{160,128},{192,160},{224,192},{256... | collective-permute-start | bytes 49160 | tf_op jit(solution)/shard_map/ppermute | solution.py:458
  75.3 40.0 %copy-start.4 = (f32[1,4,8,128]{3,2,1,0:T(8,128)S(1)}, f32[1,4,8,128]{3,2,1,0:T(8,128)}, u32[]{:S(2)}) copy-start(f32[1,4,8,128]{3,2,1,0:T(8,128)} %get-tuple-element.17.t1) | copy-start | bytes 49156
  79.9 2.0 %copy-start.5 = (f32[24,512]{1,0:T(8,128)}, f32[24,512]{1,0:T(8,128)S(1)}, u32[]{:S(2)}) copy-start(f32[24,512]{1,0:T(8,128)S(1)} %collective-permute-done.10.r2) | copy-start | bytes 147460
  79.9 35.5 %collective-permute-start.4 = (f32[1,4,8,128]{3,2,1,0:T(8,128)S(1)}, f32[1,4,8,128]{3,2,1,0:T(8,128)S(1)}, u32[]{:S(2)}, u32[]{:S(2)}) collective-permute-start(f32[1,4,8,128]{3,2,1,0:T(8,128)S(1)} %copy-done.3), channel_id=1, source_target_pairs={{0,32},{32,64},{64,96},{96,128},{128,160},{160,192},{192,224},{224... | collective-permute-start | bytes 49160 | tf_op jit(solution)/shard_map/ppermute | solution.py:457
  81.8 0.6 copy-start.6
  81.9 0.6 copy-start.7
  82.5 0.6 copy-start.8
  95.2 42.0 %all-to-all-start.1 = ((f32[32,24,128]{2,1,0:T(8,128)}), f32[32,24,128]{2,1,0:T(8,128)S(1)}, u32[]{:S(2)}, u32[]{:S(2)}) async-start(f32[32,24,128]{2,1,0:T(8,128)} %get-tuple-element.25), calls=%async_computation.1 | async-start | bytes 786432 | tf_op jit(solution)/shard_map/all_to_all | solution.py:518
  115.4 13.3 %copy-start.12 = (f32[1,4,8,128]{3,2,1,0:T(8,128)}, f32[1,4,8,128]{3,2,1,0:T(8,128)S(1)}, u32[]{:S(2)}) copy-start(f32[1,4,8,128]{3,2,1,0:T(8,128)S(1)} %collective-permute-done.4.wl) | copy-start | bytes 49156
  115.4 13.3 %copy-start.11 = (f32[1,4,8,128]{3,2,1,0:T(8,128)}, f32[1,4,8,128]{3,2,1,0:T(8,128)S(1)}, u32[]{:S(2)}) copy-start(f32[1,4,8,128]{3,2,1,0:T(8,128)S(1)} %collective-permute-done.5.wh) | copy-start | bytes 49156
  115.4 6.5 %collective-permute-start.7 = (f32[4,8,128]{2,1,0:T(8,128)S(1)}, f32[4,8,128]{2,1,0:T(8,128)S(1)}, u32[]{:S(2)}, u32[]{:S(2)}) collective-permute-start(f32[4,8,128]{2,1,0:T(8,128)S(1)} %pad_maximum_fusion.3), channel_id=1, source_target_pairs={{1,0},{2,1},{3,2},{4,3},{5,4},{6,5},{7,6},{8,7},{9,8},{10,9},{11,1... | collective-permute-start | bytes 49160 | tf_op jit(solution)/shard_map/ppermute | solution.py:464
  120.0 8.6 %collective-permute-start.6 = (f32[4,8,128]{2,1,0:T(8,128)S(1)}, f32[4,8,128]{2,1,0:T(8,128)S(1)}, u32[]{:S(2)}, u32[]{:S(2)}) collective-permute-start(f32[4,8,128]{2,1,0:T(8,128)S(1)} %pad_maximum_fusion.2), channel_id=1, source_target_pairs={{0,1},{1,2},{2,3},{3,4},{4,5},{5,6},{6,7},{7,8},{8,9},{9,10},{10,1... | collective-permute-start | bytes 49160 | tf_op jit(solution)/shard_map/ppermute | solution.py:463
  122.0 6.7 %copy-start.15 = (f32[4,8,128]{2,1,0:T(8,128)}, f32[4,8,128]{2,1,0:T(8,128)S(1)}, u32[]{:S(2)}) copy-start(f32[4,8,128]{2,1,0:T(8,128)S(1)} %collective-permute-done.7.gh) | copy-start | bytes 49156
  128.7 0.6 copy-start.16

commit v3 on v2

--- a/solution.py
+++ b/solution.py
@@ -22,6 +22,7 @@
 NTP = 1024
 COLS = NBP + 2 * NTP
 SLABS = 32
+WIDTH = 2
 ROWS = 16
 
 F32 = jnp.float32
@@ -208,31 +209,116 @@
     )
 
 
-def membrane(own, count, cs, lcell, rnear, rdrag, qown, fpart, fcell):
-    ra, rc, _ = right_features(own)
-    rnear[...] = ra
-    rdrag[...] = rc
-    qown[...] = sum_features(own)
+def sort_half(st, hot):
+    n = st.shape[1]
+    z = st[2:3, :]
+    column = jnp.broadcast_to(z, (8, n)).T[:, 0:1]
+    ranks = []
+    for k in range(n // LANES):
+        cols = slice(k * LANES, (k + 1) * LANES)
+        zj = z[:, cols]
+        count = jnp.zeros((1, LANES), F32)
+        for b in range(n // LANES):
+            zi = column[b * LANES : (b + 1) * LANES]
+            if b < k:
+                less = zi <= zj
+            elif b > k:
+                less = zi < zj
+            else:
+                first = lax.broadcasted_iota(jnp.int32, (LANES, LANES), 0)
+                second = lax.broadcasted_iota(jnp.int32, (LANES, LANES), 1)
+                less = (zi < zj) | ((zi == zj) & (first < second))
+            count = count + jnp.sum(jnp.where(less, 1.0, 0.0), 0, keepdims=True)
+        ranks.append(count)
+    rank = jnp.concatenate(ranks, 1).astype(jnp.int32)
+    place = lax.broadcasted_iota(jnp.int32, (n, n), 0)
+    hot[...] = jnp.where(place == rank, 1.0, 0.0).astype(BF16)
+    parts = nt(jnp.concatenate(split3(st), 0).astype(BF16), hot[...])
+    return parts[0:8] + parts[8:16] + parts[16:24]
+
+
+def unsort_half(force, hot):
+    parts = nn(jnp.concatenate(split3(force), 0).astype(BF16), hot[...])
+    return parts[0:8] + parts[8:16] + parts[16:24]
+
+
+def membrane(own, count, cs, work, hot, lcell, qcell, right, qown, fpart, fcell):
+    order = [[w * TF + f for w in range(TW) for f in (2 * g, 2 * g + 1)] for g in range(2)]
+    halves_of = [
+        sort_half(jnp.concatenate([own[:, t * LANES : (t + 1) * LANES] for t in o], 1), hot.at[g])
+        for g, o in enumerate(order)
+    ]
+    st = jnp.concatenate(halves_of, 1)
+    ra, rc, _ = right_features(st)
+    q = sum_features(st)
+    lane = lax.broadcasted_iota(jnp.int32, (8, LANES), 1)
+    low = jnp.full((8, LANES), 3.0e4, F32)
+    high = -low
+    for k in range(8):
+        cols = slice(k * LANES, (k + 1) * LANES)
+        right[k] = jnp.concatenate([ra[:, cols], rc[:, cols]], 1)
+        qown[k] = jnp.concatenate([q[:, cols], q[:, cols]], 1)
+        block = st[:, cols]
+        low = jnp.where(lane == k, jnp.min(block, 1, keepdims=True), low)
+        high = jnp.where(lane == k, jnp.max(block, 1, keepdims=True), high)
+    row = row_ids(LANES)
+    bits = jnp.zeros((8, LANES), F32)
+    for k in range(8):
+        bits = jnp.where(lane == k, float(1 << k), bits)
+    real = lax.broadcasted_iota(jnp.int32, (8, NVP), 1) < NV
+    right[8] = jnp.zeros((64, 2 * LANES), BF16)
+    qown[8] = jnp.zeros((32, 2 * LANES), BF16)
+    n = jnp.int32(0)
+    for m in range(MAXCOV):
+        cell = cs[m]
+        cell_low = jnp.min(jnp.where(real, cell, 3.0e4), 1, keepdims=True)
+        cell_high = jnp.max(jnp.where(real, cell, -3.0e4), 1, keepdims=True)
+        apart = (low - 1.01 > cell_high) | (high + 1.01 < cell_low)
+        apart = jnp.max(jnp.where((row < 3) & apart, 1.0, 0.0), 0, keepdims=True)
+        mask = jnp.sum(jnp.where(apart > 0.5, 0.0, bits[0:1])).astype(jnp.int32)
+        mask = jnp.where(m < count, mask, 0)
+        for k in range(8):
+            work[n] = m * 16 + k
+            n = n + ((mask >> k) & 1)
+    for k in range(WIDTH):
+        work[n + k] = 8
     fpart[...] = jnp.zeros(fpart.shape, F32)
     fcell[...] = jnp.zeros(fcell.shape, F32)
 
     def one_cell(m, carry):
-        st = cs[m]
-        lcell[...] = left_features(st).T.astype(BF16)
-        q = sum_features(st)
-        total = jnp.zeros((32, NVP), F32)
-        for k in range(4):
-            cols = slice(k * 256, (k + 1) * 256)
-            weight = jnp.maximum(nn(lcell[...], rnear[:, cols]), 0.0)
-            s = weight * (4.0 - weight * nn(lcell[...], rdrag[:, cols]))
-            hi, lo = halves(s)
-            fpart[:, cols] += nn(q, hi) + nn(q, lo)
-            qo = qown[:, cols]
-            total = total + nt(qo, hi) + nt(qo, lo)
-        fcell[m] = total
+        lcell[m] = left_features(cs[m]).T.astype(BF16)
+        qcell[m] = sum_features(cs[m])
         return carry
 
     lax.fori_loop(0, count, one_cell, 0)
+
+    def some_blocks(i, carry):
+        found = []
+        for u in range(WIDTH):
+            item = work[i * WIDTH + u]
+            m, k = item >> 4, item & 15
+            out = nn(lcell[m], right[k])
+            weight = jnp.maximum(out[:, :LANES], 0.0)
+            s = weight * (4.0 - weight * out[:, LANES:])
+            both = jnp.concatenate(halves(s), 1)
+            found.append((m, k, nn(qcell[m], both), nt(qown[k], both)))
+        for m, k, on_parts, on_cell in found:
+            fpart[k] += on_parts[:, :LANES] + on_parts[:, LANES:]
+            fcell[m] += on_cell
+        return carry
+
+    lax.fori_loop(0, (n + WIDTH - 1) // WIDTH, some_blocks, 0)
+    force = []
+    for k in range(8):
+        mom = moment(fpart[k])
+        block = st[:, k * LANES : (k + 1) * LANES]
+        force.append(jnp.where(row < 3, block * mom[3:4] - mom, 0.0))
+    tiles = [None] * 8
+    for g, o in enumerate(order):
+        whole = unsort_half(jnp.concatenate(force[4 * g : 4 * g + 4], 1), hot.at[g])
+        for place, t in enumerate(o):
+            tiles[t] = whole[:, place * LANES : (place + 1) * LANES]
+    return jnp.concatenate(tiles, 1)
 
 
 def force_of(own, fpart):
@@ -256,7 +342,7 @@
     return jnp.concatenate(out, 1)
 
 
-def near_frames(t0, t1, wl, wh, gl, gh):
+def near_frames(t0, t1, in_a, in_b, gl, gh):
     i = lax.axis_index("wa")
     j = lax.axis_index("gx")
     row = row_ids(LANES)
@@ -265,7 +351,8 @@
     flo = jnp.where(j == 0, FAR, 0.0)
     fhi = jnp.where(j == SLABS - 1, FAR, 0.0)
     near = []
-    for w, ref in enumerate((wl, t0, t1, wh)):
+    even = i % 2 == 0
+    for w, ref in enumerate((None, t0, t1, None)):
         bad_w = wlo if w == 0 else whi if w == TW + 1 else 0.0
         for f in range(TF + 2):
             if f == 0:
@@ -273,18 +360,16 @@
             elif f == TF + 1:
                 tile, bad = gh[w], bad_w + fhi
             else:
-                tile, bad = ref[0, f - 1], bad_w
+                a, b = (in_b, in_a) if w == 0 else (in_a, in_b)
+                tile = jnp.where(even, a[0, f - 1], b[0, f - 1]) if ref is None else ref[0, f - 1]
+                bad = bad_w
             shift = jnp.where(row == 2, -ZMID, 0.0)
             shift = jnp.where(row == 0, float(w - 1) + bad, shift)
             near.append(tile + jnp.where(row == 1, float(f - 1), shift))
     return near
 
 
-def early_kernel(
-    t0, t1, wl, wh, gl, gh, bonds, corners, rest_len, rest_area,
-    out_f, m_ref, par_ref,
-    lfeat, fpart,
-):
+def incidence_kernel(bonds, corners, rest_len, rest_area, m_ref, par_ref):
     def fill(start, ids, hi, lo, size, padded):
         m_ref[:, start + padded - LANES : start + padded] = jnp.zeros((NVP, LANES), BF16)
         for a in range(0, size, 512):
@@ -304,7 +389,10 @@
     sq = rest_area[...] * rest_area[...]
     par_ref[2:3, 0:NT] = sq
     par_ref[3:4, 0:NT] = -0.125 / sq
-    own = solvent(near_frames(t0, t1, wl, wh, gl, gh), lfeat, fpart)
+
+
+def early_kernel(t0, t1, in_a, in_b, gl, gh, out_f, lfeat, fpart):
+    own = solvent(near_frames(t0, t1, in_a, in_b, gl, gh), lfeat, fpart)
     out_f[...] = force_of(own, fpart)
 
 
@@ -315,8 +403,8 @@
 
 def first_kernel(
     starts, t0, t1, kicks, cells, solv,
-    out_0, out_1, out_c, out_r,
-    idx, cnt, cs, lcell, rnear, rdrag, qown, fpart, fcell,
+    out_0, out_1, out_a, out_b, out_c, out_r,
+    idx, cnt, cs, work, hot, lcell, qcell, right, qown, fpart, fcell,
 ):
     j = lax.axis_index("gx")
     count = cover_slots(starts, j, idx, None, cnt)
@@ -332,14 +420,16 @@
         cs[m] = st
         lay_rows(out_c, m, st)
     own = own_frame(t0, t1)
-    membrane(own, count, cs, lcell, rnear, rdrag, qown, fpart, fcell)
-    force = solv[...] + force_of(own, fpart)
+    force = solv[...] + membrane(own, count, cs, work, hot, lcell, qcell, right, qown, fpart, fcell)
     for w, (ref, out) in enumerate(((t0, out_0), (t1, out_1))):
         for f in range(TF):
             t = w * TF + f
             st = moved(ref[0, f], force[:, t * LANES : (t + 1) * LANES])
             out[0, f, 0:6, :] = st[0:6]
             out[0, f, 6:8, :] = kicks[w, f]
+    even = lax.axis_index("wa") % 2 == 0
+    out_a[...] = jnp.where(even, out_1[...], out_0[...])
+    out_b[...] = jnp.where(even, out_0[...], out_1[...])
     out_r[...] = jnp.zeros((24, NVP), F32)
     for m in range(MAXCOV):
         mom = moment(fcell[m])
@@ -355,7 +445,7 @@
 def second_kernel(
     starts, t0, t1, cst, share, bond, r0, r1, r2, r3, m_ref, par_ref,
     out_f, out_s,
-    idx, cnt, smap, cs, ps, lcell, rnear, rdrag, qown, fpart, fcell,
+    idx, cnt, smap, cs, ps, work, hot, lcell, qcell, right, qown, fpart, fcell,
 ):
     j = lax.axis_index("gx")
     count = cover_slots(starts, j, idx, smap, cnt)
@@ -377,8 +467,7 @@
         for c in range(6):
             cs[m, c : c + 1, :] = ps[c * 8 + m : c * 8 + m + 1, :]
     own = own_frame(t0, t1)
-    membrane(own, count, cs, lcell, rnear, rdrag, qown, fpart, fcell)
-    out_f[...] = force_of(own, fpart)
+    out_f[...] = membrane(own, count, cs, work, hot, lcell, qcell, right, qown, fpart, fcell)
     ps[24:48, :] += DT * bond_force(ps[0:24, :], m_ref, par_ref)
     out_s[...] = jnp.zeros(out_s.shape, F32)
     row = row_ids(NVP)
@@ -398,8 +487,8 @@
                 out_s[cell, k * 6 : k * 6 + 6, :] = whole[0:6, k * LANES : (k + 1) * LANES]
 
 
-def late_kernel(t0, t1, wl, wh, gl, gh, memb, out_p, out_v, lfeat, fpart):
-    own = solvent(near_frames(t0, t1, wl, wh, gl, gh), lfeat, fpart)
+def late_kernel(t0, t1, in_a, in_b, gl, gh, memb, out_p, out_v, lfeat, fpart):
+    own = solvent(near_frames(t0, t1, in_a, in_b, gl, gh), lfeat, fpart)
     force = memb[...] + force_of(own, fpart)
     for w, ref in enumerate((t0, t1)):
         for f in range(TF):
@@ -423,11 +512,13 @@
         [pltpu.SMEM((8,), jnp.int32), pltpu.SMEM((1,), jnp.int32)]
         + extra
         + [
-            pltpu.VMEM((NVP, 64), BF16),
-            pltpu.VMEM((64, 8 * LANES), BF16),
-            pltpu.VMEM((64, 8 * LANES), BF16),
-            pltpu.VMEM((32, 8 * LANES), BF16),
-            pltpu.VMEM((32, 8 * LANES), F32),
+            pltpu.SMEM((48,), jnp.int32),
+            pltpu.VMEM((2, 4 * LANES, 4 * LANES), BF16),
+            pltpu.VMEM((MAXCOV, NVP, 64), BF16),
+            pltpu.VMEM((MAXCOV, 32, NVP), BF16),
+            pltpu.VMEM((9, 64, 2 * LANES), BF16),
+            pltpu.VMEM((9, 32, 2 * LANES), BF16),
+            pltpu.VMEM((9, 32, LANES), F32),
             pltpu.VMEM((8, 32, NVP), F32),
         ]
     )
@@ -453,16 +544,25 @@
     return [(k, k + shift) for k in range(count) if 0 <= k + shift < count]
 
 
-def halo(t0, t1):
-    wl = lax.ppermute(t1, "wa", moves("wa", 1))
-    wh = lax.ppermute(t0, "wa", moves("wa", -1))
+def swap(out_a, out_b):
+    count = lax.axis_size("wa")
+    odd_pairs = [(k, k - 1 if k % 2 == 0 else k + 1) for k in range(1, count - 1)]
+    in_a = lax.ppermute(out_a, "wa", [(k, k ^ 1) for k in range(count)])
+    return in_a, lax.ppermute(out_b, "wa", odd_pairs)
+
+
+def columns(t0, t1, in_a, in_b):
+    even = lax.axis_index("wa") % 2 == 0
 
     def column(f):
-        return jnp.concatenate([wl[:, f], t0[:, f], t1[:, f], wh[:, f]], 0)
+        a, b = in_a[:, f], in_b[:, f]
+        return jnp.concatenate(
+            [jnp.where(even, b, a), t0[:, f], t1[:, f], jnp.where(even, a, b)], 0
+        )
 
     gl = lax.ppermute(column(TF - 1), "gx", moves("gx", 1))
     gh = lax.ppermute(column(0), "gx", moves("gx", -1))
-    return wl, wh, gl, gh
+    return gl, gh
 
 
 def body(
@@ -477,34 +577,47 @@
         0,
     )
     cell = jnp.transpose(cell.reshape(6, 4, LANES), (1, 0, 2)).reshape(24, LANES)
-    cells = lax.all_to_all(
-        jnp.broadcast_to(cell[None], (SLABS, 24, LANES)), "gx", 0, 0, tiled=True
-    )
     tiles = jnp.transpose(
         jnp.concatenate([part_pos, part_vel, random_kicks[0:2]], 0), (1, 2, 0, 3)
     )
     t0, t1 = tiles[:1], tiles[1:]
+    even = lax.axis_index("wa") % 2 == 0
     kicks = jnp.transpose(random_kicks[2:4], (1, 2, 0, 3))
     part = ((8, TW * TF * LANES), F32)
     row = ((1, TF, 8, LANES), F32)
-    solv, incidence, par = call(
+    incidence, par = call(
+        incidence_kernel,
+        "incidence",
+        [((NVP, COLS), BF16), ((4, NBP), F32)],
+        [],
+        (bond_ends.T, triangles.T, rest_len[None], rest_area[None]),
+    )
+    incidence, cell, t0, t1 = lax.optimization_barrier((incidence, cell, t0, t1))
+    cells = lax.all_to_all(
+        jnp.broadcast_to(cell[None], (SLABS, 24, LANES)), "gx", 0, 0, tiled=True
+    )
+    sides = (jnp.where(even, t1, t0), jnp.where(even, t0, t1))
+    swapped = swap(*sides)
+    (solv,) = call(
         early_kernel,
         "early",
-        [part, ((NVP, COLS), BF16), ((4, NBP), F32)],
+        [part],
         solvent_scratch(),
-        (t0, t1, *halo(t0, t1), bond_ends.T, triangles.T, rest_len[None], rest_area[None]),
+        (t0, t1, *swapped, *columns(t0, t1, *swapped)),
     )
     cell_scratch = pltpu.VMEM((8, 8, NVP), F32)
-    n0, n1, cst, share = call(
+    n0, n1, n_a, n_b, cst, share = call(
         first_kernel,
         "first",
-        [row, row, ((48, NVP), F32), ((24, NVP), F32)],
+        [row, row, row, row, ((48, NVP), F32), ((24, NVP), F32)],
         slot_scratch([cell_scratch]),
         (cover_start, t0, t1, kicks, cells, solv),
         1,
     )
+    swapped = swap(n_a, n_b)
     got = [lax.ppermute(share, "gx", moves("gx", -s)) for s in (-2, -1, 1, 2)]
     (bond,) = call(bond_kernel, "bond", [((24, NVP), F32)], [], (cst, incidence, par))
+    bond, *swapped = lax.optimization_barrier((bond, *swapped))
     memb, sends = call(
         second_kernel,
         "second",
@@ -521,7 +634,7 @@
         "late",
         [((3, TW, TF, LANES), F32)] * 2,
         solvent_scratch(),
-        (n0, n1, *halo(n0, n1), memb),
+        (n0, n1, *swapped, *columns(n0, n1, *swapped), memb),
     )
     final = jnp.transpose(final.reshape(4, 6, LANES), (1, 0, 2)).reshape(6, NVP)
     new_vel = final[3:6, None, :NV]

time: 139 us -> 132 us (0.950); the launches traced: 138 us -> 129 us
  starting transfers between devices: 74.9 us -> 64.9 us
  waiting for transfers between devices: 6.73 us -> 14.2 us
  Pallas kernels: 45 us -> 39.8 us
    ppermute x8, waiting for transfers between devices: 6.71 us -> 14.2 us  [the longest x2 6.97 us: columns(): gl = lax.ppermute(column(TF - 1), 'gx', moves('gx', 1))]
    all_to_all x1, starting transfers between devices: 20.2 us -> 13.2 us  [body(): final = jnp.sum(lax.all_to_all(sends, 'gx', 0, 0, tiled=True), 0)]
    pallas_call x5 -> x6, Pallas kernels: 45 us -> 39.8 us  [call(): pl.pallas_call(kernel, out_shape=tuple((jax.ShapeDtypeStruct(s, t) for s,...]
  transfers between devices with their start and end apart: 14 -> 14, of which waited for: 1 -> 5; matrix products, arithmetic and copies ran while one was open for 3% -> 1% of each run, Pallas kernels for 26% -> 16%
where the time goes in v3:
time: 132 us; the launch traced here: 129 us
  starting transfers between devices  64.9 us (49%)
  Pallas kernels  39.8 us (30%)
  waiting for transfers between devices  14.2 us (11%)
  local copies, waits for them, and re-layouts  9.4 us (7%)
    pallas_call x6, Pallas kernels, call(): pl.pallas_call(kernel, out_shape=tuple((jax.ShapeDtypeStruct(s, t) for s,...  39.8 us
    all_to_all x1, starting transfers between devices, body(): lax.all_to_all(jnp.broadcast_to(cell[None], (SLABS, 24, LANES)), 'gx', 0,...  13.6 us
    all_to_all x1, starting transfers between devices, body(): final = jnp.sum(lax.all_to_all(sends, 'gx', 0, 0, tiled=True), 0)  13.2 us
    ppermute x4, starting transfers between devices, body(): got = [lax.ppermute(share, 'gx', moves('gx', -s)) for s in (-2, -1, 1, 2)]  12.6 us
    ppermute x2, starting transfers between devices, columns(): gh = lax.ppermute(column(0), 'gx', moves('gx', -1))  9.16 us
    ppermute x2, starting transfers between devices, swap(): return (in_a, lax.ppermute(out_b, 'wa', odd_pairs))  8.66 us
    ppermute x2, waiting for transfers between devices, columns(): gl = lax.ppermute(column(TF - 1), 'gx', moves('gx', 1))  6.97 us
    ppermute x2, waiting for transfers between devices, columns(): gh = lax.ppermute(column(0), 'gx', moves('gx', -1))  5.85 us
  transfers between devices with their start and end apart: 14, of which 5 were waited for; matrix products, arithmetic and copies ran while one was open for 1% of the time, Pallas kernels for 16%

profile of v3, /device:TPU:134, one launch (start us, length us, event | category | flops | bytes accessed | tf_op | source)
XLA Modules:
  0.0 129.4 jit_solution(13404950542695946220)
XLA Ops:
  0.6 0.7 fusion.3
  1.4 0.7 copy.21
  2.1 0.7 copy.22
  2.8 0.0 copy-start.1
  2.8 0.0 copy-start.2
  2.8 0.7 copy_bitcast_fusion.1
  3.6 1.3 %broadcast_in_dim.16.rest_len = f32[1,1488]{1,0:T(1,128)} reshape(f32[1488]{0:T(1024)} %param.18) | data formatting | bytes 11904 | tf_op jit(solution)/shard_map/broadcast_in_dim | solution.py:593
  4.9 4.0 %incidence.1 = (bf16[512,3584]{1,0:T(8,128)(2,1)}, f32[4,1536]{1,0:T(4,128)}) custom-call(s32[2,1488]{1,0:T(2,128)} %bitcast.54, s32[3,992]{1,0:T(4,128)} %bitcast.53, f32[1,1488]{1,0:T(1,128)} %broadcast_in_dim.16.rest_len, f32[1,992]{1,0:T(1,128)} %bitcast.55), custom_call_target="tpu_custom_call" | custom-call | tf_op jit(solution)/shard_map/incidence/pallas_call | solution.py:532
  8.9 1.9 %collective-permute-start = (f32[1,4,8,128]{3,2,1,0:T(8,128)S(1)}, f32[1,4,8,128]{3,2,1,0:T(8,128)S(1)}, u32[]{:S(2)}, u32[]{:S(2)}) collective-permute-start(f32[1,4,8,128]{3,2,1,0:T(8,128)S(1)} %get-tuple-element.51), channel_id=1, source_target_pairs={{0,32},{32,0},{64,96},{96,64},{128,160},{160,128},{192,224},{224,1... | collective-permute-start | bytes 49160 | tf_op jit(solution)/shard_map/ppermute | solution.py:550
  10.9 4.6 %collective-permute-start.1 = (f32[1,4,8,128]{3,2,1,0:T(8,128)S(1)}, f32[1,4,8,128]{3,2,1,0:T(8,128)S(1)}, u32[]{:S(2)}, u32[]{:S(2)}) collective-permute-start(f32[1,4,8,128]{3,2,1,0:T(8,128)S(1)} %get-tuple-element.50), channel_id=1, source_target_pairs={{32,64},{64,32},{96,128},{128,96},{160,192},{192,160},{224,256},{2... | collective-permute-start | bytes 49160 | tf_op jit(solution)/shard_map/ppermute | solution.py:551
  15.5 0.8 broadcast_in_dim.18
  16.3 13.6 %all-to-all-start = ((f32[32,24,128]{2,1,0:T(8,128)}), f32[32,24,128]{2,1,0:T(8,128)S(1)}, u32[]{:S(2)}, u32[]{:S(2)}) async-start(f32[32,24,128]{2,1,0:T(8,128)} %broadcast_in_dim.18), calls=%async_computation | async-start | bytes 786432 | tf_op jit(solution)/shard_map/all_to_all | solution.py:596
  29.9 0.0 collective-permute-done.in_a
  29.9 0.0 copy-start.11
  29.9 0.0 collective-permute-done.1.in_b
  29.9 0.0 copy-start.12
  30.0 4.6 %collective-permute-start.3 = (f32[4,8,128]{2,1,0:T(8,128)S(1)}, f32[4,8,128]{2,1,0:T(8,128)S(1)}, u32[]{:S(2)}, u32[]{:S(2)}) collective-permute-start(f32[4,8,128]{2,1,0:T(8,128)S(1)} %pad_maximum_fusion.1), channel_id=1, source_target_pairs={{1,0},{2,1},{3,2},{4,3},{5,4},{6,5},{7,6},{8,7},{9,8},{10,9},{11,1... | collective-permute-start | bytes 49160 | tf_op jit(solution)/shard_map/ppermute | solution.py:564
  34.6 1.9 %collective-permute-start.2 = (f32[4,8,128]{2,1,0:T(8,128)S(1)}, f32[4,8,128]{2,1,0:T(8,128)S(1)}, u32[]{:S(2)}, u32[]{:S(2)}) collective-permute-start(f32[4,8,128]{2,1,0:T(8,128)S(1)} %pad_maximum_fusion), channel_id=1, source_target_pairs={{0,1},{1,2},{2,3},{3,4},{4,5},{5,6},{6,7},{7,8},{8,9},{9,10},{10,1... | collective-permute-start | bytes 49160 | tf_op jit(solution)/shard_map/ppermute | solution.py:563
  36.5 0.6 copy.31
  37.1 3.1 %collective-permute-done.3.gh = f32[4,8,128]{2,1,0:T(8,128)S(1)} collective-permute-done((f32[4,8,128]{2,1,0:T(8,128)S(1)}, f32[4,8,128]{2,1,0:T(8,128)S(1)}, u32[]{:S(2)}, u32[]{:S(2)}) %collective-permute-start.3) | collective-permute-done | bytes 16416 | tf_op jit(solution)/shard_map/ppermute | solution.py:564
  40.3 3.0 %collective-permute-done.2.gl = f32[4,8,128]{2,1,0:T(8,128)S(1)} collective-permute-done((f32[4,8,128]{2,1,0:T(8,128)S(1)}, f32[4,8,128]{2,1,0:T(8,128)S(1)}, u32[]{:S(2)}, u32[]{:S(2)}) %collective-permute-start.2) | collective-permute-done | bytes 16416 | tf_op jit(solution)/shard_map/ppermute | solution.py:563
  43.2 0.0 copy-done.1
  43.2 0.0 copy-done.2
  43.2 0.0 copy-done.11
  43.2 0.0 copy-done.12
  43.2 0.0 copy-done.14
  43.3 0.0 copy-start.16
  43.3 0.6 copy-done.16
  43.9 7.8 %early.1.solv = f32[8,1024]{1,0:T(8,128)} custom-call(f32[1,4,8,128]{3,2,1,0:T(8,128)} %copy-done.2, f32[1,4,8,128]{3,2,1,0:T(8,128)} %copy-done.1, f32[1,4,8,128]{3,2,1,0:T(8,128)} %copy-done.11, f32[1,4,8,128]{3,2,1,0:T(8,128)} %copy-done.12, f32[4,8,128]{2,1,0:T(8,128)} %copy-done.16, f32[4,8,128]{2,1,0:T(8,128)} %copy-done.14), custom_call_target="tpu_custom_call" | custom-call | tf_op jit(solution)/shard_map/early/pallas_call | solution.py:532
  51.7 0.0 all-to-all-done.cells
  51.7 0.8 copy-done
  52.5 6.0 %first.1 = (f32[1,4,8,128]{3,2,1,0:T(8,128)}, f32[1,4,8,128]{3,2,1,0:T(8,128)}, f32[1,4,8,128]{3,2,1,0:T(8,128)}, f32[1,4,8,128]{3,2,1,0:T(8,128)}, f32[48,512]{1,0:T(8,128)}, /*index=5*/f32[24,512]{1,0:T(8,128)}) custom-call(s32[32]{0:T(128)} %starts.3, f32[1,4,8,128]{3,2,1,0:T(8,128)} %copy-done.2, f32[1,4,8,128]{3,2,1,0:T(8,128)} %copy-done.1, ...), custom_call_target="tpu_custom_call" | custom-call | tf_op jit(solution)/shard_map/first/pallas_call | solution.py:532
  58.5 2.5 %collective-permute-start.10 = (f32[24,512]{1,0:T(8,128)}, f32[24,512]{1,0:T(8,128)S(1)}, u32[]{:S(2)}, u32[]{:S(2)}) collective-permute-start(f32[24,512]{1,0:T(8,128)} %get-tuple-element.36.share), channel_id=1, source_target_pairs={{1,0},{2,1},{3,2},{4,3},{5,4},{6,5},{7,6},{8,7},{9,8},{10,9},{11,1... | collective-permute-start | bytes 147464 | tf_op jit(solution)/shard_map/ppermute | solution.py:618
  61.0 5.2 %collective-permute-start.11 = (f32[24,512]{1,0:T(8,128)}, f32[24,512]{1,0:T(8,128)S(1)}, u32[]{:S(2)}, u32[]{:S(2)}) collective-permute-start(f32[24,512]{1,0:T(8,128)} %get-tuple-element.36.share), channel_id=1, source_target_pairs={{2,0},{3,1},{4,2},{5,3},{6,4},{7,5},{8,6},{9,7},{10,8},{11,9},{12,... | collective-permute-start | bytes 147464 | tf_op jit(solution)/shard_map/ppermute | solution.py:618
  66.2 1.9 %collective-permute-start.8 = (f32[24,512]{1,0:T(8,128)}, f32[24,512]{1,0:T(8,128)S(1)}, u32[]{:S(2)}, u32[]{:S(2)}) collective-permute-start(f32[24,512]{1,0:T(8,128)} %get-tuple-element.36.share), channel_id=1, source_target_pairs={{0,2},{1,3},{2,4},{3,5},{4,6},{5,7},{6,8},{7,9},{8,10},{9,11},{10,... | collective-permute-start | bytes 147464 | tf_op jit(solution)/shard_map/ppermute | solution.py:618
  68.1 2.9 %collective-permute-start.9 = (f32[24,512]{1,0:T(8,128)}, f32[24,512]{1,0:T(8,128)S(1)}, u32[]{:S(2)}, u32[]{:S(2)}) collective-permute-start(f32[24,512]{1,0:T(8,128)} %get-tuple-element.36.share), channel_id=1, source_target_pairs={{0,1},{1,2},{2,3},{3,4},{4,5},{5,6},{6,7},{7,8},{8,9},{9,10},{10,1... | collective-permute-start | bytes 147464 | tf_op jit(solution)/shard_map/ppermute | solution.py:618
  71.1 1.9 %collective-permute-start.4 = (f32[1,4,8,128]{3,2,1,0:T(8,128)}, f32[1,4,8,128]{3,2,1,0:T(8,128)S(1)}, u32[]{:S(2)}, u32[]{:S(2)}) collective-permute-start(f32[1,4,8,128]{3,2,1,0:T(8,128)} %get-tuple-element.32), channel_id=1, source_target_pairs={{0,32},{32,0},{64,96},{96,64},{128,160},{160,128},{192,224},{224,1... | collective-permute-start | bytes 49160 | tf_op jit(solution)/shard_map/ppermute | solution.py:550
  73.0 1.4 %collective-permute-done.4.in_a = f32[1,4,8,128]{3,2,1,0:T(8,128)S(1)} collective-permute-done((f32[1,4,8,128]{3,2,1,0:T(8,128)}, f32[1,4,8,128]{3,2,1,0:T(8,128)S(1)}, u32[]{:S(2)}, u32[]{:S(2)}) %collective-permute-start.4) | collective-permute-done | bytes 16416 | tf_op jit(solution)/shard_map/ppermute | solution.py:550
  74.4 4.0 %collective-permute-start.5 = (f32[1,4,8,128]{3,2,1,0:T(8,128)}, f32[1,4,8,128]{3,2,1,0:T(8,128)S(1)}, u32[]{:S(2)}, u32[]{:S(2)}) collective-permute-start(f32[1,4,8,128]{3,2,1,0:T(8,128)} %get-tuple-element.33), channel_id=1, source_target_pairs={{32,64},{64,32},{96,128},{128,96},{160,192},{192,160},{224,256},{2... | collective-permute-start | bytes 49160 | tf_op jit(solution)/shard_map/ppermute | solution.py:551
  78.4 4.5 %bond.1 = f32[24,512]{1,0:T(8,128)} custom-call(f32[48,512]{1,0:T(8,128)} %get-tuple-element.29.cst, bf16[512,3584]{1,0:T(8,128)(2,1)} %get-tuple-element.30.m_ref, f32[4,1536]{1,0:T(4,128)} %get-tuple-element.31.par_ref), custom_call_target="tpu_custom_call" | custom-call | tf_op jit(solution)/shard_map/bond/pallas_call | solution.py:532
  83.0 0.0 collective-permute-done.5.in_b
  83.0 0.0 collective-permute-done.10.r2
  83.0 0.0 copy-start.5
  83.0 0.0 collective-permute-done.11.r3
  83.0 0.0 collective-permute-done.8.r0
  83.0 0.0 collective-permute-done.9.r1
  83.0 0.0 copy-start.8
  83.0 0.5 copy-done.5
  83.6 0.0 copy-done.6
  83.6 0.0 copy-done.7
  83.6 0.0 copy-done.8
  83.7 9.4 %second.1 = (f32[8,1024]{1,0:T(8,128)}, f32[32,24,128]{2,1,0:T(8,128)}) custom-call(s32[32]{0:T(128)} %starts.3, f32[1,4,8,128]{3,2,1,0:T(8,128)} %get-tuple-element.27.t0, f32[1,4,8,128]{3,2,1,0:T(8,128)} %get-tuple-element.28.t1, f32[48,512]{1,0:T(8,128)} %get-tuple-element.29.cst, f32[24,512]{1,0:T(8,128)} %get-tuple-element.36.share, f32[24,512]{1,0:T(8,128)} %bond.1, ...), custom_call_target="tpu_custom_call" | custom-call | tf_op jit(solution)/shard_map/second/pallas_call | solution.py:532
  93.1 13.2 %all-to-all-start.1 = ((f32[32,24,128]{2,1,0:T(8,128)}), f32[32,24,128]{2,1,0:T(8,128)S(1)}, u32[]{:S(2)}, u32[]{:S(2)}) async-start(f32[32,24,128]{2,1,0:T(8,128)} %get-tuple-element.41), calls=%async_computation.1 | async-start | bytes 786432 | tf_op jit(solution)/shard_map/all_to_all | solution.py:631
  106.4 0.0 copy-done.9
  106.4 4.6 %collective-permute-start.7 = (f32[4,8,128]{2,1,0:T(8,128)S(1)}, f32[4,8,128]{2,1,0:T(8,128)S(1)}, u32[]{:S(2)}, u32[]{:S(2)}) collective-permute-start(f32[4,8,128]{2,1,0:T(8,128)S(1)} %pad_maximum_fusion.3), channel_id=1, source_target_pairs={{1,0},{2,1},{3,2},{4,3},{5,4},{6,5},{7,6},{8,7},{9,8},{10,9},{11,1... | collective-permute-start | bytes 49160 | tf_op jit(solution)/shard_map/ppermute | solution.py:564
  111.0 1.9 %collective-permute-start.6 = (f32[4,8,128]{2,1,0:T(8,128)S(1)}, f32[4,8,128]{2,1,0:T(8,128)S(1)}, u32[]{:S(2)}, u32[]{:S(2)}) collective-permute-start(f32[4,8,128]{2,1,0:T(8,128)S(1)} %pad_maximum_fusion.2), channel_id=1, source_target_pairs={{0,1},{1,2},{2,3},{3,4},{4,5},{5,6},{6,7},{7,8},{8,9},{9,10},{10,1... | collective-permute-start | bytes 49160 | tf_op jit(solution)/shard_map/ppermute | solution.py:563
  113.0 2.7 %collective-permute-done.7.gh = f32[4,8,128]{2,1,0:T(8,128)S(1)} collective-permute-done((f32[4,8,128]{2,1,0:T(8,128)S(1)}, f32[4,8,128]{2,1,0:T(8,128)S(1)}, u32[]{:S(2)}, u32[]{:S(2)}) %collective-permute-start.7) | collective-permute-done | bytes 16416 | tf_op jit(solution)/shard_map/ppermute | solution.py:564
  115.7 4.0 %collective-permute-done.6.gl = f32[4,8,128]{2,1,0:T(8,128)S(1)} collective-permute-done((f32[4,8,128]{2,1,0:T(8,128)S(1)}, f32[4,8,128]{2,1,0:T(8,128)S(1)}, u32[]{:S(2)}, u32[]{:S(2)}) %collective-permute-start.6) | collective-permute-done | bytes 16416 | tf_op jit(solution)/shard_map/ppermute | solution.py:563
  119.7 0.0 copy-done.13
  119.7 0.6 copy-done.15
  120.3 7.9 %late.1 = (f32[3,2,4,128]{3,2,1,0:T(4,128)}, f32[3,2,4,128]{3,2,1,0:T(4,128)}) custom-call(f32[1,4,8,128]{3,2,1,0:T(8,128)} %get-tuple-element.27.t0, f32[1,4,8,128]{3,2,1,0:T(8,128)} %get-tuple-element.28.t1, f32[1,4,8,128]{3,2,1,0:T(8,128)} %copy-done.9, f32[1,4,8,128]{3,2,1,0:T(8,128)} %copy-done.10, f32[4,8,128]{2,1,0:T(8,128)} %copy-done.15, ...), custom_call_target="tpu_custom_call" | custom-call | tf_op jit(solution)/shard_map/late/pallas_call | solution.py:532
  128.2 0.0 all-to-all-done.1
  128.2 0.6 add.18
  128.8 0.6 broadcast_in_dim.19
  (32 shorter events, 0.2 us)
Async XLA Ops:
  2.8 40.4 %copy-start.1 = (f32[1,4,8,128]{3,2,1,0:T(8,128)}, f32[1,4,8,128]{3,2,1,0:T(8,128)S(1)}, u32[]{:S(2)}) copy-start(f32[1,4,8,128]{3,2,1,0:T(8,128)S(1)} %get-tuple-element.25.t1) | copy-start | bytes 49156
  2.8 40.4 %copy-start.2 = (f32[1,4,8,128]{3,2,1,0:T(8,128)}, f32[1,4,8,128]{3,2,1,0:T(8,128)S(1)}, u32[]{:S(2)}) copy-start(f32[1,4,8,128]{3,2,1,0:T(8,128)S(1)} %get-tuple-element.24.t0) | copy-start | bytes 49156
  8.9 21.0 %collective-permute-start = (f32[1,4,8,128]{3,2,1,0:T(8,128)S(1)}, f32[1,4,8,128]{3,2,1,0:T(8,128)S(1)}, u32[]{:S(2)}, u32[]{:S(2)}) collective-permute-start(f32[1,4,8,128]{3,2,1,0:T(8,128)S(1)} %get-tuple-element.51), channel_id=1, source_target_pairs={{0,32},{32,0},{64,96},{96,64},{128,160},{160,128},{192,224},{224,1... | collective-permute-start | bytes 49160 | tf_op jit(solution)/shard_map/ppermute | solution.py:550
  10.9 19.1 %collective-permute-start.1 = (f32[1,4,8,128]{3,2,1,0:T(8,128)S(1)}, f32[1,4,8,128]{3,2,1,0:T(8,128)S(1)}, u32[]{:S(2)}, u32[]{:S(2)}) collective-permute-start(f32[1,4,8,128]{3,2,1,0:T(8,128)S(1)} %get-tuple-element.50), channel_id=1, source_target_pairs={{32,64},{64,32},{96,128},{128,96},{160,192},{192,160},{224,256},{2... | collective-permute-start | bytes 49160 | tf_op jit(solution)/shard_map/ppermute | solution.py:551
  16.3 35.4 %all-to-all-start = ((f32[32,24,128]{2,1,0:T(8,128)}), f32[32,24,128]{2,1,0:T(8,128)S(1)}, u32[]{:S(2)}, u32[]{:S(2)}) async-start(f32[32,24,128]{2,1,0:T(8,128)} %broadcast_in_dim.18), calls=%async_computation | async-start | bytes 786432 | tf_op jit(solution)/shard_map/all_to_all | solution.py:596
  29.9 13.3 %copy-start.11 = (f32[1,4,8,128]{3,2,1,0:T(8,128)}, f32[1,4,8,128]{3,2,1,0:T(8,128)S(1)}, u32[]{:S(2)}) copy-start(f32[1,4,8,128]{3,2,1,0:T(8,128)S(1)} %collective-permute-done.in_a) | copy-start | bytes 49156
  29.9 13.3 %copy-start.12 = (f32[1,4,8,128]{3,2,1,0:T(8,128)}, f32[1,4,8,128]{3,2,1,0:T(8,128)S(1)}, u32[]{:S(2)}) copy-start(f32[1,4,8,128]{3,2,1,0:T(8,128)S(1)} %collective-permute-done.1.in_b) | copy-start | bytes 49156
  30.0 10.3 %collective-permute-start.3 = (f32[4,8,128]{2,1,0:T(8,128)S(1)}, f32[4,8,128]{2,1,0:T(8,128)S(1)}, u32[]{:S(2)}, u32[]{:S(2)}) collective-permute-start(f32[4,8,128]{2,1,0:T(8,128)S(1)} %pad_maximum_fusion.1), channel_id=1, source_target_pairs={{1,0},{2,1},{3,2},{4,3},{5,4},{6,5},{7,6},{8,7},{9,8},{10,9},{11,1... | collective-permute-start | bytes 49160 | tf_op jit(solution)/shard_map/ppermute | solution.py:564
  34.6 8.6 %collective-permute-start.2 = (f32[4,8,128]{2,1,0:T(8,128)S(1)}, f32[4,8,128]{2,1,0:T(8,128)S(1)}, u32[]{:S(2)}, u32[]{:S(2)}) collective-permute-start(f32[4,8,128]{2,1,0:T(8,128)S(1)} %pad_maximum_fusion), channel_id=1, source_target_pairs={{0,1},{1,2},{2,3},{3,4},{4,5},{5,6},{6,7},{7,8},{8,9},{9,10},{10,1... | collective-permute-start | bytes 49160 | tf_op jit(solution)/shard_map/ppermute | solution.py:563
  40.3 3.0 %copy-start.14 = (f32[4,8,128]{2,1,0:T(8,128)}, f32[4,8,128]{2,1,0:T(8,128)S(1)}, u32[]{:S(2)}) copy-start(f32[4,8,128]{2,1,0:T(8,128)S(1)} %collective-permute-done.3.gh) | copy-start | bytes 49156
  43.3 0.6 copy-start.16
  51.7 0.8 copy-start
  58.5 24.5 %collective-permute-start.10 = (f32[24,512]{1,0:T(8,128)}, f32[24,512]{1,0:T(8,128)S(1)}, u32[]{:S(2)}, u32[]{:S(2)}) collective-permute-start(f32[24,512]{1,0:T(8,128)} %get-tuple-element.36.share), channel_id=1, source_target_pairs={{1,0},{2,1},{3,2},{4,3},{5,4},{6,5},{7,6},{8,7},{9,8},{10,9},{11,1... | collective-permute-start | bytes 147464 | tf_op jit(solution)/shard_map/ppermute | solution.py:618
  61.0 22.0 %collective-permute-start.11 = (f32[24,512]{1,0:T(8,128)}, f32[24,512]{1,0:T(8,128)S(1)}, u32[]{:S(2)}, u32[]{:S(2)}) collective-permute-start(f32[24,512]{1,0:T(8,128)} %get-tuple-element.36.share), channel_id=1, source_target_pairs={{2,0},{3,1},{4,2},{5,3},{6,4},{7,5},{8,6},{9,7},{10,8},{11,9},{12,... | collective-permute-start | bytes 147464 | tf_op jit(solution)/shard_map/ppermute | solution.py:618
  66.2 16.8 %collective-permute-start.8 = (f32[24,512]{1,0:T(8,128)}, f32[24,512]{1,0:T(8,128)S(1)}, u32[]{:S(2)}, u32[]{:S(2)}) collective-permute-start(f32[24,512]{1,0:T(8,128)} %get-tuple-element.36.share), channel_id=1, source_target_pairs={{0,2},{1,3},{2,4},{3,5},{4,6},{5,7},{6,8},{7,9},{8,10},{9,11},{10,... | collective-permute-start | bytes 147464 | tf_op jit(solution)/shard_map/ppermute | solution.py:618
  68.1 14.9 %collective-permute-start.9 = (f32[24,512]{1,0:T(8,128)}, f32[24,512]{1,0:T(8,128)S(1)}, u32[]{:S(2)}, u32[]{:S(2)}) collective-permute-start(f32[24,512]{1,0:T(8,128)} %get-tuple-element.36.share), channel_id=1, source_target_pairs={{0,1},{1,2},{2,3},{3,4},{4,5},{5,6},{6,7},{7,8},{8,9},{9,10},{10,1... | collective-permute-start | bytes 147464 | tf_op jit(solution)/shard_map/ppermute | solution.py:618
  71.1 3.3 %collective-permute-start.4 = (f32[1,4,8,128]{3,2,1,0:T(8,128)}, f32[1,4,8,128]{3,2,1,0:T(8,128)S(1)}, u32[]{:S(2)}, u32[]{:S(2)}) collective-permute-start(f32[1,4,8,128]{3,2,1,0:T(8,128)} %get-tuple-element.32), channel_id=1, source_target_pairs={{0,32},{32,0},{64,96},{96,64},{128,160},{160,128},{192,224},{224,1... | collective-permute-start | bytes 49160 | tf_op jit(solution)/shard_map/ppermute | solution.py:550
  74.4 32.0 %copy-start.9 = (f32[1,4,8,128]{3,2,1,0:T(8,128)}, f32[1,4,8,128]{3,2,1,0:T(8,128)S(1)}, u32[]{:S(2)}) copy-start(f32[1,4,8,128]{3,2,1,0:T(8,128)S(1)} %collective-permute-done.4.in_a) | copy-start | bytes 49156
  74.4 8.6 %collective-permute-start.5 = (f32[1,4,8,128]{3,2,1,0:T(8,128)}, f32[1,4,8,128]{3,2,1,0:T(8,128)S(1)}, u32[]{:S(2)}, u32[]{:S(2)}) collective-permute-start(f32[1,4,8,128]{3,2,1,0:T(8,128)} %get-tuple-element.33), channel_id=1, source_target_pairs={{32,64},{64,32},{96,128},{128,96},{160,192},{192,160},{224,256},{2... | collective-permute-start | bytes 49160 | tf_op jit(solution)/shard_map/ppermute | solution.py:551
  78.4 28.0 %copy-start.3 = (f32[1,4,8,128]{3,2,1,0:T(8,128)S(1)}, f32[1,4,8,128]{3,2,1,0:T(8,128)}, u32[]{:S(2)}) copy-start(f32[1,4,8,128]{3,2,1,0:T(8,128)} %get-tuple-element.27.t0) | copy-start | bytes 49156
  78.4 28.0 %copy-start.4 = (f32[1,4,8,128]{3,2,1,0:T(8,128)S(1)}, f32[1,4,8,128]{3,2,1,0:T(8,128)}, u32[]{:S(2)}) copy-start(f32[1,4,8,128]{3,2,1,0:T(8,128)} %get-tuple-element.28.t1) | copy-start | bytes 49156
  83.0 36.7 %copy-start.10 = (f32[1,4,8,128]{3,2,1,0:T(8,128)}, f32[1,4,8,128]{3,2,1,0:T(8,128)S(1)}, u32[]{:S(2)}) copy-start(f32[1,4,8,128]{3,2,1,0:T(8,128)S(1)} %collective-permute-done.5.in_b) | copy-start | bytes 49156
  83.0 0.6 copy-start.5
  83.0 0.6 copy-start.6
  83.0 0.6 copy-start.7
  83.0 0.6 copy-start.8
  93.1 35.1 %all-to-all-start.1 = ((f32[32,24,128]{2,1,0:T(8,128)}), f32[32,24,128]{2,1,0:T(8,128)S(1)}, u32[]{:S(2)}, u32[]{:S(2)}) async-start(f32[32,24,128]{2,1,0:T(8,128)} %get-tuple-element.41), calls=%async_computation.1 | async-start | bytes 786432 | tf_op jit(solution)/shard_map/all_to_all | solution.py:631
  106.4 9.2 %collective-permute-start.7 = (f32[4,8,128]{2,1,0:T(8,128)S(1)}, f32[4,8,128]{2,1,0:T(8,128)S(1)}, u32[]{:S(2)}, u32[]{:S(2)}) collective-permute-start(f32[4,8,128]{2,1,0:T(8,128)S(1)} %pad_maximum_fusion.3), channel_id=1, source_target_pairs={{1,0},{2,1},{3,2},{4,3},{5,4},{6,5},{7,6},{8,7},{9,8},{10,9},{11,1... | collective-permute-start | bytes 49160 | tf_op jit(solution)/shard_map/ppermute | solution.py:564
  111.0 8.6 %collective-permute-start.6 = (f32[4,8,128]{2,1,0:T(8,128)S(1)}, f32[4,8,128]{2,1,0:T(8,128)S(1)}, u32[]{:S(2)}, u32[]{:S(2)}) collective-permute-start(f32[4,8,128]{2,1,0:T(8,128)S(1)} %pad_maximum_fusion.2), channel_id=1, source_target_pairs={{0,1},{1,2},{2,3},{3,4},{4,5},{5,6},{6,7},{7,8},{8,9},{9,10},{10,1... | collective-permute-start | bytes 49160 | tf_op jit(solution)/shard_map/ppermute | solution.py:563
  115.7 4.0 %copy-start.13 = (f32[4,8,128]{2,1,0:T(8,128)}, f32[4,8,128]{2,1,0:T(8,128)S(1)}, u32[]{:S(2)}) copy-start(f32[4,8,128]{2,1,0:T(8,128)S(1)} %collective-permute-done.7.gh) | copy-start | bytes 49156
  119.7 0.6 copy-start.15

commit v4 on v3

--- a/solution.py
+++ b/solution.py
@@ -4,6 +4,7 @@
 from jax.experimental import pallas as pl
 from jax.experimental.pallas import tpu as pltpu
 from jax.sharding import PartitionSpec as P
+
 
 SPAN = 3
 MAXCOV = 5
@@ -17,9 +18,9 @@
 NV = 498
 NVP = 512
 NB = 1488
-NBP = 1536
+NBP = 512
 NT = 992
-NTP = 1024
+NTP = 384
 COLS = NBP + 2 * NTP
 SLABS = 32
 WIDTH = 2
@@ -190,16 +191,14 @@
             t = w * TF + f
             cols = slice(t * LANES, (t + 1) * LANES)
             rt = jnp.concatenate([ra[:, cols], rc[:, cols], rb[:, cols]], 1)
-            acc = jnp.zeros((32, LANES), F32)
-            for dw in range(3):
-                first = ((w + dw) * (TF + 2) + f) * LANES
-                out = nn(lfeat[first : first + 3 * LANES, :], rt)
-                weight = jnp.maximum(out[:, :LANES], 0.0)
-                s = weight * (out[:, 2 * LANES :] - weight * out[:, LANES : 2 * LANES])
-                hi, lo = halves(s)
-                q = qnear[:, first : first + 3 * LANES]
-                acc = acc + nn(q, hi) + nn(q, lo)
-            fpart[:, cols] = acc
+            firsts = [((w + dw) * (TF + 2) + f) * LANES for dw in range(3)]
+            near_rows = jnp.concatenate([lfeat[a : a + 3 * LANES, :] for a in firsts], 0)
+            out = nn(near_rows, rt)
+            weight = jnp.maximum(out[:, :LANES], 0.0)
+            s = weight * (out[:, 2 * LANES :] - weight * out[:, LANES : 2 * LANES])
+            q = jnp.concatenate([qnear[:, a : a + 3 * LANES] for a in firsts], 1)
+            acc = nn(q, jnp.concatenate(halves(s), 1))
+            fpart[:, cols] = acc[:, :LANES] + acc[:, LANES:]
     return own
 
 
@@ -369,26 +368,26 @@
     return near
 
 
-def incidence_kernel(bonds, corners, rest_len, rest_area, m_ref, par_ref):
-    def fill(start, ids, hi, lo, size, padded):
-        m_ref[:, start + padded - LANES : start + padded] = jnp.zeros((NVP, LANES), BF16)
-        for a in range(0, size, 512):
-            b = min(a + 512, size)
-            vid = lax.broadcasted_iota(jnp.int32, (NVP, b - a), 0)
-            plus = (vid == ids[hi : hi + 1, a:b]).astype(F32)
-            minus = (vid == ids[lo : lo + 1, a:b]).astype(F32)
-            m_ref[:, start + a : start + b] = (plus - minus).astype(BF16)
-
-    fill(0, bonds, 0, 1, NB, NBP)
-    fill(NBP, corners, 1, 0, NT, NTP)
-    fill(NBP + NTP, corners, 2, 0, NT, NTP)
-    par_ref[...] = jnp.ones((4, NBP), F32)
-    sq = rest_len[...] * rest_len[...]
-    par_ref[0:1, 0:NB] = sq
-    par_ref[1:2, 0:NB] = -2.0 / sq
-    sq = rest_area[...] * rest_area[...]
-    par_ref[2:3, 0:NT] = sq
-    par_ref[3:4, 0:NT] = -0.125 / sq
+def incidence_kernel(ids, rests, m_ref, par_ref):
+    third = lax.axis_index("gx") % SPAN
+    bonds = pl.ds(pl.multiple_of(third * NBP, LANES), NBP)
+    corners = pl.ds(pl.multiple_of(third * NTP, LANES), NTP)
+    vid = lax.broadcasted_iota(jnp.int32, (NVP, NBP), 0)
+
+    def column(hi, lo):
+        plus = (vid[:, : hi.shape[1]] == hi).astype(F32)
+        return (plus - (vid[:, : hi.shape[1]] == lo).astype(F32)).astype(BF16)
+
+    m_ref[:, 0:NBP] = column(ids[0:1, bonds], ids[1:2, bonds])
+    m_ref[:, NBP : NBP + NTP] = column(ids[3:4, corners], ids[2:3, corners])
+    m_ref[:, NBP + NTP : COLS] = column(ids[4:5, corners], ids[2:3, corners])
+    sq = rests[0:1, bonds] * rests[0:1, bonds]
+    par_ref[0:1, :] = sq
+    par_ref[1:2, :] = -2.0 / sq
+    sq = rests[1:2, corners] * rests[1:2, corners]
+    par_ref[2:3, 0:NTP] = sq
+    par_ref[3:4, 0:NTP] = -0.125 / sq
+    par_ref[2:4, NTP:NBP] = jnp.ones((2, NBP - NTP), F32)
 
 
 def early_kernel(t0, t1, in_a, in_b, gl, gh, out_f, lfeat, fpart):
@@ -402,7 +401,7 @@
 
 
 def first_kernel(
-    starts, t0, t1, kicks, cells, solv,
+    starts, t0, t1, kicks, cells, solv, m_ref, par_ref,
     out_0, out_1, out_a, out_b, out_c, out_r,
     idx, cnt, cs, work, hot, lcell, qcell, right, qown, fpart, fcell,
 ):
@@ -430,27 +429,23 @@
     even = lax.axis_index("wa") % 2 == 0
     out_a[...] = jnp.where(even, out_1[...], out_0[...])
     out_b[...] = jnp.where(even, out_0[...], out_1[...])
-    out_r[...] = jnp.zeros((24, NVP), F32)
+    out_r[...] = DT * bond_force(out_c[0:24, :], m_ref, par_ref)
     for m in range(MAXCOV):
         mom = moment(fcell[m])
         react = DT * (cs[m] * mom[3:4] - mom)
         for c in range(3):
-            out_r[c * 8 + m : c * 8 + m + 1, :] = react[c : c + 1, :]
-
-
-def bond_kernel(cst, m_ref, par_ref, out_b):
-    out_b[...] = DT * bond_force(cst[0:24, :], m_ref, par_ref)
+            out_r[c * 8 + m : c * 8 + m + 1, :] += react[c : c + 1, :]
 
 
 def second_kernel(
-    starts, t0, t1, cst, share, bond, r0, r1, r2, r3, m_ref, par_ref,
+    starts, t0, t1, cst, share, r0, r1, r2, r3, m_ref, par_ref,
     out_f, out_s,
     idx, cnt, smap, cs, ps, work, hot, lcell, qcell, right, qown, fpart, fcell,
 ):
     j = lax.axis_index("gx")
     count = cover_slots(starts, j, idx, smap, cnt)
     ps[0:24, :] = cst[0:24, :]
-    ps[24:48, :] = cst[24:48, :] + bond[...] + share[...]
+    ps[24:48, :] = cst[24:48, :] + share[...]
     for m in range(MAXCOV):
         cell = idx[m]
         s = starts[cell]
@@ -468,7 +463,7 @@
             cs[m, c : c + 1, :] = ps[c * 8 + m : c * 8 + m + 1, :]
     own = own_frame(t0, t1)
     out_f[...] = membrane(own, count, cs, work, hot, lcell, qcell, right, qown, fpart, fcell)
-    ps[24:48, :] += DT * bond_force(ps[0:24, :], m_ref, par_ref)
+    bond = DT * bond_force(ps[0:24, :], m_ref, par_ref)
     out_s[...] = jnp.zeros(out_s.shape, F32)
     row = row_ids(NVP)
     shift = jnp.where(row == 1, (j * TF).astype(F32), jnp.where(row == 2, ZMID, 0.0))
@@ -477,9 +472,10 @@
         mom = moment(fcell[m])
         react = DT * (cs[m] * mom[3:4] - mom)
         push = pltpu.roll(jnp.where(row < 3, react, 0.0), 3, 0)
-        for c in range(6):
-            cs[m, c : c + 1, :] = ps[c * 8 + m : c * 8 + m + 1, :]
         whole = push + jnp.where(starts[cell] == j, cs[m] + shift, 0.0)
+        for c in range(3):
+            cs[m, c + 3 : c + 4, :] = bond[c * 8 + m : c * 8 + m + 1, :]
+        whole = whole + jnp.where((row >= 3) & (row < 6), cs[m], 0.0)
 
         @pl.when(m < count)
         def _():
@@ -528,14 +524,13 @@
     return [pltpu.VMEM((24 * LANES, 64), BF16), pltpu.VMEM((32, 8 * LANES), F32)]
 
 
-def call(kernel, name, outs, scratch, args, scalars=0):
+def call(kernel, outs, scratch, args, scalars=0):
     return pl.pallas_call(
         kernel,
         out_shape=tuple(jax.ShapeDtypeStruct(s, t) for s, t in outs),
         in_specs=[smem()] * scalars + [vmem()] * (len(args) - scalars),
         out_specs=tuple(vmem() for _ in outs),
         scratch_shapes=scratch,
-        name=name,
     )(*args)
 
 
@@ -577,6 +572,9 @@
         0,
     )
     cell = jnp.transpose(cell.reshape(6, 4, LANES), (1, 0, 2)).reshape(24, LANES)
+    cells = lax.all_to_all(
+        jnp.broadcast_to(cell[None], (SLABS, 24, LANES)), "gx", 0, 0, tiled=True
+    )
     tiles = jnp.transpose(
         jnp.concatenate([part_pos, part_vel, random_kicks[0:2]], 0), (1, 2, 0, 3)
     )
@@ -585,53 +583,49 @@
     kicks = jnp.transpose(random_kicks[2:4], (1, 2, 0, 3))
     part = ((8, TW * TF * LANES), F32)
     row = ((1, TF, 8, LANES), F32)
+    wide = SPAN * NBP
+    ids = jnp.concatenate(
+        [
+            jnp.pad(bond_ends.T, ((0, 0), (0, wide - NB)), constant_values=-1),
+            jnp.pad(triangles.T, ((0, 0), (0, wide - NT)), constant_values=-1),
+        ],
+        0,
+    )
+    rests = jnp.stack(
+        [
+            jnp.pad(rest_len, (0, wide - NB), constant_values=1.0),
+            jnp.pad(rest_area, (0, wide - NT), constant_values=1.0),
+        ]
+    )
     incidence, par = call(
-        incidence_kernel,
-        "incidence",
-        [((NVP, COLS), BF16), ((4, NBP), F32)],
-        [],
-        (bond_ends.T, triangles.T, rest_len[None], rest_area[None]),
-    )
-    incidence, cell, t0, t1 = lax.optimization_barrier((incidence, cell, t0, t1))
-    cells = lax.all_to_all(
-        jnp.broadcast_to(cell[None], (SLABS, 24, LANES)), "gx", 0, 0, tiled=True
+        incidence_kernel, [((NVP, COLS), BF16), ((4, NBP), F32)], [], (ids, rests)
     )
     sides = (jnp.where(even, t1, t0), jnp.where(even, t0, t1))
     swapped = swap(*sides)
-    (solv,) = call(
-        early_kernel,
-        "early",
-        [part],
-        solvent_scratch(),
-        (t0, t1, *swapped, *columns(t0, t1, *swapped)),
-    )
+    ends = columns(t0, t1, *swapped)
+    (solv,) = call(early_kernel, [part], solvent_scratch(), (t0, t1, *swapped, *ends))
     cell_scratch = pltpu.VMEM((8, 8, NVP), F32)
     n0, n1, n_a, n_b, cst, share = call(
         first_kernel,
-        "first",
         [row, row, row, row, ((48, NVP), F32), ((24, NVP), F32)],
         slot_scratch([cell_scratch]),
-        (cover_start, t0, t1, kicks, cells, solv),
+        (cover_start, t0, t1, kicks, cells, solv, incidence, par),
         1,
     )
     swapped = swap(n_a, n_b)
     got = [lax.ppermute(share, "gx", moves("gx", -s)) for s in (-2, -1, 1, 2)]
-    (bond,) = call(bond_kernel, "bond", [((24, NVP), F32)], [], (cst, incidence, par))
-    bond, *swapped = lax.optimization_barrier((bond, *swapped))
     memb, sends = call(
         second_kernel,
-        "second",
         [part, ((SLABS, 24, LANES), F32)],
         slot_scratch(
             [pltpu.SMEM((4 * SLABS,), jnp.int32), cell_scratch, pltpu.VMEM((48, NVP), F32)]
         ),
-        (cover_start, n0, n1, cst, share, bond, *got, incidence, par),
+        (cover_start, n0, n1, cst, share, *got, incidence, par),
         1,
     )
     final = jnp.sum(lax.all_to_all(sends, "gx", 0, 0, tiled=True), 0)
     out_pos, out_vel = call(
         late_kernel,
-        "late",
         [((3, TW, TF, LANES), F32)] * 2,
         solvent_scratch(),
         (n0, n1, *swapped, *columns(n0, n1, *swapped), memb),

time: 132 us -> 128 us (0.970)
  the two profiles are of different devices: /device:TPU:134 before, /device:TPU:190 now
where the time goes in v4:
time: 128 us; the launch traced here: 126 us
  starting transfers between devices  64 us (50%)
  Pallas kernels  32.9 us (26%)
  waiting for transfers between devices  18.3 us (14%)
  local copies, waits for them, and re-layouts  8.1 us (6%)
  other arithmetic  1.96 us (2%)
    pallas_call x5, Pallas kernels, call(): pl.pallas_call(kernel, out_shape=tuple((jax.ShapeDtypeStruct(s, t) for s,...  32.9 us
    ppermute x4, starting transfers between devices, body(): got = [lax.ppermute(share, 'gx', moves('gx', -s)) for s in (-2, -1, 1, 2)]  16.9 us
    all_to_all x1, starting transfers between devices, body(): lax.all_to_all(jnp.broadcast_to(cell[None], (SLABS, 24, LANES)), 'gx', 0,...  12.8 us
    ppermute x2, waiting for transfers between devices, columns(): gh = lax.ppermute(column(0), 'gx', moves('gx', -1))  12 us
    ppermute x2, starting transfers between devices, columns(): gl = lax.ppermute(column(TF - 1), 'gx', moves('gx', 1))  11.6 us
    all_to_all x1, starting transfers between devices, body(): final = jnp.sum(lax.all_to_all(sends, 'gx', 0, 0, tiled=True), 0)  8.59 us
    ppermute x2, starting transfers between devices, swap(): return (in_a, lax.ppermute(out_b, 'wa', odd_pairs))  5.89 us
    unnamed x47, local copies, waits for them, and re-layouts  5.36 us
  transfers between devices with their start and end apart: 14, of which 4 were waited for; matrix products, arithmetic and copies ran while one was open for 3% of the time, Pallas kernels for 10%

profile of v4, /device:TPU:190, one launch (start us, length us, event | category | flops | bytes accessed | tf_op | source)
XLA Modules:
  0.0 126.4 jit_solution(11605002770170956721)
XLA Ops:
  0.6 0.0 copy-start.11
  0.6 0.0 copy-start.16
  0.7 0.0 copy-start.17
  0.7 0.0 copy-start.18
  0.7 0.7 copy.20
  1.4 0.7 copy.21
  2.1 0.7 fusion.2
  2.9 0.6 broadcast_select_fusion
  3.5 4.0 %collective-permute-start.1 = (f32[1,4,8,128]{3,2,1,0:T(8,128)S(1)}, f32[1,4,8,128]{3,2,1,0:T(8,128)S(1)}, u32[]{:S(2)}, u32[]{:S(2)}) collective-permute-start(f32[1,4,8,128]{3,2,1,0:T(8,128)S(1)} %get-tuple-element.40), channel_id=1, source_target_pairs={{32,64},{64,32},{96,128},{128,96},{160,192},{192,160},{224,256},{2... | collective-permute-start | bytes 49160 | tf_op jit(solution)/shard_map/ppermute | solution.py:546
  7.5 2.3 %collective-permute-start = (f32[1,4,8,128]{3,2,1,0:T(8,128)S(1)}, f32[1,4,8,128]{3,2,1,0:T(8,128)S(1)}, u32[]{:S(2)}, u32[]{:S(2)}) collective-permute-start(f32[1,4,8,128]{3,2,1,0:T(8,128)S(1)} %get-tuple-element.43), channel_id=1, source_target_pairs={{0,32},{32,0},{64,96},{96,64},{128,160},{160,128},{192,224},{224,1... | collective-permute-start | bytes 49160 | tf_op jit(solution)/shard_map/ppermute | solution.py:545
  9.8 0.7 copy_bitcast_fusion.1
  10.5 0.8 broadcast_in_dim.12
  11.3 12.8 %all-to-all-start = ((f32[32,24,128]{2,1,0:T(8,128)}), f32[32,24,128]{2,1,0:T(8,128)S(1)}, u32[]{:S(2)}, u32[]{:S(2)}) async-start(f32[32,24,128]{2,1,0:T(8,128)} %broadcast_in_dim.12), calls=%async_computation | async-start | bytes 786432 | tf_op jit(solution)/shard_map/all_to_all | solution.py:575
  24.1 0.0 copy-done.11
  24.1 0.0 copy-done.16
  24.1 0.6 select_add_fusion.ids
  24.7 0.0 copy-done.17
  24.8 0.0 copy-done.18
  24.8 0.0 collective-permute-done.1.in_b
  24.8 0.0 copy-start.7
  24.8 0.0 collective-permute-done.in_a
  24.9 5.5 %collective-permute-start.2 = (f32[4,8,128]{2,1,0:T(8,128)S(1)}, f32[4,8,128]{2,1,0:T(8,128)S(1)}, u32[]{:S(2)}, u32[]{:S(2)}) collective-permute-start(f32[4,8,128]{2,1,0:T(8,128)S(1)} %pad_maximum_fusion), channel_id=1, source_target_pairs={{0,1},{1,2},{2,3},{3,4},{4,5},{5,6},{6,7},{7,8},{8,9},{9,10},{10,1... | collective-permute-start | bytes 49160 | tf_op jit(solution)/shard_map/ppermute | solution.py:558
  30.4 1.9 %collective-permute-start.3 = (f32[4,8,128]{2,1,0:T(8,128)S(1)}, f32[4,8,128]{2,1,0:T(8,128)S(1)}, u32[]{:S(2)}, u32[]{:S(2)}) collective-permute-start(f32[4,8,128]{2,1,0:T(8,128)S(1)} %pad_maximum_fusion.1), channel_id=1, source_target_pairs={{1,0},{2,1},{3,2},{4,3},{5,4},{6,5},{7,6},{8,7},{9,8},{10,9},{11,1... | collective-permute-start | bytes 49160 | tf_op jit(solution)/shard_map/ppermute | solution.py:559
  32.3 0.6 pad_maximum_fusion.4.rests
  32.9 0.6 copy.31
  33.5 2.4 %shard_map.130 = (bf16[512,1280]{1,0:T(8,128)(2,1)}, f32[4,512]{1,0:T(4,128)}) custom-call(s32[5,1536]{1,0:T(8,128)} %select_add_fusion.ids, f32[2,1536]{1,0:T(2,128)} %pad_maximum_fusion.4.rests), custom_call_target="tpu_custom_call" | custom-call | tf_op jit(solution)/shard_map/pallas_call | solution.py:528
  36.0 0.0 collective-permute-done.2.gl
  36.0 4.3 %collective-permute-done.3.gh = f32[4,8,128]{2,1,0:T(8,128)S(1)} collective-permute-done((f32[4,8,128]{2,1,0:T(8,128)S(1)}, f32[4,8,128]{2,1,0:T(8,128)S(1)}, u32[]{:S(2)}, u32[]{:S(2)}) %collective-permute-start.3) | collective-permute-done | bytes 16416 | tf_op jit(solution)/shard_map/ppermute | solution.py:559
  40.2 0.0 copy-done.12
  40.2 0.6 copy-done.14
  40.8 5.2 %shard_map.129.solv = f32[8,1024]{1,0:T(8,128)} custom-call(f32[1,4,8,128]{3,2,1,0:T(8,128)} %get-tuple-element.42.t0, f32[1,4,8,128]{3,2,1,0:T(8,128)} %get-tuple-element.41.t1, f32[1,4,8,128]{3,2,1,0:T(8,128)} %copy-done.8, f32[1,4,8,128]{3,2,1,0:T(8,128)} %copy-done.7, f32[4,8,128]{2,1,0:T(8,128)} %copy-done.12, f32[4,8,128]{2,1,0:T(8,128)} %copy-done.14), custom_call_target="tpu_custom_call" | custom-call | tf_op jit(solution)/shard_map/pallas_call | solution.py:528
  46.0 0.0 all-to-all-done.cells
  46.0 0.8 copy-done
  46.8 9.7 %shard_map.131 = (f32[1,4,8,128]{3,2,1,0:T(8,128)}, f32[1,4,8,128]{3,2,1,0:T(8,128)}, f32[1,4,8,128]{3,2,1,0:T(8,128)}, f32[1,4,8,128]{3,2,1,0:T(8,128)}, f32[48,512]{1,0:T(8,128)}, /*index=5*/f32[24,512]{1,0:T(8,128)}) custom-call(s32[32]{0:T(128)} %starts.3, f32[1,4,8,128]{3,2,1,0:T(8,128)} %get-tuple-element.42.t0, ...), custom_call_target="tpu_custom_call" | custom-call | tf_op jit(solution)/shard_map/pallas_call | solution.py:528
  56.5 2.1 %collective-permute-start.11 = (f32[24,512]{1,0:T(8,128)}, f32[24,512]{1,0:T(8,128)S(1)}, u32[]{:S(2)}, u32[]{:S(2)}) collective-permute-start(f32[24,512]{1,0:T(8,128)} %get-tuple-element.23.share), channel_id=1, source_target_pairs={{2,0},{3,1},{4,2},{5,3},{6,4},{7,5},{8,6},{9,7},{10,8},{11,9},{12,... | collective-permute-start | bytes 147464 | tf_op jit(solution)/shard_map/ppermute | solution.py:616
  58.6 1.9 %collective-permute-start.10 = (f32[24,512]{1,0:T(8,128)}, f32[24,512]{1,0:T(8,128)S(1)}, u32[]{:S(2)}, u32[]{:S(2)}) collective-permute-start(f32[24,512]{1,0:T(8,128)} %get-tuple-element.23.share), channel_id=1, source_target_pairs={{1,0},{2,1},{3,2},{4,3},{5,4},{6,5},{7,6},{8,7},{9,8},{10,9},{11,1... | collective-permute-start | bytes 147464 | tf_op jit(solution)/shard_map/ppermute | solution.py:616
  60.5 8.1 %collective-permute-start.9 = (f32[24,512]{1,0:T(8,128)}, f32[24,512]{1,0:T(8,128)S(1)}, u32[]{:S(2)}, u32[]{:S(2)}) collective-permute-start(f32[24,512]{1,0:T(8,128)} %get-tuple-element.23.share), channel_id=1, source_target_pairs={{0,1},{1,2},{2,3},{3,4},{4,5},{5,6},{6,7},{7,8},{8,9},{9,10},{10,1... | collective-permute-start | bytes 147464 | tf_op jit(solution)/shard_map/ppermute | solution.py:616
  68.7 4.8 %collective-permute-start.8 = (f32[24,512]{1,0:T(8,128)}, f32[24,512]{1,0:T(8,128)S(1)}, u32[]{:S(2)}, u32[]{:S(2)}) collective-permute-start(f32[24,512]{1,0:T(8,128)} %get-tuple-element.23.share), channel_id=1, source_target_pairs={{0,2},{1,3},{2,4},{3,5},{4,6},{5,7},{6,8},{7,9},{8,10},{9,11},{10,... | collective-permute-start | bytes 147464 | tf_op jit(solution)/shard_map/ppermute | solution.py:616
  73.5 0.0 collective-permute-done.11.r3
  73.5 0.0 collective-permute-done.10.r2
  73.5 0.0 collective-permute-done.9.r1
  73.6 0.0 copy-start.5
  73.6 2.3 %collective-permute-done.8.r0 = f32[24,512]{1,0:T(8,128)S(1)} collective-permute-done((f32[24,512]{1,0:T(8,128)}, f32[24,512]{1,0:T(8,128)S(1)}, u32[]{:S(2)}, u32[]{:S(2)}) %collective-permute-start.8) | collective-permute-done | bytes 49184 | tf_op jit(solution)/shard_map/ppermute | solution.py:616
  75.9 0.0 copy-done.4
  75.9 0.6 copy-done.6
  76.5 10.2 %shard_map.132 = (f32[8,1024]{1,0:T(8,128)}, f32[32,24,128]{2,1,0:T(8,128)}) custom-call(s32[32]{0:T(128)} %starts.3, f32[1,4,8,128]{3,2,1,0:T(8,128)} %get-tuple-element.18.t0, f32[1,4,8,128]{3,2,1,0:T(8,128)} %get-tuple-element.19.t1, f32[48,512]{1,0:T(8,128)} %get-tuple-element.22.cst, f32[24,512]{1,0:T(8,128)} %get-tuple-element.23.share, ...), custom_call_target="tpu_custom_call" | custom-call | tf_op jit(solution)/shard_map/pallas_call | solution.py:528
  86.7 8.6 %all-to-all-start.1 = ((f32[32,24,128]{2,1,0:T(8,128)}), f32[32,24,128]{2,1,0:T(8,128)S(1)}, u32[]{:S(2)}, u32[]{:S(2)}) async-start(f32[32,24,128]{2,1,0:T(8,128)} %get-tuple-element.27), calls=%async_computation.1 | async-start | bytes 786432 | tf_op jit(solution)/shard_map/all_to_all | solution.py:626
  95.3 0.0 copy-done.20
  95.3 1.9 %collective-permute-start.4 = (f32[1,4,8,128]{3,2,1,0:T(8,128)S(1)}, f32[1,4,8,128]{3,2,1,0:T(8,128)S(1)}, u32[]{:S(2)}, u32[]{:S(2)}) collective-permute-start(f32[1,4,8,128]{3,2,1,0:T(8,128)S(1)} %copy-done.20), channel_id=1, source_target_pairs={{0,32},{32,0},{64,96},{96,64},{128,160},{160,128},{192,224},{224,1... | collective-permute-start | bytes 49160 | tf_op jit(solution)/shard_map/ppermute | solution.py:545
  97.3 0.0 copy-done.19
  97.3 1.9 %collective-permute-start.5 = (f32[1,4,8,128]{3,2,1,0:T(8,128)S(1)}, f32[1,4,8,128]{3,2,1,0:T(8,128)S(1)}, u32[]{:S(2)}, u32[]{:S(2)}) collective-permute-start(f32[1,4,8,128]{3,2,1,0:T(8,128)S(1)} %copy-done.19), channel_id=1, source_target_pairs={{32,64},{64,32},{96,128},{128,96},{160,192},{192,160},{224,256},{2... | collective-permute-start | bytes 49160 | tf_op jit(solution)/shard_map/ppermute | solution.py:546
  99.2 0.0 collective-permute-done.4.in_a
  99.2 0.0 copy-start.9
  99.3 4.0 %collective-permute-done.5.in_b = f32[1,4,8,128]{3,2,1,0:T(8,128)S(1)} collective-permute-done((f32[1,4,8,128]{3,2,1,0:T(8,128)S(1)}, f32[1,4,8,128]{3,2,1,0:T(8,128)S(1)}, u32[]{:S(2)}, u32[]{:S(2)}) %collective-permute-start.5) | collective-permute-done | bytes 16416 | tf_op jit(solution)/shard_map/ppermute | solution.py:546
  103.3 6.1 %collective-permute-start.6 = (f32[4,8,128]{2,1,0:T(8,128)S(1)}, f32[4,8,128]{2,1,0:T(8,128)S(1)}, u32[]{:S(2)}, u32[]{:S(2)}) collective-permute-start(f32[4,8,128]{2,1,0:T(8,128)S(1)} %pad_maximum_fusion.2), channel_id=1, source_target_pairs={{0,1},{1,2},{2,3},{3,4},{4,5},{5,6},{6,7},{7,8},{8,9},{9,10},{10,1... | collective-permute-start | bytes 49160 | tf_op jit(solution)/shard_map/ppermute | solution.py:558
  109.3 2.1 %collective-permute-start.7 = (f32[4,8,128]{2,1,0:T(8,128)S(1)}, f32[4,8,128]{2,1,0:T(8,128)S(1)}, u32[]{:S(2)}, u32[]{:S(2)}) collective-permute-start(f32[4,8,128]{2,1,0:T(8,128)S(1)} %pad_maximum_fusion.3), channel_id=1, source_target_pairs={{1,0},{2,1},{3,2},{4,3},{5,4},{6,5},{7,6},{8,7},{9,8},{10,9},{11,1... | collective-permute-start | bytes 49160 | tf_op jit(solution)/shard_map/ppermute | solution.py:559
  111.5 0.0 collective-permute-done.6.gl
  111.5 7.7 %collective-permute-done.7.gh = f32[4,8,128]{2,1,0:T(8,128)S(1)} collective-permute-done((f32[4,8,128]{2,1,0:T(8,128)S(1)}, f32[4,8,128]{2,1,0:T(8,128)S(1)}, u32[]{:S(2)}, u32[]{:S(2)}) %collective-permute-start.7) | collective-permute-done | bytes 16416 | tf_op jit(solution)/shard_map/ppermute | solution.py:559
  119.2 0.0 copy-done.10
  119.2 0.6 copy-done.15
  119.8 5.3 %shard_map.133 = (f32[3,2,4,128]{3,2,1,0:T(4,128)}, f32[3,2,4,128]{3,2,1,0:T(4,128)}) custom-call(f32[1,4,8,128]{3,2,1,0:T(8,128)} %get-tuple-element.18.t0, f32[1,4,8,128]{3,2,1,0:T(8,128)} %get-tuple-element.19.t1, f32[1,4,8,128]{3,2,1,0:T(8,128)} %copy-done.9, f32[1,4,8,128]{3,2,1,0:T(8,128)} %copy-done.10, f32[4,8,128]{2,1,0:T(8,128)} %copy-done.13, ...), custom_call_target="tpu_custom_call" | custom-call | tf_op jit(solution)/shard_map/pallas_call | solution.py:528
  125.1 0.0 all-to-all-done.1
  125.2 0.6 broadcast_in_dim.13
  125.8 0.6 add.26
  (42 shorter events, 0.2 us)
Async XLA Ops:
  0.6 23.5 %copy-start.11 = (s32[992,3]{0,1:T(4,128)S(1)}, s32[992,3]{0,1:T(4,128)}, u32[]{:S(2)}) copy-start(s32[992,3]{0,1:T(4,128)} %param.17) | copy-start | bytes 35716
  0.6 23.5 %copy-start.16 = (s32[1488,2]{0,1:T(2,128)S(1)}, s32[1488,2]{0,1:T(2,128)}, u32[]{:S(2)}) copy-start(s32[1488,2]{0,1:T(2,128)} %param.16) | copy-start | bytes 35716
  0.7 24.1 %copy-start.17 = (f32[1488]{0:T(1024)S(1)}, f32[1488]{0:T(1024)}, u32[]{:S(2)}) copy-start(f32[1488]{0:T(1024)} %param.18) | copy-start | bytes 17860
  0.7 24.1 %copy-start.18 = (f32[992]{0:T(1024)S(1)}, f32[992]{0:T(1024)}, u32[]{:S(2)}) copy-start(f32[992]{0:T(1024)} %param.19) | copy-start | bytes 11908
  3.5 21.3 %collective-permute-start.1 = (f32[1,4,8,128]{3,2,1,0:T(8,128)S(1)}, f32[1,4,8,128]{3,2,1,0:T(8,128)S(1)}, u32[]{:S(2)}, u32[]{:S(2)}) collective-permute-start(f32[1,4,8,128]{3,2,1,0:T(8,128)S(1)} %get-tuple-element.40), channel_id=1, source_target_pairs={{32,64},{64,32},{96,128},{128,96},{160,192},{192,160},{224,256},{2... | collective-permute-start | bytes 49160 | tf_op jit(solution)/shard_map/ppermute | solution.py:546
  7.5 17.4 %collective-permute-start = (f32[1,4,8,128]{3,2,1,0:T(8,128)S(1)}, f32[1,4,8,128]{3,2,1,0:T(8,128)S(1)}, u32[]{:S(2)}, u32[]{:S(2)}) collective-permute-start(f32[1,4,8,128]{3,2,1,0:T(8,128)S(1)} %get-tuple-element.43), channel_id=1, source_target_pairs={{0,32},{32,0},{64,96},{96,64},{128,160},{160,128},{192,224},{224,1... | collective-permute-start | bytes 49160 | tf_op jit(solution)/shard_map/ppermute | solution.py:545
  11.3 34.7 %all-to-all-start = ((f32[32,24,128]{2,1,0:T(8,128)}), f32[32,24,128]{2,1,0:T(8,128)S(1)}, u32[]{:S(2)}, u32[]{:S(2)}) async-start(f32[32,24,128]{2,1,0:T(8,128)} %broadcast_in_dim.12), calls=%async_computation | async-start | bytes 786432 | tf_op jit(solution)/shard_map/all_to_all | solution.py:575
  24.8 15.4 %copy-start.7 = (f32[1,4,8,128]{3,2,1,0:T(8,128)}, f32[1,4,8,128]{3,2,1,0:T(8,128)S(1)}, u32[]{:S(2)}) copy-start(f32[1,4,8,128]{3,2,1,0:T(8,128)S(1)} %collective-permute-done.1.in_b) | copy-start | bytes 49156
  24.8 15.4 %copy-start.8 = (f32[1,4,8,128]{3,2,1,0:T(8,128)}, f32[1,4,8,128]{3,2,1,0:T(8,128)S(1)}, u32[]{:S(2)}) copy-start(f32[1,4,8,128]{3,2,1,0:T(8,128)S(1)} %collective-permute-done.in_a) | copy-start | bytes 49156
  24.9 11.1 %collective-permute-start.2 = (f32[4,8,128]{2,1,0:T(8,128)S(1)}, f32[4,8,128]{2,1,0:T(8,128)S(1)}, u32[]{:S(2)}, u32[]{:S(2)}) collective-permute-start(f32[4,8,128]{2,1,0:T(8,128)S(1)} %pad_maximum_fusion), channel_id=1, source_target_pairs={{0,1},{1,2},{2,3},{3,4},{4,5},{5,6},{6,7},{7,8},{8,9},{9,10},{10,1... | collective-permute-start | bytes 49160 | tf_op jit(solution)/shard_map/ppermute | solution.py:558
  30.4 9.9 %collective-permute-start.3 = (f32[4,8,128]{2,1,0:T(8,128)S(1)}, f32[4,8,128]{2,1,0:T(8,128)S(1)}, u32[]{:S(2)}, u32[]{:S(2)}) collective-permute-start(f32[4,8,128]{2,1,0:T(8,128)S(1)} %pad_maximum_fusion.1), channel_id=1, source_target_pairs={{1,0},{2,1},{3,2},{4,3},{5,4},{6,5},{7,6},{8,7},{9,8},{10,9},{11,1... | collective-permute-start | bytes 49160 | tf_op jit(solution)/shard_map/ppermute | solution.py:559
  36.0 4.3 %copy-start.12 = (f32[4,8,128]{2,1,0:T(8,128)}, f32[4,8,128]{2,1,0:T(8,128)S(1)}, u32[]{:S(2)}) copy-start(f32[4,8,128]{2,1,0:T(8,128)S(1)} %collective-permute-done.2.gl) | copy-start | bytes 49156
  40.2 0.6 copy-start.14
  46.0 0.8 copy-start
  56.5 38.8 %copy-start.1 = (f32[1,4,8,128]{3,2,1,0:T(8,128)S(1)}, f32[1,4,8,128]{3,2,1,0:T(8,128)}, u32[]{:S(2)}) copy-start(f32[1,4,8,128]{3,2,1,0:T(8,128)} %get-tuple-element.18.t0) | copy-start | bytes 49156
  56.5 38.8 %copy-start.20 = (f32[1,4,8,128]{3,2,1,0:T(8,128)S(1)}, f32[1,4,8,128]{3,2,1,0:T(8,128)}, u32[]{:S(2)}) copy-start(f32[1,4,8,128]{3,2,1,0:T(8,128)} %get-tuple-element.20) | copy-start | bytes 49156
  56.5 40.8 %copy-start.19 = (f32[1,4,8,128]{3,2,1,0:T(8,128)S(1)}, f32[1,4,8,128]{3,2,1,0:T(8,128)}, u32[]{:S(2)}) copy-start(f32[1,4,8,128]{3,2,1,0:T(8,128)} %get-tuple-element.21) | copy-start | bytes 49156
  56.5 42.7 %copy-start.2 = (f32[1,4,8,128]{3,2,1,0:T(8,128)S(1)}, f32[1,4,8,128]{3,2,1,0:T(8,128)}, u32[]{:S(2)}) copy-start(f32[1,4,8,128]{3,2,1,0:T(8,128)} %get-tuple-element.19.t1) | copy-start | bytes 49156
  56.5 17.0 %collective-permute-start.11 = (f32[24,512]{1,0:T(8,128)}, f32[24,512]{1,0:T(8,128)S(1)}, u32[]{:S(2)}, u32[]{:S(2)}) collective-permute-start(f32[24,512]{1,0:T(8,128)} %get-tuple-element.23.share), channel_id=1, source_target_pairs={{2,0},{3,1},{4,2},{5,3},{6,4},{7,5},{8,6},{9,7},{10,8},{11,9},{12,... | collective-permute-start | bytes 147464 | tf_op jit(solution)/shard_map/ppermute | solution.py:616
  58.6 14.9 %collective-permute-start.10 = (f32[24,512]{1,0:T(8,128)}, f32[24,512]{1,0:T(8,128)S(1)}, u32[]{:S(2)}, u32[]{:S(2)}) collective-permute-start(f32[24,512]{1,0:T(8,128)} %get-tuple-element.23.share), channel_id=1, source_target_pairs={{1,0},{2,1},{3,2},{4,3},{5,4},{6,5},{7,6},{8,7},{9,8},{10,9},{11,1... | collective-permute-start | bytes 147464 | tf_op jit(solution)/shard_map/ppermute | solution.py:616
  60.5 13.0 %collective-permute-start.9 = (f32[24,512]{1,0:T(8,128)}, f32[24,512]{1,0:T(8,128)S(1)}, u32[]{:S(2)}, u32[]{:S(2)}) collective-permute-start(f32[24,512]{1,0:T(8,128)} %get-tuple-element.23.share), channel_id=1, source_target_pairs={{0,1},{1,2},{2,3},{3,4},{4,5},{5,6},{6,7},{7,8},{8,9},{9,10},{10,1... | collective-permute-start | bytes 147464 | tf_op jit(solution)/shard_map/ppermute | solution.py:616
  68.7 7.2 %collective-permute-start.8 = (f32[24,512]{1,0:T(8,128)}, f32[24,512]{1,0:T(8,128)S(1)}, u32[]{:S(2)}, u32[]{:S(2)}) collective-permute-start(f32[24,512]{1,0:T(8,128)} %get-tuple-element.23.share), channel_id=1, source_target_pairs={{0,2},{1,3},{2,4},{3,5},{4,6},{5,7},{6,8},{7,9},{8,10},{9,11},{10,... | collective-permute-start | bytes 147464 | tf_op jit(solution)/shard_map/ppermute | solution.py:616
  73.5 2.4 %copy-start.3 = (f32[24,512]{1,0:T(8,128)}, f32[24,512]{1,0:T(8,128)S(1)}, u32[]{:S(2)}) copy-start(f32[24,512]{1,0:T(8,128)S(1)} %collective-permute-done.11.r3) | copy-start | bytes 147460
  73.5 2.4 %copy-start.4 = (f32[24,512]{1,0:T(8,128)}, f32[24,512]{1,0:T(8,128)S(1)}, u32[]{:S(2)}) copy-start(f32[24,512]{1,0:T(8,128)S(1)} %collective-permute-done.10.r2) | copy-start | bytes 147460
  73.6 2.4 %copy-start.5 = (f32[24,512]{1,0:T(8,128)}, f32[24,512]{1,0:T(8,128)S(1)}, u32[]{:S(2)}) copy-start(f32[24,512]{1,0:T(8,128)S(1)} %collective-permute-done.9.r1) | copy-start | bytes 147460
  75.9 0.6 copy-start.6
  86.7 38.4 %all-to-all-start.1 = ((f32[32,24,128]{2,1,0:T(8,128)}), f32[32,24,128]{2,1,0:T(8,128)S(1)}, u32[]{:S(2)}, u32[]{:S(2)}) async-start(f32[32,24,128]{2,1,0:T(8,128)} %get-tuple-element.27), calls=%async_computation.1 | async-start | bytes 786432 | tf_op jit(solution)/shard_map/all_to_all | solution.py:626
  95.3 3.9 %collective-permute-start.4 = (f32[1,4,8,128]{3,2,1,0:T(8,128)S(1)}, f32[1,4,8,128]{3,2,1,0:T(8,128)S(1)}, u32[]{:S(2)}, u32[]{:S(2)}) collective-permute-start(f32[1,4,8,128]{3,2,1,0:T(8,128)S(1)} %copy-done.20), channel_id=1, source_target_pairs={{0,32},{32,0},{64,96},{96,64},{128,160},{160,128},{192,224},{224,1... | collective-permute-start | bytes 49160 | tf_op jit(solution)/shard_map/ppermute | solution.py:545
  97.3 6.0 %collective-permute-start.5 = (f32[1,4,8,128]{3,2,1,0:T(8,128)S(1)}, f32[1,4,8,128]{3,2,1,0:T(8,128)S(1)}, u32[]{:S(2)}, u32[]{:S(2)}) collective-permute-start(f32[1,4,8,128]{3,2,1,0:T(8,128)S(1)} %copy-done.19), channel_id=1, source_target_pairs={{32,64},{64,32},{96,128},{128,96},{160,192},{192,160},{224,256},{2... | collective-permute-start | bytes 49160 | tf_op jit(solution)/shard_map/ppermute | solution.py:546
  99.2 20.0 %copy-start.9 = (f32[1,4,8,128]{3,2,1,0:T(8,128)}, f32[1,4,8,128]{3,2,1,0:T(8,128)S(1)}, u32[]{:S(2)}) copy-start(f32[1,4,8,128]{3,2,1,0:T(8,128)S(1)} %collective-permute-done.4.in_a) | copy-start | bytes 49156
  103.2 16.0 %copy-start.10 = (f32[1,4,8,128]{3,2,1,0:T(8,128)}, f32[1,4,8,128]{3,2,1,0:T(8,128)S(1)}, u32[]{:S(2)}) copy-start(f32[1,4,8,128]{3,2,1,0:T(8,128)S(1)} %collective-permute-done.5.in_b) | copy-start | bytes 49156
  103.3 8.2 %collective-permute-start.6 = (f32[4,8,128]{2,1,0:T(8,128)S(1)}, f32[4,8,128]{2,1,0:T(8,128)S(1)}, u32[]{:S(2)}, u32[]{:S(2)}) collective-permute-start(f32[4,8,128]{2,1,0:T(8,128)S(1)} %pad_maximum_fusion.2), channel_id=1, source_target_pairs={{0,1},{1,2},{2,3},{3,4},{4,5},{5,6},{6,7},{7,8},{8,9},{9,10},{10,1... | collective-permute-start | bytes 49160 | tf_op jit(solution)/shard_map/ppermute | solution.py:558
  109.3 9.9 %collective-permute-start.7 = (f32[4,8,128]{2,1,0:T(8,128)S(1)}, f32[4,8,128]{2,1,0:T(8,128)S(1)}, u32[]{:S(2)}, u32[]{:S(2)}) collective-permute-start(f32[4,8,128]{2,1,0:T(8,128)S(1)} %pad_maximum_fusion.3), channel_id=1, source_target_pairs={{1,0},{2,1},{3,2},{4,3},{5,4},{6,5},{7,6},{8,7},{9,8},{10,9},{11,1... | collective-permute-start | bytes 49160 | tf_op jit(solution)/shard_map/ppermute | solution.py:559
  111.5 7.7 %copy-start.13 = (f32[4,8,128]{2,1,0:T(8,128)}, f32[4,8,128]{2,1,0:T(8,128)S(1)}, u32[]{:S(2)}) copy-start(f32[4,8,128]{2,1,0:T(8,128)S(1)} %collective-permute-done.6.gl) | copy-start | bytes 49156
  119.2 0.6 copy-start.15

commit v5 on v4

--- a/solution.py
+++ b/solution.py
@@ -139,7 +139,7 @@
         count = count + covered.astype(jnp.int32)
         if slot_map is not None:
             for k, shift in enumerate(shifts):
-                slot_map[k * SLABS + c] = jnp.minimum(counts[k], 7)
+                slot_map[k * SLABS + c] = jnp.minimum(counts[k], MAXCOV - 1)
                 cov = (s <= j + shift) & (j + shift < s + SPAN)
                 counts[k] = counts[k] + cov.astype(jnp.int32)
     count = jnp.minimum(count, MAXCOV)
@@ -180,26 +180,53 @@
     return force + back(jnp.concatenate(cross(g, a), 0), three)
 
 
-def solvent(near, lfeat, fpart):
-    nst = jnp.concatenate(near, 1)
-    own = own_of(near)
+def solvent(own, others, runs, lfeat, fpart):
     ra, rc, rb = right_features(own)
-    lfeat[...] = left_features(nst).T.astype(BF16)
-    qnear = sum_features(nst)
+    lfeat[...] = left_features(others).T.astype(BF16)
+    qnear = sum_features(others)
+    for t in range(TW * TF):
+        cols = slice(t * LANES, (t + 1) * LANES)
+        rt = jnp.concatenate([ra[:, cols], rc[:, cols], rb[:, cols]], 1)
+        spans = [(a * LANES, (a + n) * LANES) for a, n in runs[t]]
+        out = nn(jnp.concatenate([lfeat[a:b, :] for a, b in spans], 0), rt)
+        weight = jnp.maximum(out[:, :LANES], 0.0)
+        s = weight * (out[:, 2 * LANES :] - weight * out[:, LANES : 2 * LANES])
+        q = jnp.concatenate([qnear[:, a:b] for a, b in spans], 1)
+        acc = nn(q, jnp.concatenate(halves(s), 1))
+        fpart[:, cols] = acc[:, :LANES] + acc[:, LANES:]
+
+
+def all_runs():
+    return [[((w + dw) * (TF + 2) + f, 3) for dw in range(3)] for w in range(TW) for f in range(TF)]
+
+
+def inner_runs():
+    out = []
+    for _ in range(TW):
+        for f in range(TF):
+            first, last = max(f - 1, 0), min(f + 1, TF - 1)
+            out.append([(v * TF + first, last - first + 1) for v in range(TW)])
+    return out
+
+
+def outer_tiles(near):
+    wide = TF + 2
+    rows = near[:wide] + near[-wide:]
+    return rows + [near[(w + 1) * wide] for w in range(TW)] + [near[(w + 2) * wide - 1] for w in range(TW)]
+
+
+def outer_runs():
+    wide = TF + 2
+    out = []
     for w in range(TW):
         for f in range(TF):
-            t = w * TF + f
-            cols = slice(t * LANES, (t + 1) * LANES)
-            rt = jnp.concatenate([ra[:, cols], rc[:, cols], rb[:, cols]], 1)
-            firsts = [((w + dw) * (TF + 2) + f) * LANES for dw in range(3)]
-            near_rows = jnp.concatenate([lfeat[a : a + 3 * LANES, :] for a in firsts], 0)
-            out = nn(near_rows, rt)
-            weight = jnp.maximum(out[:, :LANES], 0.0)
-            s = weight * (out[:, 2 * LANES :] - weight * out[:, LANES : 2 * LANES])
-            q = jnp.concatenate([qnear[:, a : a + 3 * LANES] for a in firsts], 1)
-            acc = nn(q, jnp.concatenate(halves(s), 1))
-            fpart[:, cols] = acc[:, :LANES] + acc[:, LANES:]
-    return own
+            run = [(w * wide + f, 3)]
+            if f == 0:
+                run.append((2 * wide, TW))
+            if f == TF - 1:
+                run.append((2 * wide + TW, TW))
+            out.append(run)
+    return out
 
 
 def own_of(near):
@@ -391,7 +418,9 @@
 
 
 def early_kernel(t0, t1, in_a, in_b, gl, gh, out_f, lfeat, fpart):
-    own = solvent(near_frames(t0, t1, in_a, in_b, gl, gh), lfeat, fpart)
+    near = near_frames(t0, t1, in_a, in_b, gl, gh)
+    own = own_of(near)
+    solvent(own, jnp.concatenate(near, 1), all_runs(), lfeat, fpart)
     out_f[...] = force_of(own, fpart)
 
 
@@ -429,12 +458,14 @@
     even = lax.axis_index("wa") % 2 == 0
     out_a[...] = jnp.where(even, out_1[...], out_0[...])
     out_b[...] = jnp.where(even, out_0[...], out_1[...])
-    out_r[...] = DT * bond_force(out_c[0:24, :], m_ref, par_ref)
+    bond = DT * bond_force(out_c[0:24, :], m_ref, par_ref)
+    out_r[15:16, :] = jnp.zeros((1, NVP), F32)
     for m in range(MAXCOV):
         mom = moment(fcell[m])
         react = DT * (cs[m] * mom[3:4] - mom)
         for c in range(3):
-            out_r[c * 8 + m : c * 8 + m + 1, :] += react[c : c + 1, :]
+            at = c * MAXCOV + m
+            out_r[at : at + 1, :] = bond[c * 8 + m : c * 8 + m + 1, :] + react[c : c + 1, :]
 
 
 def second_kernel(
@@ -445,16 +476,19 @@
     j = lax.axis_index("gx")
     count = cover_slots(starts, j, idx, smap, cnt)
     ps[0:24, :] = cst[0:24, :]
-    ps[24:48, :] = cst[24:48, :] + share[...]
+    ps[24:48, :] = cst[24:48, :]
     for m in range(MAXCOV):
         cell = idx[m]
         s = starts[cell]
+        for c in range(3):
+            at = c * MAXCOV + m
+            ps[24 + c * 8 + m : 25 + c * 8 + m, :] += share[at : at + 1, :]
         for k, (shift, ref) in enumerate(((-2, r0), (-1, r1), (1, r2), (2, r3))):
             slot = smap[k * SLABS + cell]
             there = (m < count) & (s <= j + shift) & (j + shift < s + SPAN)
             for c in range(3):
                 at = 24 + c * 8 + m
-                got = ref[pl.ds(c * 8 + slot, 1), :]
+                got = ref[pl.ds(c * MAXCOV + slot, 1), :]
                 ps[at : at + 1, :] += jnp.where(there, got, 0.0)
     ps[0:24, :] += DT * ps[24:48, :]
     for m in range(MAXCOV):
@@ -483,8 +517,16 @@
                 out_s[cell, k * 6 : k * 6 + 6, :] = whole[0:6, k * LANES : (k + 1) * LANES]
 
 
+def inner_kernel(t0, t1, memb, out_f, lfeat, fpart):
+    own = own_frame(t0, t1)
+    solvent(own, own, inner_runs(), lfeat, fpart)
+    out_f[...] = memb[...] + force_of(own, fpart)
+
+
 def late_kernel(t0, t1, in_a, in_b, gl, gh, memb, out_p, out_v, lfeat, fpart):
-    own = solvent(near_frames(t0, t1, in_a, in_b, gl, gh), lfeat, fpart)
+    near = near_frames(t0, t1, in_a, in_b, gl, gh)
+    own = own_of(near)
+    solvent(own, jnp.concatenate(outer_tiles(near), 1), outer_runs(), lfeat, fpart)
     force = memb[...] + force_of(own, fpart)
     for w, ref in enumerate((t0, t1)):
         for f in range(TF):
@@ -520,8 +562,8 @@
     )
 
 
-def solvent_scratch():
-    return [pltpu.VMEM((24 * LANES, 64), BF16), pltpu.VMEM((32, 8 * LANES), F32)]
+def solvent_scratch(tiles):
+    return [pltpu.VMEM((tiles * LANES, 64), BF16), pltpu.VMEM((32, 8 * LANES), F32)]
 
 
 def call(kernel, outs, scratch, args, scalars=0):
@@ -603,11 +645,11 @@
     sides = (jnp.where(even, t1, t0), jnp.where(even, t0, t1))
     swapped = swap(*sides)
     ends = columns(t0, t1, *swapped)
-    (solv,) = call(early_kernel, [part], solvent_scratch(), (t0, t1, *swapped, *ends))
+    (solv,) = call(early_kernel, [part], solvent_scratch(24), (t0, t1, *swapped, *ends))
     cell_scratch = pltpu.VMEM((8, 8, NVP), F32)
     n0, n1, n_a, n_b, cst, share = call(
         first_kernel,
-        [row, row, row, row, ((48, NVP), F32), ((24, NVP), F32)],
+        [row, row, row, row, ((48, NVP), F32), ((16, NVP), F32)],
         slot_scratch([cell_scratch]),
         (cover_start, t0, t1, kicks, cells, solv, incidence, par),
         1,
@@ -624,11 +666,13 @@
         1,
     )
     final = jnp.sum(lax.all_to_all(sends, "gx", 0, 0, tiled=True), 0)
+    ends = columns(n0, n1, *swapped)
+    (inner,) = call(inner_kernel, [part], solvent_scratch(8), (n0, n1, memb))
     out_pos, out_vel = call(
         late_kernel,
         [((3, TW, TF, LANES), F32)] * 2,
-        solvent_scratch(),
-        (n0, n1, *swapped, *columns(n0, n1, *swapped), memb),
+        solvent_scratch(16),
+        (n0, n1, *swapped, *ends, inner),
     )
     final = jnp.transpose(final.reshape(4, 6, LANES), (1, 0, 2)).reshape(6, NVP)
     new_vel = final[3:6, None, :NV]

time: 128 us -> 126 us (0.984)
  waiting for transfers between devices: 18.3 us -> 14.1 us
  Pallas kernels: 32.9 us -> 35.5 us
    ppermute x2, waiting for transfers between devices: 12 us -> 7.95 us  [columns(): gh = lax.ppermute(column(0), 'gx', moves('gx', -1))]
    pallas_call x5 -> x6, Pallas kernels: 32.9 us -> 35.5 us  [call(): pl.pallas_call(kernel, out_shape=tuple((jax.ShapeDtypeStruct(s, t) for s,...]
  transfers between devices with their start and end apart: 14 -> 14, of which waited for: 4 -> 4; matrix products, arithmetic and copies ran while one was open for 3% -> 3% of each run, Pallas kernels for 10% -> 13%
where the time goes in v5:
time: 126 us; the launch traced here: 125 us
  starting transfers between devices  63.9 us (51%)
  Pallas kernels  35.5 us (28%)
  waiting for transfers between devices  14.1 us (11%)
  local copies, waits for them, and re-layouts  8.09 us (6%)
  other arithmetic  1.96 us (2%)
    pallas_call x6, Pallas kernels, call(): pl.pallas_call(kernel, out_shape=tuple((jax.ShapeDtypeStruct(s, t) for s,...  35.5 us
    ppermute x4, starting transfers between devices, body(): got = [lax.ppermute(share, 'gx', moves('gx', -s)) for s in (-2, -1, 1, 2)]  16.9 us
    all_to_all x1, starting transfers between devices, body(): lax.all_to_all(jnp.broadcast_to(cell[None], (SLABS, 24, LANES)), 'gx', 0,...  12.8 us
    ppermute x2, starting transfers between devices, columns(): gl = lax.ppermute(column(TF - 1), 'gx', moves('gx', 1))  11.6 us
    all_to_all x1, starting transfers between devices, body(): final = jnp.sum(lax.all_to_all(sends, 'gx', 0, 0, tiled=True), 0)  8.38 us
    ppermute x2, waiting for transfers between devices, columns(): gh = lax.ppermute(column(0), 'gx', moves('gx', -1))  7.95 us
    ppermute x2, starting transfers between devices, swap(): return (in_a, lax.ppermute(out_b, 'wa', odd_pairs))  5.89 us
    unnamed x47, local copies, waits for them, and re-layouts  5.35 us
  transfers between devices with their start and end apart: 14, of which 4 were waited for; matrix products, arithmetic and copies ran while one was open for 3% of the time, Pallas kernels for 13%

profile of v5, /device:TPU:190, one launch (start us, length us, event | category | flops | bytes accessed | tf_op | source)
XLA Modules:
  0.0 124.6 jit_solution(6542102714204147265)
XLA Ops:
  0.6 0.0 copy-start.11
  0.6 0.0 copy-start.16
  0.7 0.0 copy-start.17
  0.7 0.0 copy-start.18
  0.7 0.7 copy.20
  1.4 0.7 copy.21
  2.1 0.7 fusion.2
  2.9 0.6 broadcast_select_fusion
  3.5 4.0 %collective-permute-start.1 = (f32[1,4,8,128]{3,2,1,0:T(8,128)S(1)}, f32[1,4,8,128]{3,2,1,0:T(8,128)S(1)}, u32[]{:S(2)}, u32[]{:S(2)}) collective-permute-start(f32[1,4,8,128]{3,2,1,0:T(8,128)S(1)} %get-tuple-element.40), channel_id=1, source_target_pairs={{32,64},{64,32},{96,128},{128,96},{160,192},{192,160},{224,256},{2... | collective-permute-start | bytes 49160 | tf_op jit(solution)/shard_map/ppermute | solution.py:588
  7.5 2.3 %collective-permute-start = (f32[1,4,8,128]{3,2,1,0:T(8,128)S(1)}, f32[1,4,8,128]{3,2,1,0:T(8,128)S(1)}, u32[]{:S(2)}, u32[]{:S(2)}) collective-permute-start(f32[1,4,8,128]{3,2,1,0:T(8,128)S(1)} %get-tuple-element.43), channel_id=1, source_target_pairs={{0,32},{32,0},{64,96},{96,64},{128,160},{160,128},{192,224},{224,1... | collective-permute-start | bytes 49160 | tf_op jit(solution)/shard_map/ppermute | solution.py:587
  9.8 0.7 copy_bitcast_fusion.1
  10.5 0.8 broadcast_in_dim.12
  11.3 12.8 %all-to-all-start = ((f32[32,24,128]{2,1,0:T(8,128)}), f32[32,24,128]{2,1,0:T(8,128)S(1)}, u32[]{:S(2)}, u32[]{:S(2)}) async-start(f32[32,24,128]{2,1,0:T(8,128)} %broadcast_in_dim.12), calls=%async_computation | async-start | bytes 786432 | tf_op jit(solution)/shard_map/all_to_all | solution.py:617
  24.1 0.0 copy-done.11
  24.1 0.0 copy-done.16
  24.1 0.6 select_add_fusion.ids
  24.7 0.0 copy-done.17
  24.8 0.0 copy-done.18
  24.8 0.0 collective-permute-done.1.in_b
  24.8 0.0 copy-start.3
  24.8 0.0 collective-permute-done.in_a
  24.8 0.0 copy-start.4
  24.9 5.5 %collective-permute-start.2 = (f32[4,8,128]{2,1,0:T(8,128)S(1)}, f32[4,8,128]{2,1,0:T(8,128)S(1)}, u32[]{:S(2)}, u32[]{:S(2)}) collective-permute-start(f32[4,8,128]{2,1,0:T(8,128)S(1)} %pad_maximum_fusion), channel_id=1, source_target_pairs={{0,1},{1,2},{2,3},{3,4},{4,5},{5,6},{6,7},{7,8},{8,9},{9,10},{10,1... | collective-permute-start | bytes 49160 | tf_op jit(solution)/shard_map/ppermute | solution.py:600
  30.4 1.9 %collective-permute-start.3 = (f32[4,8,128]{2,1,0:T(8,128)S(1)}, f32[4,8,128]{2,1,0:T(8,128)S(1)}, u32[]{:S(2)}, u32[]{:S(2)}) collective-permute-start(f32[4,8,128]{2,1,0:T(8,128)S(1)} %pad_maximum_fusion.1), channel_id=1, source_target_pairs={{1,0},{2,1},{3,2},{4,3},{5,4},{6,5},{7,6},{8,7},{9,8},{10,9},{11,1... | collective-permute-start | bytes 49160 | tf_op jit(solution)/shard_map/ppermute | solution.py:601
  32.3 0.6 pad_maximum_fusion.4.rests
  32.9 0.6 copy.31
  33.5 2.4 %shard_map.130 = (bf16[512,1280]{1,0:T(8,128)(2,1)}, f32[4,512]{1,0:T(4,128)}) custom-call(s32[5,1536]{1,0:T(8,128)} %select_add_fusion.ids, f32[2,1536]{1,0:T(2,128)} %pad_maximum_fusion.4.rests), custom_call_target="tpu_custom_call" | custom-call | tf_op jit(solution)/shard_map/pallas_call | solution.py:570
  36.0 0.0 collective-permute-done.2.gl
  36.0 4.3 %collective-permute-done.3.gh = f32[4,8,128]{2,1,0:T(8,128)S(1)} collective-permute-done((f32[4,8,128]{2,1,0:T(8,128)S(1)}, f32[4,8,128]{2,1,0:T(8,128)S(1)}, u32[]{:S(2)}, u32[]{:S(2)}) %collective-permute-start.3) | collective-permute-done | bytes 16416 | tf_op jit(solution)/shard_map/ppermute | solution.py:601
  40.2 0.6 copy-done.14
  40.8 5.2 %shard_map.129.solv = f32[8,1024]{1,0:T(8,128)} custom-call(f32[1,4,8,128]{3,2,1,0:T(8,128)} %get-tuple-element.42.t0, f32[1,4,8,128]{3,2,1,0:T(8,128)} %get-tuple-element.41.t1, f32[1,4,8,128]{3,2,1,0:T(8,128)} %copy-done.4, f32[1,4,8,128]{3,2,1,0:T(8,128)} %copy-done.3, f32[4,8,128]{2,1,0:T(8,128)} %copy-done.12, f32[4,8,128]{2,1,0:T(8,128)} %copy-done.14), custom_call_target="tpu_custom_call" | custom-call | tf_op jit(solution)/shard_map/pallas_call | solution.py:570
  46.0 0.0 all-to-all-done.cells
  46.0 0.8 copy-done
  46.8 9.7 %shard_map.131 = (f32[1,4,8,128]{3,2,1,0:T(8,128)}, f32[1,4,8,128]{3,2,1,0:T(8,128)}, f32[1,4,8,128]{3,2,1,0:T(8,128)}, f32[1,4,8,128]{3,2,1,0:T(8,128)}, f32[48,512]{1,0:T(8,128)}, /*index=5*/f32[16,512]{1,0:T(8,128)}) custom-call(s32[32]{0:T(128)} %starts.3, f32[1,4,8,128]{3,2,1,0:T(8,128)} %get-tuple-element.42.t0, ...), custom_call_target="tpu_custom_call" | custom-call | tf_op jit(solution)/shard_map/pallas_call | solution.py:570
  56.5 0.0 copy-start.19
  56.5 0.0 copy-start.2
  56.5 2.1 %collective-permute-start.11 = (f32[16,512]{1,0:T(8,128)}, f32[16,512]{1,0:T(8,128)S(1)}, u32[]{:S(2)}, u32[]{:S(2)}) collective-permute-start(f32[16,512]{1,0:T(8,128)} %get-tuple-element.23.share), channel_id=1, source_target_pairs={{2,0},{3,1},{4,2},{5,3},{6,4},{7,5},{8,6},{9,7},{10,8},{11,9},{12,... | collective-permute-start | bytes 98312 | tf_op jit(solution)/shard_map/ppermute | solution.py:658
  58.6 1.9 %collective-permute-start.10 = (f32[16,512]{1,0:T(8,128)}, f32[16,512]{1,0:T(8,128)S(1)}, u32[]{:S(2)}, u32[]{:S(2)}) collective-permute-start(f32[16,512]{1,0:T(8,128)} %get-tuple-element.23.share), channel_id=1, source_target_pairs={{1,0},{2,1},{3,2},{4,3},{5,4},{6,5},{7,6},{8,7},{9,8},{10,9},{11,1... | collective-permute-start | bytes 98312 | tf_op jit(solution)/shard_map/ppermute | solution.py:658
  60.5 8.1 %collective-permute-start.9 = (f32[16,512]{1,0:T(8,128)}, f32[16,512]{1,0:T(8,128)S(1)}, u32[]{:S(2)}, u32[]{:S(2)}) collective-permute-start(f32[16,512]{1,0:T(8,128)} %get-tuple-element.23.share), channel_id=1, source_target_pairs={{0,1},{1,2},{2,3},{3,4},{4,5},{5,6},{6,7},{7,8},{8,9},{9,10},{10,1... | collective-permute-start | bytes 98312 | tf_op jit(solution)/shard_map/ppermute | solution.py:658
  68.7 4.8 %collective-permute-start.8 = (f32[16,512]{1,0:T(8,128)}, f32[16,512]{1,0:T(8,128)S(1)}, u32[]{:S(2)}, u32[]{:S(2)}) collective-permute-start(f32[16,512]{1,0:T(8,128)} %get-tuple-element.23.share), channel_id=1, source_target_pairs={{0,2},{1,3},{2,4},{3,5},{4,6},{5,7},{6,8},{7,9},{8,10},{9,11},{10,... | collective-permute-start | bytes 98312 | tf_op jit(solution)/shard_map/ppermute | solution.py:658
  73.5 0.0 collective-permute-done.11.r3
  73.5 0.0 copy-start.7
  73.5 0.0 collective-permute-done.10.r2
  73.5 0.0 collective-permute-done.9.r1
  73.6 2.1 %collective-permute-done.8.r0 = f32[16,512]{1,0:T(8,128)S(1)} collective-permute-done((f32[16,512]{1,0:T(8,128)}, f32[16,512]{1,0:T(8,128)S(1)}, u32[]{:S(2)}, u32[]{:S(2)}) %collective-permute-start.8) | collective-permute-done | bytes 32800 | tf_op jit(solution)/shard_map/ppermute | solution.py:658
  75.6 0.6 copy-done.10
  76.2 10.2 %shard_map.132 = (f32[8,1024]{1,0:T(8,128)}, f32[32,24,128]{2,1,0:T(8,128)}) custom-call(s32[32]{0:T(128)} %starts.3, f32[1,4,8,128]{3,2,1,0:T(8,128)} %get-tuple-element.18.t0, f32[1,4,8,128]{3,2,1,0:T(8,128)} %get-tuple-element.19.t1, f32[48,512]{1,0:T(8,128)} %get-tuple-element.22.cst, f32[16,512]{1,0:T(8,128)} %get-tuple-element.23.share, ...), custom_call_target="tpu_custom_call" | custom-call | tf_op jit(solution)/shard_map/pallas_call | solution.py:570
  86.4 8.4 %all-to-all-start.1 = ((f32[32,24,128]{2,1,0:T(8,128)}), f32[32,24,128]{2,1,0:T(8,128)S(1)}, u32[]{:S(2)}, u32[]{:S(2)}) async-start(f32[32,24,128]{2,1,0:T(8,128)} %get-tuple-element.27), calls=%async_computation.1 | async-start | bytes 786432 | tf_op jit(solution)/shard_map/all_to_all | solution.py:668
  94.8 0.0 copy-done.1
  94.8 1.9 %collective-permute-start.4 = (f32[1,4,8,128]{3,2,1,0:T(8,128)S(1)}, f32[1,4,8,128]{3,2,1,0:T(8,128)S(1)}, u32[]{:S(2)}, u32[]{:S(2)}) collective-permute-start(f32[1,4,8,128]{3,2,1,0:T(8,128)S(1)} %copy-done.20), channel_id=1, source_target_pairs={{0,32},{32,0},{64,96},{96,64},{128,160},{160,128},{192,224},{224,1... | collective-permute-start | bytes 49160 | tf_op jit(solution)/shard_map/ppermute | solution.py:587
  96.7 1.9 %collective-permute-start.5 = (f32[1,4,8,128]{3,2,1,0:T(8,128)S(1)}, f32[1,4,8,128]{3,2,1,0:T(8,128)S(1)}, u32[]{:S(2)}, u32[]{:S(2)}) collective-permute-start(f32[1,4,8,128]{3,2,1,0:T(8,128)S(1)} %copy-done.19), channel_id=1, source_target_pairs={{32,64},{64,32},{96,128},{128,96},{160,192},{192,160},{224,256},{2... | collective-permute-start | bytes 49160 | tf_op jit(solution)/shard_map/ppermute | solution.py:588
  98.7 0.0 collective-permute-done.4.in_a
  98.7 4.0 %collective-permute-done.5.in_b = f32[1,4,8,128]{3,2,1,0:T(8,128)S(1)} collective-permute-done((f32[1,4,8,128]{3,2,1,0:T(8,128)S(1)}, f32[1,4,8,128]{3,2,1,0:T(8,128)S(1)}, u32[]{:S(2)}, u32[]{:S(2)}) %collective-permute-start.5) | collective-permute-done | bytes 16416 | tf_op jit(solution)/shard_map/ppermute | solution.py:588
  102.7 6.2 %collective-permute-start.6 = (f32[4,8,128]{2,1,0:T(8,128)S(1)}, f32[4,8,128]{2,1,0:T(8,128)S(1)}, u32[]{:S(2)}, u32[]{:S(2)}) collective-permute-start(f32[4,8,128]{2,1,0:T(8,128)S(1)} %pad_maximum_fusion.2), channel_id=1, source_target_pairs={{0,1},{1,2},{2,3},{3,4},{4,5},{5,6},{6,7},{7,8},{8,9},{9,10},{10,1... | collective-permute-start | bytes 49160 | tf_op jit(solution)/shard_map/ppermute | solution.py:600
  108.9 2.1 %collective-permute-start.7 = (f32[4,8,128]{2,1,0:T(8,128)S(1)}, f32[4,8,128]{2,1,0:T(8,128)S(1)}, u32[]{:S(2)}, u32[]{:S(2)}) collective-permute-start(f32[4,8,128]{2,1,0:T(8,128)S(1)} %pad_maximum_fusion.3), channel_id=1, source_target_pairs={{1,0},{2,1},{3,2},{4,3},{5,4},{6,5},{7,6},{8,7},{9,8},{10,9},{11,1... | collective-permute-start | bytes 49160 | tf_op jit(solution)/shard_map/ppermute | solution.py:601
  111.0 4.0 %shard_map.133.memb = f32[8,1024]{1,0:T(8,128)} custom-call(f32[1,4,8,128]{3,2,1,0:T(8,128)} %get-tuple-element.18.t0, f32[1,4,8,128]{3,2,1,0:T(8,128)} %get-tuple-element.19.t1, f32[8,1024]{1,0:T(8,128)} %get-tuple-element.24.memb), custom_call_target="tpu_custom_call" | custom-call | tf_op jit(solution)/shard_map/pallas_call | solution.py:570
  115.1 0.0 collective-permute-done.6.gl
  115.1 3.7 %collective-permute-done.7.gh = f32[4,8,128]{2,1,0:T(8,128)S(1)} collective-permute-done((f32[4,8,128]{2,1,0:T(8,128)S(1)}, f32[4,8,128]{2,1,0:T(8,128)S(1)}, u32[]{:S(2)}, u32[]{:S(2)}) %collective-permute-start.7) | collective-permute-done | bytes 16416 | tf_op jit(solution)/shard_map/ppermute | solution.py:601
  118.8 0.0 copy-done.6
  118.8 0.6 copy-done.15
  119.4 3.9 %shard_map.134 = (f32[3,2,4,128]{3,2,1,0:T(4,128)}, f32[3,2,4,128]{3,2,1,0:T(4,128)}) custom-call(f32[1,4,8,128]{3,2,1,0:T(8,128)} %get-tuple-element.18.t0, f32[1,4,8,128]{3,2,1,0:T(8,128)} %get-tuple-element.19.t1, f32[1,4,8,128]{3,2,1,0:T(8,128)} %copy-done.5, f32[1,4,8,128]{3,2,1,0:T(8,128)} %copy-done.6, f32[4,8,128]{2,1,0:T(8,128)} %copy-done.13, ...), custom_call_target="tpu_custom_call" | custom-call | tf_op jit(solution)/shard_map/pallas_call | solution.py:570
  123.3 0.0 all-to-all-done.1
  123.4 0.6 broadcast_in_dim.13
  124.0 0.6 add.26
  (43 shorter events, 0.2 us)
Async XLA Ops:
  0.6 23.5 %copy-start.11 = (s32[992,3]{0,1:T(4,128)S(1)}, s32[992,3]{0,1:T(4,128)}, u32[]{:S(2)}) copy-start(s32[992,3]{0,1:T(4,128)} %param.17) | copy-start | bytes 35716
  0.6 23.5 %copy-start.16 = (s32[1488,2]{0,1:T(2,128)S(1)}, s32[1488,2]{0,1:T(2,128)}, u32[]{:S(2)}) copy-start(s32[1488,2]{0,1:T(2,128)} %param.16) | copy-start | bytes 35716
  0.7 24.1 %copy-start.17 = (f32[1488]{0:T(1024)S(1)}, f32[1488]{0:T(1024)}, u32[]{:S(2)}) copy-start(f32[1488]{0:T(1024)} %param.18) | copy-start | bytes 17860
  0.7 24.1 %copy-start.18 = (f32[992]{0:T(1024)S(1)}, f32[992]{0:T(1024)}, u32[]{:S(2)}) copy-start(f32[992]{0:T(1024)} %param.19) | copy-start | bytes 11908
  3.5 21.3 %collective-permute-start.1 = (f32[1,4,8,128]{3,2,1,0:T(8,128)S(1)}, f32[1,4,8,128]{3,2,1,0:T(8,128)S(1)}, u32[]{:S(2)}, u32[]{:S(2)}) collective-permute-start(f32[1,4,8,128]{3,2,1,0:T(8,128)S(1)} %get-tuple-element.40), channel_id=1, source_target_pairs={{32,64},{64,32},{96,128},{128,96},{160,192},{192,160},{224,256},{2... | collective-permute-start | bytes 49160 | tf_op jit(solution)/shard_map/ppermute | solution.py:588
  7.5 17.4 %collective-permute-start = (f32[1,4,8,128]{3,2,1,0:T(8,128)S(1)}, f32[1,4,8,128]{3,2,1,0:T(8,128)S(1)}, u32[]{:S(2)}, u32[]{:S(2)}) collective-permute-start(f32[1,4,8,128]{3,2,1,0:T(8,128)S(1)} %get-tuple-element.43), channel_id=1, source_target_pairs={{0,32},{32,0},{64,96},{96,64},{128,160},{160,128},{192,224},{224,1... | collective-permute-start | bytes 49160 | tf_op jit(solution)/shard_map/ppermute | solution.py:587
  11.3 34.7 %all-to-all-start = ((f32[32,24,128]{2,1,0:T(8,128)}), f32[32,24,128]{2,1,0:T(8,128)S(1)}, u32[]{:S(2)}, u32[]{:S(2)}) async-start(f32[32,24,128]{2,1,0:T(8,128)} %broadcast_in_dim.12), calls=%async_computation | async-start | bytes 786432 | tf_op jit(solution)/shard_map/all_to_all | solution.py:617
  24.8 15.4 %copy-start.3 = (f32[1,4,8,128]{3,2,1,0:T(8,128)}, f32[1,4,8,128]{3,2,1,0:T(8,128)S(1)}, u32[]{:S(2)}) copy-start(f32[1,4,8,128]{3,2,1,0:T(8,128)S(1)} %collective-permute-done.1.in_b) | copy-start | bytes 49156
  24.8 15.4 %copy-start.4 = (f32[1,4,8,128]{3,2,1,0:T(8,128)}, f32[1,4,8,128]{3,2,1,0:T(8,128)S(1)}, u32[]{:S(2)}) copy-start(f32[1,4,8,128]{3,2,1,0:T(8,128)S(1)} %collective-permute-done.in_a) | copy-start | bytes 49156
  24.9 11.1 %collective-permute-start.2 = (f32[4,8,128]{2,1,0:T(8,128)S(1)}, f32[4,8,128]{2,1,0:T(8,128)S(1)}, u32[]{:S(2)}, u32[]{:S(2)}) collective-permute-start(f32[4,8,128]{2,1,0:T(8,128)S(1)} %pad_maximum_fusion), channel_id=1, source_target_pairs={{0,1},{1,2},{2,3},{3,4},{4,5},{5,6},{6,7},{7,8},{8,9},{9,10},{10,1... | collective-permute-start | bytes 49160 | tf_op jit(solution)/shard_map/ppermute | solution.py:600
  30.4 9.9 %collective-permute-start.3 = (f32[4,8,128]{2,1,0:T(8,128)S(1)}, f32[4,8,128]{2,1,0:T(8,128)S(1)}, u32[]{:S(2)}, u32[]{:S(2)}) collective-permute-start(f32[4,8,128]{2,1,0:T(8,128)S(1)} %pad_maximum_fusion.1), channel_id=1, source_target_pairs={{1,0},{2,1},{3,2},{4,3},{5,4},{6,5},{7,6},{8,7},{9,8},{10,9},{11,1... | collective-permute-start | bytes 49160 | tf_op jit(solution)/shard_map/ppermute | solution.py:601
  36.0 4.3 %copy-start.12 = (f32[4,8,128]{2,1,0:T(8,128)}, f32[4,8,128]{2,1,0:T(8,128)S(1)}, u32[]{:S(2)}) copy-start(f32[4,8,128]{2,1,0:T(8,128)S(1)} %collective-permute-done.2.gl) | copy-start | bytes 49156
  40.2 0.6 copy-start.14
  46.0 0.8 copy-start
  56.5 38.3 %copy-start.1 = (f32[1,4,8,128]{3,2,1,0:T(8,128)S(1)}, f32[1,4,8,128]{3,2,1,0:T(8,128)}, u32[]{:S(2)}) copy-start(f32[1,4,8,128]{3,2,1,0:T(8,128)} %get-tuple-element.18.t0) | copy-start | bytes 49156
  56.5 38.3 %copy-start.20 = (f32[1,4,8,128]{3,2,1,0:T(8,128)S(1)}, f32[1,4,8,128]{3,2,1,0:T(8,128)}, u32[]{:S(2)}) copy-start(f32[1,4,8,128]{3,2,1,0:T(8,128)} %get-tuple-element.20) | copy-start | bytes 49156
  56.5 40.2 %copy-start.19 = (f32[1,4,8,128]{3,2,1,0:T(8,128)S(1)}, f32[1,4,8,128]{3,2,1,0:T(8,128)}, u32[]{:S(2)}) copy-start(f32[1,4,8,128]{3,2,1,0:T(8,128)} %get-tuple-element.21) | copy-start | bytes 49156
  56.5 42.1 %copy-start.2 = (f32[1,4,8,128]{3,2,1,0:T(8,128)S(1)}, f32[1,4,8,128]{3,2,1,0:T(8,128)}, u32[]{:S(2)}) copy-start(f32[1,4,8,128]{3,2,1,0:T(8,128)} %get-tuple-element.19.t1) | copy-start | bytes 49156
  56.5 17.0 %collective-permute-start.11 = (f32[16,512]{1,0:T(8,128)}, f32[16,512]{1,0:T(8,128)S(1)}, u32[]{:S(2)}, u32[]{:S(2)}) collective-permute-start(f32[16,512]{1,0:T(8,128)} %get-tuple-element.23.share), channel_id=1, source_target_pairs={{2,0},{3,1},{4,2},{5,3},{6,4},{7,5},{8,6},{9,7},{10,8},{11,9},{12,... | collective-permute-start | bytes 98312 | tf_op jit(solution)/shard_map/ppermute | solution.py:658
  58.6 14.9 %collective-permute-start.10 = (f32[16,512]{1,0:T(8,128)}, f32[16,512]{1,0:T(8,128)S(1)}, u32[]{:S(2)}, u32[]{:S(2)}) collective-permute-start(f32[16,512]{1,0:T(8,128)} %get-tuple-element.23.share), channel_id=1, source_target_pairs={{1,0},{2,1},{3,2},{4,3},{5,4},{6,5},{7,6},{8,7},{9,8},{10,9},{11,1... | collective-permute-start | bytes 98312 | tf_op jit(solution)/shard_map/ppermute | solution.py:658
  60.5 13.0 %collective-permute-start.9 = (f32[16,512]{1,0:T(8,128)}, f32[16,512]{1,0:T(8,128)S(1)}, u32[]{:S(2)}, u32[]{:S(2)}) collective-permute-start(f32[16,512]{1,0:T(8,128)} %get-tuple-element.23.share), channel_id=1, source_target_pairs={{0,1},{1,2},{2,3},{3,4},{4,5},{5,6},{6,7},{7,8},{8,9},{9,10},{10,1... | collective-permute-start | bytes 98312 | tf_op jit(solution)/shard_map/ppermute | solution.py:658
  68.7 7.0 %collective-permute-start.8 = (f32[16,512]{1,0:T(8,128)}, f32[16,512]{1,0:T(8,128)S(1)}, u32[]{:S(2)}, u32[]{:S(2)}) collective-permute-start(f32[16,512]{1,0:T(8,128)} %get-tuple-element.23.share), channel_id=1, source_target_pairs={{0,2},{1,3},{2,4},{3,5},{4,6},{5,7},{6,8},{7,9},{8,10},{9,11},{10,... | collective-permute-start | bytes 98312 | tf_op jit(solution)/shard_map/ppermute | solution.py:658
  73.5 2.1 %copy-start.7 = (f32[16,512]{1,0:T(8,128)}, f32[16,512]{1,0:T(8,128)S(1)}, u32[]{:S(2)}) copy-start(f32[16,512]{1,0:T(8,128)S(1)} %collective-permute-done.11.r3) | copy-start | bytes 98308
  73.5 2.1 %copy-start.8 = (f32[16,512]{1,0:T(8,128)}, f32[16,512]{1,0:T(8,128)S(1)}, u32[]{:S(2)}) copy-start(f32[16,512]{1,0:T(8,128)S(1)} %collective-permute-done.10.r2) | copy-start | bytes 98308
  73.5 2.1 %copy-start.9 = (f32[16,512]{1,0:T(8,128)}, f32[16,512]{1,0:T(8,128)S(1)}, u32[]{:S(2)}) copy-start(f32[16,512]{1,0:T(8,128)S(1)} %collective-permute-done.9.r1) | copy-start | bytes 98308
  75.6 0.6 copy-start.10
  86.4 37.0 %all-to-all-start.1 = ((f32[32,24,128]{2,1,0:T(8,128)}), f32[32,24,128]{2,1,0:T(8,128)S(1)}, u32[]{:S(2)}, u32[]{:S(2)}) async-start(f32[32,24,128]{2,1,0:T(8,128)} %get-tuple-element.27), calls=%async_computation.1 | async-start | bytes 786432 | tf_op jit(solution)/shard_map/all_to_all | solution.py:668
  94.8 3.9 %collective-permute-start.4 = (f32[1,4,8,128]{3,2,1,0:T(8,128)S(1)}, f32[1,4,8,128]{3,2,1,0:T(8,128)S(1)}, u32[]{:S(2)}, u32[]{:S(2)}) collective-permute-start(f32[1,4,8,128]{3,2,1,0:T(8,128)S(1)} %copy-done.20), channel_id=1, source_target_pairs={{0,32},{32,0},{64,96},{96,64},{128,160},{160,128},{192,224},{224,1... | collective-permute-start | bytes 49160 | tf_op jit(solution)/shard_map/ppermute | solution.py:587
  96.7 6.0 %collective-permute-start.5 = (f32[1,4,8,128]{3,2,1,0:T(8,128)S(1)}, f32[1,4,8,128]{3,2,1,0:T(8,128)S(1)}, u32[]{:S(2)}, u32[]{:S(2)}) collective-permute-start(f32[1,4,8,128]{3,2,1,0:T(8,128)S(1)} %copy-done.19), channel_id=1, source_target_pairs={{32,64},{64,32},{96,128},{128,96},{160,192},{192,160},{224,256},{2... | collective-permute-start | bytes 49160 | tf_op jit(solution)/shard_map/ppermute | solution.py:588
  98.7 20.1 %copy-start.5 = (f32[1,4,8,128]{3,2,1,0:T(8,128)}, f32[1,4,8,128]{3,2,1,0:T(8,128)S(1)}, u32[]{:S(2)}) copy-start(f32[1,4,8,128]{3,2,1,0:T(8,128)S(1)} %collective-permute-done.4.in_a) | copy-start | bytes 49156
  102.7 16.1 %copy-start.6 = (f32[1,4,8,128]{3,2,1,0:T(8,128)}, f32[1,4,8,128]{3,2,1,0:T(8,128)S(1)}, u32[]{:S(2)}) copy-start(f32[1,4,8,128]{3,2,1,0:T(8,128)S(1)} %collective-permute-done.5.in_b) | copy-start | bytes 49156
  102.7 12.3 %collective-permute-start.6 = (f32[4,8,128]{2,1,0:T(8,128)S(1)}, f32[4,8,128]{2,1,0:T(8,128)S(1)}, u32[]{:S(2)}, u32[]{:S(2)}) collective-permute-start(f32[4,8,128]{2,1,0:T(8,128)S(1)} %pad_maximum_fusion.2), channel_id=1, source_target_pairs={{0,1},{1,2},{2,3},{3,4},{4,5},{5,6},{6,7},{7,8},{8,9},{9,10},{10,1... | collective-permute-start | bytes 49160 | tf_op jit(solution)/shard_map/ppermute | solution.py:600
  108.9 9.9 %collective-permute-start.7 = (f32[4,8,128]{2,1,0:T(8,128)S(1)}, f32[4,8,128]{2,1,0:T(8,128)S(1)}, u32[]{:S(2)}, u32[]{:S(2)}) collective-permute-start(f32[4,8,128]{2,1,0:T(8,128)S(1)} %pad_maximum_fusion.3), channel_id=1, source_target_pairs={{1,0},{2,1},{3,2},{4,3},{5,4},{6,5},{7,6},{8,7},{9,8},{10,9},{11,1... | collective-permute-start | bytes 49160 | tf_op jit(solution)/shard_map/ppermute | solution.py:601
  115.1 3.7 %copy-start.13 = (f32[4,8,128]{2,1,0:T(8,128)}, f32[4,8,128]{2,1,0:T(8,128)S(1)}, u32[]{:S(2)}) copy-start(f32[4,8,128]{2,1,0:T(8,128)S(1)} %collective-permute-done.6.gl) | copy-start | bytes 49156
  118.8 0.6 copy-start.15

commit v6 on v5

--- a/solution.py
+++ b/solution.py
@@ -395,7 +395,13 @@
     return near
 
 
-def incidence_kernel(ids, rests, m_ref, par_ref):
+def incidence_kernel(bond_ids, corner_ids, rest_len, rest_area, m_ref, par_ref, ids, rests):
+    ids[...] = jnp.full(ids.shape, -1, jnp.int32)
+    rests[...] = jnp.ones(rests.shape, F32)
+    ids[0:2, 0:NB] = bond_ids[...]
+    ids[2:5, 0:NT] = corner_ids[...]
+    rests[0:1, 0:NB] = rest_len[...]
+    rests[1:2, 0:NT] = rest_area[...]
     third = lax.axis_index("gx") % SPAN
     bonds = pl.ds(pl.multiple_of(third * NBP, LANES), NBP)
     corners = pl.ds(pl.multiple_of(third * NTP, LANES), NTP)
@@ -614,33 +620,23 @@
         0,
     )
     cell = jnp.transpose(cell.reshape(6, 4, LANES), (1, 0, 2)).reshape(24, LANES)
+    tiles = jnp.transpose(
+        jnp.concatenate([part_pos, part_vel, random_kicks[0:2]], 0), (1, 2, 0, 3)
+    )
+    t0, t1 = tiles[:1], tiles[1:]
+    even = lax.axis_index("wa") % 2 == 0
+    cell, t0, t1 = lax.optimization_barrier((cell, t0, t1))
     cells = lax.all_to_all(
         jnp.broadcast_to(cell[None], (SLABS, 24, LANES)), "gx", 0, 0, tiled=True
     )
-    tiles = jnp.transpose(
-        jnp.concatenate([part_pos, part_vel, random_kicks[0:2]], 0), (1, 2, 0, 3)
-    )
-    t0, t1 = tiles[:1], tiles[1:]
-    even = lax.axis_index("wa") % 2 == 0
     kicks = jnp.transpose(random_kicks[2:4], (1, 2, 0, 3))
     part = ((8, TW * TF * LANES), F32)
     row = ((1, TF, 8, LANES), F32)
-    wide = SPAN * NBP
-    ids = jnp.concatenate(
-        [
-            jnp.pad(bond_ends.T, ((0, 0), (0, wide - NB)), constant_values=-1),
-            jnp.pad(triangles.T, ((0, 0), (0, wide - NT)), constant_values=-1),
-        ],
-        0,
-    )
-    rests = jnp.stack(
-        [
-            jnp.pad(rest_len, (0, wide - NB), constant_values=1.0),
-            jnp.pad(rest_area, (0, wide - NT), constant_values=1.0),
-        ]
-    )
     incidence, par = call(
-        incidence_kernel, [((NVP, COLS), BF16), ((4, NBP), F32)], [], (ids, rests)
+        incidence_kernel,
+        [((NVP, COLS), BF16), ((4, NBP), F32)],
+        [pltpu.VMEM((8, SPAN * NBP), jnp.int32), pltpu.VMEM((8, SPAN * NBP), F32)],
+        (bond_ends.T, triangles.T, rest_len[None], rest_area[None]),
     )
     sides = (jnp.where(even, t1, t0), jnp.where(even, t0, t1))
     swapped = swap(*sides)
@@ -655,7 +651,9 @@
         1,
     )
     swapped = swap(n_a, n_b)
-    got = [lax.ppermute(share, "gx", moves("gx", -s)) for s in (-2, -1, 1, 2)]
+    got = []
+    for shift in (-2, -1, 1, 2):
+        got.append(lax.ppermute(share, "gx", moves("gx", -shift)))
     memb, sends = call(
         second_kernel,
         [part, ((SLABS, 24, LANES), F32)],

time: 126 us -> 125 us (level)
  the two profiles are of different devices: /device:TPU:190 before, /device:TPU:58 now
where the time goes in v6:
time: 125 us; the launch traced here: 123 us
  starting transfers between devices  73.7 us (59%)
  Pallas kernels  32.6 us (26%)
  local copies, waits for them, and re-layouts  9.81 us (8%)
  waiting for transfers between devices  6.05 us (5%)
    pallas_call x6, Pallas kernels, call(): pl.pallas_call(kernel, out_shape=tuple((jax.ShapeDtypeStruct(s, t) for s,...  32.6 us
    ppermute x4, starting transfers between devices, body(): got.append(lax.ppermute(share, 'gx', moves('gx', -shift)))  15.7 us
    all_to_all x1, starting transfers between devices, body(): final = jnp.sum(lax.all_to_all(sends, 'gx', 0, 0, tiled=True), 0)  15.4 us
    all_to_all x1, starting transfers between devices, body(): lax.all_to_all(jnp.broadcast_to(cell[None], (SLABS, 24, LANES)), 'gx', 0,...  14.6 us
    ppermute x2, starting transfers between devices, columns(): gl = lax.ppermute(column(TF - 1), 'gx', moves('gx', 1))  11.1 us
    ppermute x2, starting transfers between devices, columns(): gh = lax.ppermute(column(0), 'gx', moves('gx', -1))  6.75 us
    unnamed x45, local copies, waits for them, and re-layouts  6.48 us
    ppermute x2, starting transfers between devices, swap(): return (in_a, lax.ppermute(out_b, 'wa', odd_pairs))  6.28 us
  transfers between devices with their start and end apart: 14, of which 2 were waited for; matrix products, arithmetic and copies ran while one was open for 2% of the time, Pallas kernels for 13%

profile of v6, /device:TPU:58, one launch (start us, length us, event | category | flops | bytes accessed | tf_op | source)
XLA Modules:
  0.0 123.4 jit_solution(17158315708366246231)
XLA Ops:
  0.6 0.0 copy-start.17
  0.7 0.7 fusion.3
  1.4 0.7 copy.21
  2.1 0.7 copy.22
  2.8 0.0 copy-start.1
  2.8 0.0 copy-start.2
  2.9 0.7 copy_bitcast_fusion.1
  3.6 1.9 %collective-permute-start = (f32[1,4,8,128]{3,2,1,0:T(8,128)S(1)}, f32[1,4,8,128]{3,2,1,0:T(8,128)S(1)}, u32[]{:S(2)}, u32[]{:S(2)}) collective-permute-start(f32[1,4,8,128]{3,2,1,0:T(8,128)S(1)} %get-tuple-element.43), channel_id=1, source_target_pairs={{0,32},{32,0},{64,96},{96,64},{128,160},{160,128},{192,224},{224,1... | collective-permute-start | bytes 49160 | tf_op jit(solution)/shard_map/ppermute | solution.py:593
  5.5 4.4 %collective-permute-start.1 = (f32[1,4,8,128]{3,2,1,0:T(8,128)S(1)}, f32[1,4,8,128]{3,2,1,0:T(8,128)S(1)}, u32[]{:S(2)}, u32[]{:S(2)}) collective-permute-start(f32[1,4,8,128]{3,2,1,0:T(8,128)S(1)} %get-tuple-element.42), channel_id=1, source_target_pairs={{32,64},{64,32},{96,128},{128,96},{160,192},{192,160},{224,256},{2... | collective-permute-start | bytes 49160 | tf_op jit(solution)/shard_map/ppermute | solution.py:594
  9.9 0.8 broadcast_in_dim.16
  10.7 14.6 %all-to-all-start = ((f32[32,24,128]{2,1,0:T(8,128)}), f32[32,24,128]{2,1,0:T(8,128)S(1)}, u32[]{:S(2)}, u32[]{:S(2)}) async-start(f32[32,24,128]{2,1,0:T(8,128)} %broadcast_in_dim.16), calls=%async_computation | async-start | bytes 786432 | tf_op jit(solution)/shard_map/all_to_all | solution.py:629
  25.3 0.0 collective-permute-done.in_a
  25.3 0.0 copy-start.5
  25.3 0.0 collective-permute-done.1.in_b
  25.3 0.0 copy-start.6
  25.4 3.4 %collective-permute-start.3 = (f32[4,8,128]{2,1,0:T(8,128)S(1)}, f32[4,8,128]{2,1,0:T(8,128)S(1)}, u32[]{:S(2)}, u32[]{:S(2)}) collective-permute-start(f32[4,8,128]{2,1,0:T(8,128)S(1)} %pad_maximum_fusion.1), channel_id=1, source_target_pairs={{1,0},{2,1},{3,2},{4,3},{5,4},{6,5},{7,6},{8,7},{9,8},{10,9},{11,1... | collective-permute-start | bytes 49160 | tf_op jit(solution)/shard_map/ppermute | solution.py:607
  28.8 5.5 %collective-permute-start.2 = (f32[4,8,128]{2,1,0:T(8,128)S(1)}, f32[4,8,128]{2,1,0:T(8,128)S(1)}, u32[]{:S(2)}, u32[]{:S(2)}) collective-permute-start(f32[4,8,128]{2,1,0:T(8,128)S(1)} %pad_maximum_fusion), channel_id=1, source_target_pairs={{0,1},{1,2},{2,3},{3,4},{4,5},{5,6},{6,7},{7,8},{8,9},{9,10},{10,1... | collective-permute-start | bytes 49160 | tf_op jit(solution)/shard_map/ppermute | solution.py:606
  34.3 0.0 copy-done.17
  34.3 0.6 broadcast_in_dim.17.rest_len
  34.9 0.6 copy.31
  35.5 3.0 %shard_map.130 = (bf16[512,1280]{1,0:T(8,128)(2,1)}, f32[4,512]{1,0:T(4,128)}) custom-call(s32[2,1488]{1,0:T(2,128)} %bitcast.54, s32[3,992]{1,0:T(4,128)} %bitcast.53, f32[1,1488]{1,0:T(1,128)} %broadcast_in_dim.17.rest_len, f32[1,992]{1,0:T(1,128)} %bitcast.55), custom_call_target="tpu_custom_call" | custom-call | tf_op jit(solution)/shard_map/pallas_call | solution.py:576
  38.4 0.0 collective-permute-done.3.gh
  38.4 0.0 collective-permute-done.2.gl
  38.5 0.0 copy-done.1
  38.5 0.0 copy-done.2
  38.5 0.0 copy-done.5
  38.5 0.0 copy-done.6
  38.5 0.5 copy-done.13
  39.0 0.6 copy-done.15
  39.6 5.2 %shard_map.129.solv = f32[8,1024]{1,0:T(8,128)} custom-call(f32[1,4,8,128]{3,2,1,0:T(8,128)} %copy-done.2, f32[1,4,8,128]{3,2,1,0:T(8,128)} %copy-done.1, f32[1,4,8,128]{3,2,1,0:T(8,128)} %copy-done.5, f32[1,4,8,128]{3,2,1,0:T(8,128)} %copy-done.6, f32[4,8,128]{2,1,0:T(8,128)} %copy-done.15, f32[4,8,128]{2,1,0:T(8,128)} %copy-done.13), custom_call_target="tpu_custom_call" | custom-call | tf_op jit(solution)/shard_map/pallas_call | solution.py:576
  44.9 0.0 all-to-all-done.cells
  44.9 0.8 copy-done
  45.6 8.0 %shard_map.131 = (f32[1,4,8,128]{3,2,1,0:T(8,128)}, f32[1,4,8,128]{3,2,1,0:T(8,128)}, f32[1,4,8,128]{3,2,1,0:T(8,128)}, f32[1,4,8,128]{3,2,1,0:T(8,128)}, f32[48,512]{1,0:T(8,128)}, /*index=5*/f32[16,512]{1,0:T(8,128)}) custom-call(s32[32]{0:T(128)} %starts.3, f32[1,4,8,128]{3,2,1,0:T(8,128)} %copy-done.2, f32[1,4,8,128]{3,2,1,0:T(8,128)} %copy-done.1, ...), custom_call_target="tpu_custom_call" | custom-call | tf_op jit(solution)/shard_map/pallas_call | solution.py:576
  53.6 0.0 copy-start.18
  53.6 0.0 copy-start.4
  53.6 2.1 %collective-permute-start.10 = (f32[16,512]{1,0:T(8,128)}, f32[16,512]{1,0:T(8,128)S(1)}, u32[]{:S(2)}, u32[]{:S(2)}) collective-permute-start(f32[16,512]{1,0:T(8,128)} %get-tuple-element.29.share), channel_id=1, source_target_pairs={{1,0},{2,1},{3,2},{4,3},{5,4},{6,5},{7,6},{8,7},{9,8},{10,9},{11,1... | collective-permute-start | bytes 98312 | tf_op jit(solution)/shard_map/ppermute | solution.py:656
  55.7 1.9 %collective-permute-start.11 = (f32[16,512]{1,0:T(8,128)}, f32[16,512]{1,0:T(8,128)S(1)}, u32[]{:S(2)}, u32[]{:S(2)}) collective-permute-start(f32[16,512]{1,0:T(8,128)} %get-tuple-element.29.share), channel_id=1, source_target_pairs={{2,0},{3,1},{4,2},{5,3},{6,4},{7,5},{8,6},{9,7},{10,8},{11,9},{12,... | collective-permute-start | bytes 98312 | tf_op jit(solution)/shard_map/ppermute | solution.py:656
  57.6 7.8 %collective-permute-start.8 = (f32[16,512]{1,0:T(8,128)}, f32[16,512]{1,0:T(8,128)S(1)}, u32[]{:S(2)}, u32[]{:S(2)}) collective-permute-start(f32[16,512]{1,0:T(8,128)} %get-tuple-element.29.share), channel_id=1, source_target_pairs={{0,2},{1,3},{2,4},{3,5},{4,6},{5,7},{6,8},{7,9},{8,10},{9,11},{10,... | collective-permute-start | bytes 98312 | tf_op jit(solution)/shard_map/ppermute | solution.py:656
  65.4 3.9 %collective-permute-start.9 = (f32[16,512]{1,0:T(8,128)}, f32[16,512]{1,0:T(8,128)S(1)}, u32[]{:S(2)}, u32[]{:S(2)}) collective-permute-start(f32[16,512]{1,0:T(8,128)} %get-tuple-element.29.share), channel_id=1, source_target_pairs={{0,1},{1,2},{2,3},{3,4},{4,5},{5,6},{6,7},{7,8},{8,9},{9,10},{10,1... | collective-permute-start | bytes 98312 | tf_op jit(solution)/shard_map/ppermute | solution.py:656
  69.4 0.0 collective-permute-done.10.r2
  69.4 0.0 copy-start.9
  69.4 0.0 collective-permute-done.11.r3
  69.4 0.0 collective-permute-done.8.r0
  69.4 0.0 copy-start.11
  69.4 2.0 %collective-permute-done.9.r1 = f32[16,512]{1,0:T(8,128)S(1)} collective-permute-done((f32[16,512]{1,0:T(8,128)}, f32[16,512]{1,0:T(8,128)S(1)}, u32[]{:S(2)}, u32[]{:S(2)}) %collective-permute-start.9) | collective-permute-done | bytes 32800 | tf_op jit(solution)/shard_map/ppermute | solution.py:656
  71.5 0.0 copy-done.9
  71.5 0.6 copy-done.12
  72.1 8.4 %shard_map.132 = (f32[8,1024]{1,0:T(8,128)}, f32[32,24,128]{2,1,0:T(8,128)}) custom-call(s32[32]{0:T(128)} %starts.3, f32[1,4,8,128]{3,2,1,0:T(8,128)} %get-tuple-element.24.t0, f32[1,4,8,128]{3,2,1,0:T(8,128)} %get-tuple-element.25.t1, f32[48,512]{1,0:T(8,128)} %get-tuple-element.28.cst, f32[16,512]{1,0:T(8,128)} %get-tuple-element.29.share, ...), custom_call_target="tpu_custom_call" | custom-call | tf_op jit(solution)/shard_map/pallas_call | solution.py:576
  80.5 15.4 %all-to-all-start.1 = ((f32[32,24,128]{2,1,0:T(8,128)}), f32[32,24,128]{2,1,0:T(8,128)S(1)}, u32[]{:S(2)}, u32[]{:S(2)}) async-start(f32[32,24,128]{2,1,0:T(8,128)} %get-tuple-element.33), calls=%async_computation.1 | async-start | bytes 786432 | tf_op jit(solution)/shard_map/all_to_all | solution.py:666
  95.9 1.9 %collective-permute-start.4 = (f32[1,4,8,128]{3,2,1,0:T(8,128)S(1)}, f32[1,4,8,128]{3,2,1,0:T(8,128)S(1)}, u32[]{:S(2)}, u32[]{:S(2)}) collective-permute-start(f32[1,4,8,128]{3,2,1,0:T(8,128)S(1)} %copy-done.19), channel_id=1, source_target_pairs={{0,32},{32,0},{64,96},{96,64},{128,160},{160,128},{192,224},{224,1... | collective-permute-start | bytes 49160 | tf_op jit(solution)/shard_map/ppermute | solution.py:593
  97.9 1.9 %collective-permute-start.5 = (f32[1,4,8,128]{3,2,1,0:T(8,128)S(1)}, f32[1,4,8,128]{3,2,1,0:T(8,128)S(1)}, u32[]{:S(2)}, u32[]{:S(2)}) collective-permute-start(f32[1,4,8,128]{3,2,1,0:T(8,128)S(1)} %copy-done.18), channel_id=1, source_target_pairs={{32,64},{64,32},{96,128},{128,96},{160,192},{192,160},{224,256},{2... | collective-permute-start | bytes 49160 | tf_op jit(solution)/shard_map/ppermute | solution.py:594
  99.8 0.0 collective-permute-done.4.in_a
  99.8 4.0 %collective-permute-done.5.in_b = f32[1,4,8,128]{3,2,1,0:T(8,128)S(1)} collective-permute-done((f32[1,4,8,128]{3,2,1,0:T(8,128)S(1)}, f32[1,4,8,128]{3,2,1,0:T(8,128)S(1)}, u32[]{:S(2)}, u32[]{:S(2)}) %collective-permute-start.5) | collective-permute-done | bytes 16416 | tf_op jit(solution)/shard_map/ppermute | solution.py:594
  103.8 3.4 %collective-permute-start.7 = (f32[4,8,128]{2,1,0:T(8,128)S(1)}, f32[4,8,128]{2,1,0:T(8,128)S(1)}, u32[]{:S(2)}, u32[]{:S(2)}) collective-permute-start(f32[4,8,128]{2,1,0:T(8,128)S(1)} %pad_maximum_fusion.3), channel_id=1, source_target_pairs={{1,0},{2,1},{3,2},{4,3},{5,4},{6,5},{7,6},{8,7},{9,8},{10,9},{11,1... | collective-permute-start | bytes 49160 | tf_op jit(solution)/shard_map/ppermute | solution.py:607
  107.2 5.7 %collective-permute-start.6 = (f32[4,8,128]{2,1,0:T(8,128)S(1)}, f32[4,8,128]{2,1,0:T(8,128)S(1)}, u32[]{:S(2)}, u32[]{:S(2)}) collective-permute-start(f32[4,8,128]{2,1,0:T(8,128)S(1)} %pad_maximum_fusion.2), channel_id=1, source_target_pairs={{0,1},{1,2},{2,3},{3,4},{4,5},{5,6},{6,7},{7,8},{8,9},{9,10},{10,1... | collective-permute-start | bytes 49160 | tf_op jit(solution)/shard_map/ppermute | solution.py:606
  112.9 4.0 %shard_map.133.memb = f32[8,1024]{1,0:T(8,128)} custom-call(f32[1,4,8,128]{3,2,1,0:T(8,128)} %get-tuple-element.24.t0, f32[1,4,8,128]{3,2,1,0:T(8,128)} %get-tuple-element.25.t1, f32[8,1024]{1,0:T(8,128)} %get-tuple-element.30.memb), custom_call_target="tpu_custom_call" | custom-call | tf_op jit(solution)/shard_map/pallas_call | solution.py:576
  116.9 0.0 collective-permute-done.7.gh
  116.9 0.0 collective-permute-done.6.gl
  117.0 0.6 copy-done.14
  117.5 0.6 copy-done.16
  118.1 3.9 %shard_map.134 = (f32[3,2,4,128]{3,2,1,0:T(4,128)}, f32[3,2,4,128]{3,2,1,0:T(4,128)}) custom-call(f32[1,4,8,128]{3,2,1,0:T(8,128)} %get-tuple-element.24.t0, f32[1,4,8,128]{3,2,1,0:T(8,128)} %get-tuple-element.25.t1, f32[1,4,8,128]{3,2,1,0:T(8,128)} %copy-done.7, f32[1,4,8,128]{3,2,1,0:T(8,128)} %copy-done.8, f32[4,8,128]{2,1,0:T(8,128)} %copy-done.16, ...), custom_call_target="tpu_custom_call" | custom-call | tf_op jit(solution)/shard_map/pallas_call | solution.py:576
  122.1 0.0 all-to-all-done.1
  122.2 0.6 add.18
  122.8 0.6 broadcast_in_dim.19
  (38 shorter events, 0.2 us)
Async XLA Ops:
  0.6 33.6 %copy-start.17 = (f32[1488]{0:T(1024)S(1)}, f32[1488]{0:T(1024)}, u32[]{:S(2)}) copy-start(f32[1488]{0:T(1024)} %param.18) | copy-start | bytes 17860
  2.8 35.6 %copy-start.1 = (f32[1,4,8,128]{3,2,1,0:T(8,128)}, f32[1,4,8,128]{3,2,1,0:T(8,128)S(1)}, u32[]{:S(2)}) copy-start(f32[1,4,8,128]{3,2,1,0:T(8,128)S(1)} %get-tuple-element.20.t1) | copy-start | bytes 49156
  2.8 35.6 %copy-start.2 = (f32[1,4,8,128]{3,2,1,0:T(8,128)}, f32[1,4,8,128]{3,2,1,0:T(8,128)S(1)}, u32[]{:S(2)}) copy-start(f32[1,4,8,128]{3,2,1,0:T(8,128)S(1)} %get-tuple-element.19.t0) | copy-start | bytes 49156
  3.6 21.7 %collective-permute-start = (f32[1,4,8,128]{3,2,1,0:T(8,128)S(1)}, f32[1,4,8,128]{3,2,1,0:T(8,128)S(1)}, u32[]{:S(2)}, u32[]{:S(2)}) collective-permute-start(f32[1,4,8,128]{3,2,1,0:T(8,128)S(1)} %get-tuple-element.43), channel_id=1, source_target_pairs={{0,32},{32,0},{64,96},{96,64},{128,160},{160,128},{192,224},{224,1... | collective-permute-start | bytes 49160 | tf_op jit(solution)/shard_map/ppermute | solution.py:593
  5.5 19.8 %collective-permute-start.1 = (f32[1,4,8,128]{3,2,1,0:T(8,128)S(1)}, f32[1,4,8,128]{3,2,1,0:T(8,128)S(1)}, u32[]{:S(2)}, u32[]{:S(2)}) collective-permute-start(f32[1,4,8,128]{3,2,1,0:T(8,128)S(1)} %get-tuple-element.42), channel_id=1, source_target_pairs={{32,64},{64,32},{96,128},{128,96},{160,192},{192,160},{224,256},{2... | collective-permute-start | bytes 49160 | tf_op jit(solution)/shard_map/ppermute | solution.py:594
  10.7 34.2 %all-to-all-start = ((f32[32,24,128]{2,1,0:T(8,128)}), f32[32,24,128]{2,1,0:T(8,128)S(1)}, u32[]{:S(2)}, u32[]{:S(2)}) async-start(f32[32,24,128]{2,1,0:T(8,128)} %broadcast_in_dim.16), calls=%async_computation | async-start | bytes 786432 | tf_op jit(solution)/shard_map/all_to_all | solution.py:629
  25.3 13.2 %copy-start.5 = (f32[1,4,8,128]{3,2,1,0:T(8,128)}, f32[1,4,8,128]{3,2,1,0:T(8,128)S(1)}, u32[]{:S(2)}) copy-start(f32[1,4,8,128]{3,2,1,0:T(8,128)S(1)} %collective-permute-done.in_a) | copy-start | bytes 49156
  25.3 13.2 %copy-start.6 = (f32[1,4,8,128]{3,2,1,0:T(8,128)}, f32[1,4,8,128]{3,2,1,0:T(8,128)S(1)}, u32[]{:S(2)}) copy-start(f32[1,4,8,128]{3,2,1,0:T(8,128)S(1)} %collective-permute-done.1.in_b) | copy-start | bytes 49156
  25.4 13.1 %collective-permute-start.3 = (f32[4,8,128]{2,1,0:T(8,128)S(1)}, f32[4,8,128]{2,1,0:T(8,128)S(1)}, u32[]{:S(2)}, u32[]{:S(2)}) collective-permute-start(f32[4,8,128]{2,1,0:T(8,128)S(1)} %pad_maximum_fusion.1), channel_id=1, source_target_pairs={{1,0},{2,1},{3,2},{4,3},{5,4},{6,5},{7,6},{8,7},{9,8},{10,9},{11,1... | collective-permute-start | bytes 49160 | tf_op jit(solution)/shard_map/ppermute | solution.py:607
  28.8 9.7 %collective-permute-start.2 = (f32[4,8,128]{2,1,0:T(8,128)S(1)}, f32[4,8,128]{2,1,0:T(8,128)S(1)}, u32[]{:S(2)}, u32[]{:S(2)}) collective-permute-start(f32[4,8,128]{2,1,0:T(8,128)S(1)} %pad_maximum_fusion), channel_id=1, source_target_pairs={{0,1},{1,2},{2,3},{3,4},{4,5},{5,6},{6,7},{7,8},{8,9},{9,10},{10,1... | collective-permute-start | bytes 49160 | tf_op jit(solution)/shard_map/ppermute | solution.py:606
  38.4 0.6 copy-start.13
  39.0 0.6 copy-start.15
  44.9 0.8 copy-start
  53.6 42.3 %copy-start.3 = (f32[1,4,8,128]{3,2,1,0:T(8,128)S(1)}, f32[1,4,8,128]{3,2,1,0:T(8,128)}, u32[]{:S(2)}) copy-start(f32[1,4,8,128]{3,2,1,0:T(8,128)} %get-tuple-element.24.t0) | copy-start | bytes 49156
  53.6 42.3 %copy-start.19 = (f32[1,4,8,128]{3,2,1,0:T(8,128)S(1)}, f32[1,4,8,128]{3,2,1,0:T(8,128)}, u32[]{:S(2)}) copy-start(f32[1,4,8,128]{3,2,1,0:T(8,128)} %get-tuple-element.26) | copy-start | bytes 49156
  53.6 44.2 %copy-start.18 = (f32[1,4,8,128]{3,2,1,0:T(8,128)S(1)}, f32[1,4,8,128]{3,2,1,0:T(8,128)}, u32[]{:S(2)}) copy-start(f32[1,4,8,128]{3,2,1,0:T(8,128)} %get-tuple-element.27) | copy-start | bytes 49156
  53.6 46.2 %copy-start.4 = (f32[1,4,8,128]{3,2,1,0:T(8,128)S(1)}, f32[1,4,8,128]{3,2,1,0:T(8,128)}, u32[]{:S(2)}) copy-start(f32[1,4,8,128]{3,2,1,0:T(8,128)} %get-tuple-element.25.t1) | copy-start | bytes 49156
  53.6 15.8 %collective-permute-start.10 = (f32[16,512]{1,0:T(8,128)}, f32[16,512]{1,0:T(8,128)S(1)}, u32[]{:S(2)}, u32[]{:S(2)}) collective-permute-start(f32[16,512]{1,0:T(8,128)} %get-tuple-element.29.share), channel_id=1, source_target_pairs={{1,0},{2,1},{3,2},{4,3},{5,4},{6,5},{7,6},{8,7},{9,8},{10,9},{11,1... | collective-permute-start | bytes 98312 | tf_op jit(solution)/shard_map/ppermute | solution.py:656
  55.7 13.7 %collective-permute-start.11 = (f32[16,512]{1,0:T(8,128)}, f32[16,512]{1,0:T(8,128)S(1)}, u32[]{:S(2)}, u32[]{:S(2)}) collective-permute-start(f32[16,512]{1,0:T(8,128)} %get-tuple-element.29.share), channel_id=1, source_target_pairs={{2,0},{3,1},{4,2},{5,3},{6,4},{7,5},{8,6},{9,7},{10,8},{11,9},{12,... | collective-permute-start | bytes 98312 | tf_op jit(solution)/shard_map/ppermute | solution.py:656
  57.6 11.8 %collective-permute-start.8 = (f32[16,512]{1,0:T(8,128)}, f32[16,512]{1,0:T(8,128)S(1)}, u32[]{:S(2)}, u32[]{:S(2)}) collective-permute-start(f32[16,512]{1,0:T(8,128)} %get-tuple-element.29.share), channel_id=1, source_target_pairs={{0,2},{1,3},{2,4},{3,5},{4,6},{5,7},{6,8},{7,9},{8,10},{9,11},{10,... | collective-permute-start | bytes 98312 | tf_op jit(solution)/shard_map/ppermute | solution.py:656
  65.4 6.0 %collective-permute-start.9 = (f32[16,512]{1,0:T(8,128)}, f32[16,512]{1,0:T(8,128)S(1)}, u32[]{:S(2)}, u32[]{:S(2)}) collective-permute-start(f32[16,512]{1,0:T(8,128)} %get-tuple-element.29.share), channel_id=1, source_target_pairs={{0,1},{1,2},{2,3},{3,4},{4,5},{5,6},{6,7},{7,8},{8,9},{9,10},{10,1... | collective-permute-start | bytes 98312 | tf_op jit(solution)/shard_map/ppermute | solution.py:656
  69.4 2.1 %copy-start.9 = (f32[16,512]{1,0:T(8,128)}, f32[16,512]{1,0:T(8,128)S(1)}, u32[]{:S(2)}) copy-start(f32[16,512]{1,0:T(8,128)S(1)} %collective-permute-done.10.r2) | copy-start | bytes 98308
  69.4 2.1 %copy-start.10 = (f32[16,512]{1,0:T(8,128)}, f32[16,512]{1,0:T(8,128)S(1)}, u32[]{:S(2)}) copy-start(f32[16,512]{1,0:T(8,128)S(1)} %collective-permute-done.11.r3) | copy-start | bytes 98308
  69.4 2.0 %copy-start.11 = (f32[16,512]{1,0:T(8,128)}, f32[16,512]{1,0:T(8,128)S(1)}, u32[]{:S(2)}) copy-start(f32[16,512]{1,0:T(8,128)S(1)} %collective-permute-done.8.r0) | copy-start | bytes 98308
  71.5 0.6 copy-start.12
  80.5 41.6 %all-to-all-start.1 = ((f32[32,24,128]{2,1,0:T(8,128)}), f32[32,24,128]{2,1,0:T(8,128)S(1)}, u32[]{:S(2)}, u32[]{:S(2)}) async-start(f32[32,24,128]{2,1,0:T(8,128)} %get-tuple-element.33), calls=%async_computation.1 | async-start | bytes 786432 | tf_op jit(solution)/shard_map/all_to_all | solution.py:666
  95.9 3.9 %collective-permute-start.4 = (f32[1,4,8,128]{3,2,1,0:T(8,128)S(1)}, f32[1,4,8,128]{3,2,1,0:T(8,128)S(1)}, u32[]{:S(2)}, u32[]{:S(2)}) collective-permute-start(f32[1,4,8,128]{3,2,1,0:T(8,128)S(1)} %copy-done.19), channel_id=1, source_target_pairs={{0,32},{32,0},{64,96},{96,64},{128,160},{160,128},{192,224},{224,1... | collective-permute-start | bytes 49160 | tf_op jit(solution)/shard_map/ppermute | solution.py:593
  97.9 6.0 %collective-permute-start.5 = (f32[1,4,8,128]{3,2,1,0:T(8,128)S(1)}, f32[1,4,8,128]{3,2,1,0:T(8,128)S(1)}, u32[]{:S(2)}, u32[]{:S(2)}) collective-permute-start(f32[1,4,8,128]{3,2,1,0:T(8,128)S(1)} %copy-done.18), channel_id=1, source_target_pairs={{32,64},{64,32},{96,128},{128,96},{160,192},{192,160},{224,256},{2... | collective-permute-start | bytes 49160 | tf_op jit(solution)/shard_map/ppermute | solution.py:594
  99.8 17.1 %copy-start.7 = (f32[1,4,8,128]{3,2,1,0:T(8,128)}, f32[1,4,8,128]{3,2,1,0:T(8,128)S(1)}, u32[]{:S(2)}) copy-start(f32[1,4,8,128]{3,2,1,0:T(8,128)S(1)} %collective-permute-done.4.in_a) | copy-start | bytes 49156
  103.8 13.1 %copy-start.8 = (f32[1,4,8,128]{3,2,1,0:T(8,128)}, f32[1,4,8,128]{3,2,1,0:T(8,128)S(1)}, u32[]{:S(2)}) copy-start(f32[1,4,8,128]{3,2,1,0:T(8,128)S(1)} %collective-permute-done.5.in_b) | copy-start | bytes 49156
  103.8 13.1 %collective-permute-start.7 = (f32[4,8,128]{2,1,0:T(8,128)S(1)}, f32[4,8,128]{2,1,0:T(8,128)S(1)}, u32[]{:S(2)}, u32[]{:S(2)}) collective-permute-start(f32[4,8,128]{2,1,0:T(8,128)S(1)} %pad_maximum_fusion.3), channel_id=1, source_target_pairs={{1,0},{2,1},{3,2},{4,3},{5,4},{6,5},{7,6},{8,7},{9,8},{10,9},{11,1... | collective-permute-start | bytes 49160 | tf_op jit(solution)/shard_map/ppermute | solution.py:607
  107.2 9.7 %collective-permute-start.6 = (f32[4,8,128]{2,1,0:T(8,128)S(1)}, f32[4,8,128]{2,1,0:T(8,128)S(1)}, u32[]{:S(2)}, u32[]{:S(2)}) collective-permute-start(f32[4,8,128]{2,1,0:T(8,128)S(1)} %pad_maximum_fusion.2), channel_id=1, source_target_pairs={{0,1},{1,2},{2,3},{3,4},{4,5},{5,6},{6,7},{7,8},{8,9},{9,10},{10,1... | collective-permute-start | bytes 49160 | tf_op jit(solution)/shard_map/ppermute | solution.py:606
  116.9 0.6 copy-start.14
  117.5 0.6 copy-start.16
